TPU v7x, 32 devices: a whole 2x2x4 slice. The times are simulated.
32 devices in a mesh: space: 4 (over y, x), snap: 8 (over z, core).
Axes of the slice: x: 2, y: 2, z: 4, core: 2. Of those that a mesh axis runs over, the one named last changes fastest.
Arguments:
- snapshots: bfloat16 [4096, 32768], P('space', 'snap'), may hold values from -6 to 6
- vectors_cyclic: float32 [32768, 64], P('snap', 'space'), may hold values from -0.03125 to 0.03125
- eigen_values: float32 [64], replicated, may hold values from 0.25 to 25
- held_out: bfloat16 [4096, 256], P(('space', 'snap')), may hold values from -6 to 6
Outputs:
- modes: bfloat16 [4096, 64], P(('space', 'snap'))
- coefficients: float32 [64, 256], replicated
All inputs are finite; a program needn't handle non-finite values.
Results may differ from a plain program's by a relative error of at most 0.0052.
Values sent between devices are 32-bit elements; how exact they have to be, the bound alone decides.
No kernel may reach another device: no remote copies, remote signals or barrier semaphores. Data moves between devices by JAX's collectives and lax.ppermute only.
A program may use at most 64 MiB of HBM per device.

v0:
```python
import math

import jax
import jax.numpy as jnp
from jax import lax
from jax.sharding import PartitionSpec as P

ROW_BLOCK = 16
COL_BLOCK = 4


def order_rows(received, snap_count):
    slab_rows, width = received.shape
    blocks_each = slab_rows // (snap_count * ROW_BLOCK)
    shaped = received.reshape(snap_count, blocks_each, ROW_BLOCK, width)
    return shaped.transpose(1, 0, 2, 3).reshape(slab_rows, width)


def order_columns(gathered, space_count):
    slab_rows, width = gathered.shape
    shaped = gathered.reshape(slab_rows, space_count, width // (space_count * COL_BLOCK), COL_BLOCK)
    return shaped.transpose(0, 2, 1, 3).reshape(slab_rows, width)


def per_device(snapshots, vectors_cyclic, eigen_values, held_out):
    snap_count = lax.axis_size("snap")
    space_count = lax.axis_size("space")
    moved = lax.all_to_all(vectors_cyclic, "snap", split_axis=0, concat_axis=0, tiled=True)
    moved = order_rows(moved, snap_count)
    widened = lax.all_gather(moved, "space", axis=1, tiled=True)
    eigvec = order_columns(widened, space_count)
    scaled = (eigvec * lax.rsqrt(eigen_values)[None, :]).astype(jnp.bfloat16)
    summed = lax.psum_scatter(
        jnp.dot(snapshots, scaled, preferred_element_type=jnp.float32),
        "snap",
        scatter_dimension=0,
        tiled=True,
    )
    modes = summed.astype(jnp.bfloat16)
    total_cells = snapshots.shape[0] * space_count
    partial_value = lax.dot_general(
        modes, held_out, (((0,), (0,)), ((), ())), preferred_element_type=jnp.float32
    )
    coefficients = lax.psum(partial_value, ("space", "snap")) / math.sqrt(total_cells)
    return (modes, coefficients)


def solution(mesh):
    return jax.shard_map(
        per_device,
        mesh=mesh,
        in_specs=(P("space", "snap"), P("snap", "space"), P(), P(("space", "snap"), None)),
        out_specs=(P(("space", "snap"), None), P()),
        check_vma=False,
    )
```

profile of v0, /device:TPU:0, one launch (start us, length us, event | category | flops | bytes accessed | tf_op | source)
XLA Modules:
  0.0 228.7 jit_solution(1001698393581418239)
XLA Ops:
  7.2 0.0 copy-start
  7.2 0.0 copy-start.2
  7.2 0.0 all-gather.2.cloned.1.call-start
  7.2 1.0 copy.11
  8.2 15.9 %all_to_all.9 = f32[8,512,16]{1,2,0:T(8,128)S(1)} all-to-all(f32[8,512,16]{1,2,0:T(8,128)S(1)} %bitcast.23), channel_id=1, replica_groups=mesh['space'=4,'snap'=8] {'snap'}, dimensions={0} | all-to-all | bytes 524288 | tf_op jit(solution)/shard_map/all_to_all | solution.py:28
  24.1 0.7 reshape.20
  24.8 3.0 %copy.7 = f32[32,8,16,16]{2,1,0,3:T(8,128)} copy(f32[32,8,16,16]{2,0,3,1:T(8,128)S(1)} %bitcast.21) | data formatting | bytes 524288 | tf_op jit(solution)/shard_map/transpose | solution.py:16
  27.8 3.8 %reshape.21 = f32[4096,16]{0,1:T(8,128)} reshape(f32[32,8,16,16]{2,1,0,3:T(8,128)} %copy.7) | data formatting | bytes 524288 | tf_op jit(solution)/shard_map/reshape | solution.py:16
  31.6 0.0 all-gather.2.cloned.1.call-update
  31.6 0.0 reduce-scatter.2.cloned.1.call-start
  31.7 0.0 copy-done.2
  31.7 25.5 %all-gather.2.cloned.1.call-done = f32[4096,64]{0,1:T(8,128)} async-done(((f32[4096,16]{0,1:T(8,128)}), f32[4096,64]{0,1:T(8,128)}) %all-gather.2.cloned.1.call-update) | async-done | bytes 1048592 | tf_op jit(solution)/shard_map/all_gather | solution.py:30
  57.2 1.5 reshape.22
  58.8 0.1 copy.8
  58.9 0.4 reshape.23
  59.2 6.8 %convolution_bitcast_fusion = f32[1024,64]{0,1:T(8,128)} fusion(bf16[1024,4096]{1,0:T(8,128)(2,1)} %param.4, f32[4096,64]{0,1:T(8,128)S(1)} %reshape.23, f32[64]{0:T(128)S(1)} %rsqrt.3), kind=kOutput, calls=%fused_computation | convolution fusion | flops 537395200 | bytes 9699584 | tf_op jit(solution)/shard_map/dot_general | solution.py:34
  66.0 0.0 reduce-scatter.2.cloned.1.call-update
  66.0 0.0 all-reduce.2.cloned.1.call-start
  66.1 30.9 %reduce-scatter.2.cloned.1.call-done = f32[128,64]{0,1:T(8,128)} async-done(((f32[1024,64]{0,1:T(8,128)}), f32[128,64]{0,1:T(8,128)}) %reduce-scatter.2.cloned.1.call-update) | async-done | bytes 32784 | tf_op jit(solution)/shard_map/reduce_scatter | solution.py:33
  97.0 0.8 convert_element_type.7
  97.7 0.0 copy-done
  97.7 0.0 copy-start.1
  97.8 0.8 fusion.1
  98.5 0.0 all-reduce.2.cloned.1.call-update
  98.5 122.2 %all-reduce.2.cloned.1.call-done = f32[64,256]{1,0:T(8,128)} async-done(((f32[64,256]{1,0:T(8,128)}), f32[64,256]{1,0:T(8,128)}) %all-reduce.2.cloned.1.call-update) | async-done | bytes 65552 | tf_op jit(solution)/shard_map/psum | solution.py:44
  220.7 1.5 broadcast_multiply_fusion
  222.2 0.0 copy-done.1
  (1 shorter events, 0.0 us)
Async XLA Ops:
  7.2 90.6 %copy-start = (bf16[128,256]{1,0:T(8,128)(2,1)S(1)}, bf16[128,256]{1,0:T(8,128)(2,1)}, u32[]{:S(2)}) copy-start(bf16[128,256]{1,0:T(8,128)(2,1)} %param.7) | copy-start | bytes 196612
  7.2 24.5 %copy-start.2 = (f32[64]{0:T(128)S(1)}, f32[64]{0:T(128)}, u32[]{:S(2)}) copy-start(f32[64]{0:T(128)} %param.6) | copy-start | bytes 772
  7.2 50.0 %all-gather.2.cloned.1.call-start = ((), (), s32[]{:S(2)}) async-start(), calls=%async_computation.2 | async-start | bytes 1310720 | tf_op jit(solution)/shard_map/all_gather | solution.py:30
  31.6 65.3 %reduce-scatter.2.cloned.1.call-start = ((), (), s32[]{:S(2)}) async-start(), calls=%async_computation.3 | async-start | bytes 294912 | tf_op jit(solution)/shard_map/reduce_scatter | solution.py:33
  66.0 154.7 %all-reduce.2.cloned.1.call-start = ((), (), s32[]{:S(2)}) async-start(), calls=%async_computation.4 | async-start | bytes 131072 | tf_op jit(solution)/shard_map/psum | solution.py:44
  97.7 124.4 %copy-start.1 = (bf16[128,64]{0,1:T(8,128)(2,1)}, bf16[128,64]{0,1:T(8,128)(2,1)S(1)}, u32[]{:S(2)}) copy-start(bf16[128,64]{0,1:T(8,128)(2,1)S(1)} %convert_element_type.7) | copy-start | bytes 49156
Sparse Core Ops, SparseCore 0:
  31.8 25.4 all-gather.1
  66.1 30.7 reduce-scatter.1
  103.1 117.5 all-reduce.1
where the time goes:
time: 230 us; the launch traced here: 229 us
  waiting for transfers between devices  179 us (78%)
  blocking collectives  15.9 us (7%)
  between operations  13.8 us (6%)
  local copies, waits for them, and re-layouts  10.5 us (5%)
  matrix products  7.53 us (3%)
    psum x1, waiting for transfers between devices, per_device(): lax.psum(partial_value, ('space', 'snap')) / math.sqrt(total_cells)  122 us
    reduce_scatter x1, waiting for transfers between devices, per_device(): lax.psum_scatter(jnp.dot(snapshots, scaled, preferred_element_type=jnp.fl...  30.9 us
    all_gather x1, waiting for transfers between devices, per_device(): widened = lax.all_gather(moved, 'space', axis=1, tiled=True)  25.5 us
    all_to_all x1, blocking collectives, per_device(): lax.all_to_all(vectors_cyclic, 'snap', split_axis=0, concat_axis=0, tiled...  15.9 us
    dot_general x1, matrix products, per_device(): jnp.dot(snapshots, scaled, preferred_element_type=jnp.float32)  6.77 us
  transfers between devices with their start and end apart: 3, of which 3 were waited for; matrix products, arithmetic and copies ran while one was open for 0% of the time, Pallas kernels for 0%

commit v1 on v0

v1 whole, which is shorter than its diff:
```python
import math

import jax
import jax.numpy as jnp
from jax import lax
from jax.experimental import pallas as pl
from jax.experimental.pallas import tpu as pltpu
from jax.sharding import PartitionSpec as P

ROW_BLOCK = 16
COL_BLOCK = 4
LANES = 128
GROUPS = LANES // ROW_BLOCK
VMEM = pltpu.VMEM
SMEM_SPEC = pl.BlockSpec(memory_space=pltpu.SMEM)
VMEM_SPEC = pl.BlockSpec(memory_space=pltpu.VMEM)


def swap(value, axis, mask):
    count = lax.axis_size(axis)
    return lax.ppermute(value, axis, [(i, i ^ mask) for i in range(count)])


def tree_sum(terms):
    while len(terms) > 1:
        terms = [terms[i] + terms[i + 1] for i in range(0, len(terms), 2)]
    return terms[0]


def split_kernel(space_count, pos_ref, own_ref, other_ref, eig_ref, *out_refs):
    p, q = pos_ref[0], pos_ref[1]
    width = own_ref.shape[0]
    chunk = out_refs[0].shape[2]
    row = lax.broadcasted_iota(jnp.int32, (width, eig_ref.shape[1]), 0)
    mode = lax.broadcasted_iota(jnp.int32, (width, eig_ref.shape[1]), 1)
    mine = (row // COL_BLOCK * space_count + q) * COL_BLOCK + row % COL_BLOCK
    picked = jnp.where(mode == mine, eig_ref[...], 0.0)
    scale = lax.rsqrt(jnp.sum(picked, axis=1, keepdims=True))
    for d, out_ref in enumerate(out_refs):
        start = pl.multiple_of((p ^ (2 * d)) * chunk, LANES)
        out_ref[0] = own_ref[:, pl.ds(start, chunk)] * scale
        out_ref[1] = other_ref[:, pl.ds(start, chunk)] * scale


def split_pieces(pos, own, other, eig, snap_count, space_count):
    width, rows = own.shape
    chunk = rows // snap_count
    piece = jax.ShapeDtypeStruct((2, width, chunk), jnp.float32)
    return pl.pallas_call(
        lambda *refs: split_kernel(space_count, *refs),
        out_shape=[piece] * (snap_count // 2),
        in_specs=[SMEM_SPEC, VMEM_SPEC, VMEM_SPEC, VMEM_SPEC],
        out_specs=[VMEM_SPEC] * (snap_count // 2),
        name="split_pieces",
    )(pos, own, other, eig)


def interleave(blocks):
    lane = lax.broadcasted_iota(jnp.int32, blocks[0].shape, 1) // ROW_BLOCK
    step = 1
    while step < GROUPS:
        high = (lane & step) != 0
        mixed = list(blocks)
        for a in range(GROUPS):
            if a & step == 0:
                b = a | step
                low_of_b = pltpu.roll(blocks[b], step * ROW_BLOCK, 1)
                high_of_a = pltpu.roll(blocks[a], LANES - step * ROW_BLOCK, 1)
                mixed[a] = jnp.where(high, low_of_b, blocks[a])
                mixed[b] = jnp.where(high, blocks[b], high_of_a)
        blocks = mixed
        step *= 2
    return blocks


def multiply_kernel(pos_ref, *refs):
    parts, (snap_ref, keep_ref, send_ref, scaled_ref, cells_ref) = refs[:-5], refs[-5:]
    p = pos_ref[0]
    snap_count, width, chunk = parts[0].shape
    groups_of_p = snap_count // GROUPS
    for e, part in enumerate(parts):
        for outer in range(groups_of_p):
            slots = [p ^ (outer * GROUPS + g) for g in range(GROUPS)]
            for t in range(chunk // LANES):
                blocks = [part[slot, :, t * LANES : (t + 1) * LANES] for slot in slots]
                for j, block in enumerate(interleave(blocks)):
                    tile = (t * GROUPS + j) * groups_of_p + outer
                    scaled_ref[e * width : (e + 1) * width, tile * LANES : (tile + 1) * LANES] = block.astype(
                        jnp.bfloat16
                    )
    cells = cells_ref.shape[2]
    total = lax.dot_general(
        scaled_ref[...], snap_ref[...], (((1,), (1,)), ((), ())), preferred_element_type=jnp.float32
    )
    for owner in range(snap_count):
        cells_ref[owner] = total[:, owner * cells : (owner + 1) * cells]
    for d in range(snap_count // 2):
        keep_ref[d] = cells_ref[p ^ (2 * d)]
        send_ref[d] = cells_ref[p ^ (2 * d + 1)]


def multiply(pos, parts, snapshots):
    snap_count, width, chunk = parts[0].shape
    cells, depth = snapshots.shape
    modes = width * len(parts)
    half = jax.ShapeDtypeStruct((snap_count // 2, modes, cells // snap_count), jnp.float32)
    return pl.pallas_call(
        multiply_kernel,
        out_shape=[half, half],
        in_specs=[SMEM_SPEC] + [VMEM_SPEC] * (len(parts) + 1),
        out_specs=[VMEM_SPEC, VMEM_SPEC],
        scratch_shapes=[
            VMEM((modes, depth), jnp.bfloat16),
            VMEM((snap_count, modes, cells // snap_count), jnp.float32),
        ],
        name="multiply",
    )(pos, *parts, snapshots)


def project_kernel(width, pos_ref, *refs):
    sums, (held_ref, modes_ref, keep_ref, send_ref, coef_ref) = refs[:-5], refs[-5:]
    p, q = pos_ref[0], pos_ref[1]
    rounded = tree_sum([ref[...] for ref in sums]).astype(jnp.bfloat16)
    modes = rounded.shape[0]
    space_count = modes // width
    target = lax.broadcasted_iota(jnp.int32, (modes, modes), 0)
    source = lax.broadcasted_iota(jnp.int32, (modes, modes), 1)
    e, r = source // width, source % width
    mode = (r // COL_BLOCK * space_count + (q ^ e)) * COL_BLOCK + r % COL_BLOCK
    order = jnp.where(mode == target, 1.0, 0.0).astype(jnp.bfloat16)
    ordered = jnp.dot(order, rounded, preferred_element_type=jnp.float32).astype(jnp.bfloat16)
    modes_ref[...] = ordered
    coef_ref[...] = jnp.dot(ordered, held_ref[...], preferred_element_type=jnp.float32)
    half = modes // 2
    core = p & 1
    keep_ref[...] = coef_ref[pl.ds(pl.multiple_of(core * half, 8), half), :]
    send_ref[...] = coef_ref[pl.ds(pl.multiple_of((1 - core) * half, 8), half), :]


def project(pos, sums, held, width):
    modes, cells = sums[0].shape
    count = held.shape[1]
    half = jax.ShapeDtypeStruct((modes // 2, count), jnp.float32)
    return pl.pallas_call(
        lambda *refs: project_kernel(width, *refs),
        out_shape=[jax.ShapeDtypeStruct((modes, cells), jnp.bfloat16), half, half],
        in_specs=[SMEM_SPEC] + [VMEM_SPEC] * (len(sums) + 1),
        out_specs=[VMEM_SPEC] * 3,
        scratch_shapes=[VMEM((modes, count), jnp.float32)],
        name="project",
    )(pos, *sums, held)


def per_device(snapshots, vectors_cyclic, eigen_values, held_out):
    snap_count = lax.axis_size("snap")
    space_count = lax.axis_size("space")
    p, q = lax.axis_index("snap"), lax.axis_index("space")
    pos = jnp.stack([p, q]).astype(jnp.int32)
    distances = range(1, snap_count // 2)
    width = vectors_cyclic.shape[1]

    own = vectors_cyclic.T
    other = swap(own, "snap", 1)
    pieces = split_pieces(pos, own, other, eigen_values[None, :], snap_count, space_count)
    pieces = [pieces[0]] + [swap(pieces[d], "snap", 2 * d) for d in distances]
    slab = jnp.concatenate(pieces)
    parts = [slab] + [swap(slab, "space", e) for e in range(1, space_count)]

    keep, send = multiply(pos, parts, snapshots)
    paired = keep + swap(send, "snap", 1)
    sums = [paired[0]] + [swap(paired[d], "snap", 2 * d) for d in distances]

    modes, keep, send = project(pos, sums, held_out, width)
    half = keep + swap(send, "snap", 1)
    half = tree_sum([half] + [swap(half, "snap", 2 * d) for d in distances])
    half = tree_sum([half] + [swap(half, "space", e) for e in range(1, space_count)])
    far = swap(half, "snap", 1)
    first = p % 2 == 0
    coefficients = jnp.concatenate([jnp.where(first, half, far), jnp.where(first, far, half)])
    total_cells = snapshots.shape[0] * space_count
    return (modes.T, coefficients / math.sqrt(total_cells))


def solution(mesh):
    return jax.shard_map(
        per_device,
        mesh=mesh,
        in_specs=(P("space", "snap"), P("snap", "space"), P(), P(("space", "snap"), None)),
        out_specs=(P(("space", "snap"), None), P()),
        check_vma=False,
    )
```

time: 230 us -> 70.1 us (0.30)
  waiting for transfers between devices: 179 us -> 28.8 us
  starting transfers between devices: 0.12 us -> 22 us
  blocking collectives: 15.9 us -> 0 us
  between operations: 13.8 us -> 0.7 us
  Pallas kernels: 0 us -> 11.1 us
  matrix products: 7.53 us -> 0 us
  local copies, waits for them, and re-layouts: 10.5 us -> 4.12 us
    psum x1 -> x0, waiting for transfers between devices: 122 us -> none  [per_device(): lax.psum(partial_value, ('space', 'snap')) / math.sqrt(total_cells)]
    reduce_scatter x1 -> x0, waiting for transfers between devices: 30.9 us -> none  [per_device(): lax.psum_scatter(jnp.dot(snapshots, scaled, preferred_element_type=jnp.fl...]
    ppermute x0 -> x19, waiting for transfers between devices: none -> 28.8 us  [swap(): return lax.ppermute(value, axis, [(i, i ^ mask) for i in range(count)])]
    all_gather x1 -> x0, waiting for transfers between devices: 25.5 us -> none  [per_device(): widened = lax.all_gather(moved, 'space', axis=1, tiled=True)]
    ppermute x0 -> x19, starting transfers between devices: none -> 22 us  [swap(): return lax.ppermute(value, axis, [(i, i ^ mask) for i in range(count)])]
    all_to_all x1 -> x0, blocking collectives: 15.9 us -> none  [per_device(): lax.all_to_all(vectors_cyclic, 'snap', split_axis=0, concat_axis=0, tiled...]
    pallas_call x0 -> x3, Pallas kernels: none -> 11.1 us  [the longest x1 7.43 us: multiply(): pl.pallas_call(multiply_kernel, out_shape=[half, half], in_specs=[SMEM_SP...]
    dot_general x2 -> x0, matrix products: 7.53 us -> none  [the longest x1 6.77 us: per_device(): jnp.dot(snapshots, scaled, preferred_element_type=jnp.float32)]
  transfers between devices with their start and end apart: 3 -> 19, of which waited for: 3 -> 18; matrix products, arithmetic and copies ran while one was open for 0% -> 2% of each run, Pallas kernels for 0% -> 0%
where the time goes in v1:
time: 70.1 us; the launch traced here: 69.8 us
  waiting for transfers between devices  28.8 us (41%)
  starting transfers between devices  22 us (31%)
  Pallas kernels  11.1 us (16%)
  local copies, waits for them, and re-layouts  4.12 us (6%)
  other arithmetic  3.01 us (4%)
    ppermute x19, waiting for transfers between devices, swap(): return lax.ppermute(value, axis, [(i, i ^ mask) for i in range(count)])  28.8 us
    ppermute x19, starting transfers between devices, swap(): return lax.ppermute(value, axis, [(i, i ^ mask) for i in range(count)])  22 us
    pallas_call x1, Pallas kernels, multiply(): pl.pallas_call(multiply_kernel, out_shape=[half, half], in_specs=[SMEM_SP...  7.43 us
    unnamed x19, local copies, waits for them, and re-layouts  3.49 us
    pallas_call x1, Pallas kernels, split_pieces(): pl.pallas_call(lambda *refs: split_kernel(space_count, *refs), out_shape=...  1.82 us
    pallas_call x1, Pallas kernels, project(): pl.pallas_call(lambda *refs: project_kernel(width, *refs), out_shape=[jax...  1.8 us
  transfers between devices with their start and end apart: 19, of which 18 were waited for; matrix products, arithmetic and copies ran while one was open for 2% of the time, Pallas kernels for 0%

profile of v1, /device:TPU:0, one launch (start us, length us, event | category | flops | bytes accessed | tf_op | source)
XLA Modules:
  0.0 69.8 jit_solution(12408681146257611687)
XLA Ops:
  1.8 0.7 %collective-permute-done.refs_2_ = f32[16,4096]{1,0:T(8,128)S(1)} collective-permute-done((f32[16,4096]{1,0:T(8,128)}, f32[16,4096]{1,0:T(8,128)S(1)}, u32[]{:S(2)}, u32[]{:S(2)}) %collective-permute-start) | collective-permute-done | bytes 262176 | tf_op jit(solution)/shard_map/ppermute | solution.py:21
  2.6 0.7 %copy-done.4 = f32[16,4096]{1,0:T(8,128)} copy-done((f32[16,4096]{1,0:T(8,128)}, f32[16,4096]{1,0:T(8,128)S(1)}, u32[]{:S(2)}) %copy-start.4) | copy-done | bytes 262168
  3.3 1.8 %split_pieces.1 = (f32[2,16,512]{2,1,0:T(8,128)}, f32[2,16,512]{2,1,0:T(8,128)}, f32[2,16,512]{2,1,0:T(8,128)}, f32[2,16,512]{2,1,0:T(8,128)}) custom-call(s32[2]{0:T(128)} %pad_add_fusion.refs_0_.pos_ref, f32[16,4096]{1,0:T(8,128)} %bitcast.14, f32[16,4096]{1,0:T(8,128)} %copy-done.4, f32[1,64]{1,0:T(1,128)} %bitcast.15), custom_call_target="tpu_custom_call" | custom-call | tf_op jit(solution)/shard_map/split_pieces/pallas_call | solution.py:49
  5.1 2.9 %collective-permute-start.1 = (f32[2,16,512]{2,1,0:T(8,128)}, f32[2,16,512]{2,1,0:T(8,128)S(1)}, u32[]{:S(2)}, u32[]{:S(2)}) collective-permute-start(f32[2,16,512]{2,1,0:T(8,128)} %get-tuple-element.12), channel_id=1, source_target_pairs={{0,2},{1,3},{2,0},{3,1},{4,6},{5,7},{6,4},{7,5},{8,10},{9,11},{10,... | collective-permute-start | bytes 196616 | tf_op jit(solution)/shard_map/ppermute | solution.py:21
  8.0 2.6 %collective-permute-start.2 = (f32[2,16,512]{2,1,0:T(8,128)}, f32[2,16,512]{2,1,0:T(8,128)S(1)}, u32[]{:S(2)}, u32[]{:S(2)}) collective-permute-start(f32[2,16,512]{2,1,0:T(8,128)} %get-tuple-element.13), channel_id=1, source_target_pairs={{0,4},{1,5},{2,6},{3,7},{4,0},{5,1},{6,2},{7,3},{8,12},{9,13},{10,... | collective-permute-start | bytes 196616 | tf_op jit(solution)/shard_map/ppermute | solution.py:21
  10.6 0.8 %constant_dynamic-update-slice_fusion.3 = f32[8,16,512]{2,1,0:T(8,128)S(1)} fusion(f32[2,16,512]{2,1,0:T(8,128)} %get-tuple-element.11), kind=kLoop, calls=%fused_computation.12 | loop fusion | bytes 131072
  11.5 4.3 %collective-permute-done.2 = f32[2,16,512]{2,1,0:T(8,128)S(1)} collective-permute-done((f32[2,16,512]{2,1,0:T(8,128)}, f32[2,16,512]{2,1,0:T(8,128)S(1)}, u32[]{:S(2)}, u32[]{:S(2)}) %collective-permute-start.2) | collective-permute-done | bytes 65568 | tf_op jit(solution)/shard_map/ppermute | solution.py:21
  15.8 1.2 %collective-permute-done.3 = f32[2,16,512]{2,1,0:T(8,128)S(1)} collective-permute-done((f32[2,16,512]{2,1,0:T(8,128)}, f32[2,16,512]{2,1,0:T(8,128)S(1)}, u32[]{:S(2)}, u32[]{:S(2)}) %collective-permute-start.3) | collective-permute-done | bytes 65568 | tf_op jit(solution)/shard_map/ppermute | solution.py:21
  17.0 2.5 %collective-permute-start.6 = (f32[8,16,512]{2,1,0:T(8,128)S(1)}, f32[8,16,512]{2,1,0:T(8,128)S(1)}, u32[]{:S(2)}, u32[]{:S(2)}) collective-permute-start(f32[8,16,512]{2,1,0:T(8,128)S(1)} %constant_dynamic-update-slice_fusion.refs_0_), channel_id=1, source_target_pairs={{0,24},{8,16},{16,8},{24,0},{1,25},{9,17},{17,9},{25,1},{2,26},{10... | collective-permute-start | bytes 786440 | tf_op jit(solution)/shard_map/ppermute | solution.py:21
  20.5 6.6 %collective-permute-done.6.refs_3_ = f32[8,16,512]{2,1,0:T(8,128)S(1)} collective-permute-done((f32[8,16,512]{2,1,0:T(8,128)S(1)}, f32[8,16,512]{2,1,0:T(8,128)S(1)}, u32[]{:S(2)}, u32[]{:S(2)}) %collective-permute-start.6) | collective-permute-done | bytes 262176 | tf_op jit(solution)/shard_map/ppermute | solution.py:21
  27.2 3.0 %collective-permute-done.5.refs_2_ = f32[8,16,512]{2,1,0:T(8,128)S(1)} collective-permute-done((f32[8,16,512]{2,1,0:T(8,128)S(1)}, f32[8,16,512]{2,1,0:T(8,128)S(1)}, u32[]{:S(2)}, u32[]{:S(2)}) %collective-permute-start.5) | collective-permute-done | bytes 262176 | tf_op jit(solution)/shard_map/ppermute | solution.py:21
  30.9 0.7 %copy-done.3 = f32[8,16,512]{2,1,0:T(8,128)} copy-done((f32[8,16,512]{2,1,0:T(8,128)}, f32[8,16,512]{2,1,0:T(8,128)S(1)}, u32[]{:S(2)}) %copy-start.3) | copy-done | bytes 262168
  31.6 7.4 %multiply.2 = (f32[4,64,128]{2,1,0:T(8,128)}, f32[4,64,128]{2,1,0:T(8,128)}) custom-call(s32[2]{0:T(128)} %pad_add_fusion.refs_0_.pos_ref, f32[8,16,512]{2,1,0:T(8,128)} %copy-done, f32[8,16,512]{2,1,0:T(8,128)} %copy-done.3, f32[8,16,512]{2,1,0:T(8,128)} %copy-done.2, f32[8,16,512]{2,1,0:T(8,128)} %copy-done.1, bf16[1024,4096]{1,0:T(8,128)(2,1)} %refs_4_.1), custom_call_target="tpu_custom_call" | custom-call | tf_op jit(solution)/shard_map/multiply/pallas_call | solution.py:107
  39.1 1.6 %collective-permute-done.7 = f32[4,64,128]{2,1,0:T(8,128)S(1)} collective-permute-done((f32[4,64,128]{2,1,0:T(8,128)}, f32[4,64,128]{2,1,0:T(8,128)S(1)}, u32[]{:S(2)}, u32[]{:S(2)}) %collective-permute-start.7) | collective-permute-done | bytes 131104 | tf_op jit(solution)/shard_map/ppermute | solution.py:21
  40.6 0.9 %add.28 = f32[4,64,128]{2,1,0:T(8,128)S(1)} add(f32[4,64,128]{2,1,0:T(8,128)} %get-tuple-element.15, f32[4,64,128]{2,1,0:T(8,128)S(1)} %collective-permute-done.7) | non-fusion elementwise | flops 32768 | bytes 393216 | tf_op jit(solution)/shard_map/add | solution.py:170
  42.2 1.3 %collective-permute-start.10 = (f32[64,128]{1,0:T(8,128)S(1)}, f32[64,128]{1,0:T(8,128)S(1)}, u32[]{:S(2)}, u32[]{:S(2)}) collective-permute-start(f32[64,128]{1,0:T(8,128)S(1)} %get-tuple-element.20), channel_id=1, source_target_pairs={{0,6},{1,7},{2,4},{3,5},{4,2},{5,3},{6,0},{7,1},{8,14},{9,15},{10,... | collective-permute-start | bytes 98312 | tf_op jit(solution)/shard_map/ppermute | solution.py:21
  43.5 1.3 %collective-permute-start.9 = (f32[64,128]{1,0:T(8,128)S(1)}, f32[64,128]{1,0:T(8,128)S(1)}, u32[]{:S(2)}, u32[]{:S(2)}) collective-permute-start(f32[64,128]{1,0:T(8,128)S(1)} %get-tuple-element.21), channel_id=1, source_target_pairs={{0,4},{1,5},{2,6},{3,7},{4,0},{5,1},{6,2},{7,3},{8,12},{9,13},{10,... | collective-permute-start | bytes 98312 | tf_op jit(solution)/shard_map/ppermute | solution.py:21
  44.9 1.7 %collective-permute-start.8 = (f32[64,128]{1,0:T(8,128)S(1)}, f32[64,128]{1,0:T(8,128)S(1)}, u32[]{:S(2)}, u32[]{:S(2)}) collective-permute-start(f32[64,128]{1,0:T(8,128)S(1)} %get-tuple-element.22), channel_id=1, source_target_pairs={{0,2},{1,3},{2,0},{3,1},{4,6},{5,7},{6,4},{7,5},{8,10},{9,11},{10,... | collective-permute-start | bytes 98312 | tf_op jit(solution)/shard_map/ppermute | solution.py:21
  46.6 1.6 %collective-permute-done.10.refs_4_ = f32[64,128]{1,0:T(8,128)S(1)} collective-permute-done((f32[64,128]{1,0:T(8,128)S(1)}, f32[64,128]{1,0:T(8,128)S(1)}, u32[]{:S(2)}, u32[]{:S(2)}) %collective-permute-start.10) | collective-permute-done | bytes 32800 | tf_op jit(solution)/shard_map/ppermute | solution.py:21
  49.6 1.8 %project.1 = (bf16[64,128]{1,0:T(8,128)(2,1)}, f32[32,256]{1,0:T(8,128)}, f32[32,256]{1,0:T(8,128)}) custom-call(s32[2]{0:T(128)} %pad_add_fusion.refs_0_.pos_ref, f32[64,128]{1,0:T(8,128)} %get-tuple-element.23.refs_1_, f32[64,128]{1,0:T(8,128)} %copy-done.7, f32[64,128]{1,0:T(8,128)} %copy-done.6, f32[64,128]{1,0:T(8,128)} %copy-done.5, ...), custom_call_target="tpu_custom_call" | custom-call | tf_op jit(solution)/shard_map/project/pallas_call | solution.py:144
  51.4 1.4 %collective-permute-done.11 = f32[32,256]{1,0:T(8,128)S(1)} collective-permute-done((f32[32,256]{1,0:T(8,128)}, f32[32,256]{1,0:T(8,128)S(1)}, u32[]{:S(2)}, u32[]{:S(2)}) %collective-permute-start.11) | collective-permute-done | bytes 32800 | tf_op jit(solution)/shard_map/ppermute | solution.py:21
  52.8 0.8 %add.30 = f32[32,256]{1,0:T(8,128)S(1)} add(f32[32,256]{1,0:T(8,128)} %get-tuple-element.18, f32[32,256]{1,0:T(8,128)S(1)} %collective-permute-done.11) | non-fusion elementwise | flops 8192 | bytes 98304 | tf_op jit(solution)/shard_map/add | solution.py:174
  53.5 2.3 %collective-permute-start.14 = (f32[32,256]{1,0:T(8,128)S(1)}, f32[32,256]{1,0:T(8,128)S(1)}, u32[]{:S(2)}, u32[]{:S(2)}) collective-permute-start(f32[32,256]{1,0:T(8,128)S(1)} %add.30), channel_id=1, source_target_pairs={{0,6},{1,7},{2,4},{3,5},{4,2},{5,3},{6,0},{7,1},{8,14},{9,15},{10,... | collective-permute-start | bytes 98312 | tf_op jit(solution)/shard_map/ppermute | solution.py:21
  55.9 0.7 collective-permute-start.13
  56.5 1.4 %collective-permute-start.12 = (f32[32,256]{1,0:T(8,128)S(1)}, f32[32,256]{1,0:T(8,128)S(1)}, u32[]{:S(2)}, u32[]{:S(2)}) collective-permute-start(f32[32,256]{1,0:T(8,128)S(1)} %add.30), channel_id=1, source_target_pairs={{0,2},{1,3},{2,0},{3,1},{4,6},{5,7},{6,4},{7,5},{8,10},{9,11},{10,... | collective-permute-start | bytes 98312 | tf_op jit(solution)/shard_map/ppermute | solution.py:21
  57.9 1.4 %collective-permute-done.14 = f32[32,256]{1,0:T(8,128)S(1)} collective-permute-done((f32[32,256]{1,0:T(8,128)S(1)}, f32[32,256]{1,0:T(8,128)S(1)}, u32[]{:S(2)}, u32[]{:S(2)}) %collective-permute-start.14) | collective-permute-done | bytes 32800 | tf_op jit(solution)/shard_map/ppermute | solution.py:21
  59.4 1.3 %collective-permute-done.13 = f32[32,256]{1,0:T(8,128)S(1)} collective-permute-done((f32[32,256]{1,0:T(8,128)S(1)}, f32[32,256]{1,0:T(8,128)S(1)}, u32[]{:S(2)}, u32[]{:S(2)}) %collective-permute-start.13) | collective-permute-done | bytes 32800 | tf_op jit(solution)/shard_map/ppermute | solution.py:21
  60.9 1.8 %collective-permute-start.17 = (f32[32,256]{1,0:T(8,128)S(1)}, f32[32,256]{1,0:T(8,128)S(1)}, u32[]{:S(2)}, u32[]{:S(2)}) collective-permute-start(f32[32,256]{1,0:T(8,128)S(1)} %add_add_fusion.1), channel_id=1, source_target_pairs={{0,24},{8,16},{16,8},{24,0},{1,25},{9,17},{17,9},{25,1},{2,26},{10... | collective-permute-start | bytes 98312 | tf_op jit(solution)/shard_map/ppermute | solution.py:21
  62.7 1.2 %collective-permute-start.16 = (f32[32,256]{1,0:T(8,128)S(1)}, f32[32,256]{1,0:T(8,128)S(1)}, u32[]{:S(2)}, u32[]{:S(2)}) collective-permute-start(f32[32,256]{1,0:T(8,128)S(1)} %add_add_fusion.1), channel_id=1, source_target_pairs={{0,16},{8,24},{16,0},{24,8},{1,17},{9,25},{17,1},{25,9},{2,18},{10... | collective-permute-start | bytes 98312 | tf_op jit(solution)/shard_map/ppermute | solution.py:21
  64.5 1.6 %collective-permute-done.17 = f32[32,256]{1,0:T(8,128)S(1)} collective-permute-done((f32[32,256]{1,0:T(8,128)S(1)}, f32[32,256]{1,0:T(8,128)S(1)}, u32[]{:S(2)}, u32[]{:S(2)}) %collective-permute-start.17) | collective-permute-done | bytes 32800 | tf_op jit(solution)/shard_map/ppermute | solution.py:21
  66.6 1.2 %collective-permute-done.15 = f32[32,256]{1,0:T(8,128)S(1)} collective-permute-done((f32[32,256]{1,0:T(8,128)S(1)}, f32[32,256]{1,0:T(8,128)S(1)}, u32[]{:S(2)}, u32[]{:S(2)}) %collective-permute-start.15) | collective-permute-done | bytes 32800 | tf_op jit(solution)/shard_map/ppermute | solution.py:21
  67.9 1.2 %collective-permute-done.18 = f32[32,256]{1,0:T(8,128)S(1)} collective-permute-done((f32[32,256]{1,0:T(8,128)S(1)}, f32[32,256]{1,0:T(8,128)S(1)}, u32[]{:S(2)}, u32[]{:S(2)}) %collective-permute-start.18) | collective-permute-done | bytes 32800 | tf_op jit(solution)/shard_map/ppermute | solution.py:21
  (37 shorter events, 7.1 us)
Async XLA Ops:
  0.6 1.9 %collective-permute-start = (f32[16,4096]{1,0:T(8,128)}, f32[16,4096]{1,0:T(8,128)S(1)}, u32[]{:S(2)}, u32[]{:S(2)}) collective-permute-start(f32[16,4096]{1,0:T(8,128)} %bitcast.13), channel_id=1, source_target_pairs={{0,1},{1,0},{2,3},{3,2},{4,5},{5,4},{6,7},{7,6},{8,9},{9,8},{10,11... | collective-permute-start | bytes 786440 | tf_op jit(solution)/shard_map/ppermute | solution.py:21
  2.6 0.7 %copy-start.4 = (f32[16,4096]{1,0:T(8,128)}, f32[16,4096]{1,0:T(8,128)S(1)}, u32[]{:S(2)}) copy-start(f32[16,4096]{1,0:T(8,128)S(1)} %collective-permute-done.refs_2_) | copy-start | bytes 786436
  5.1 6.4 %collective-permute-start.1 = (f32[2,16,512]{2,1,0:T(8,128)}, f32[2,16,512]{2,1,0:T(8,128)S(1)}, u32[]{:S(2)}, u32[]{:S(2)}) collective-permute-start(f32[2,16,512]{2,1,0:T(8,128)} %get-tuple-element.12), channel_id=1, source_target_pairs={{0,2},{1,3},{2,0},{3,1},{4,6},{5,7},{6,4},{7,5},{8,10},{9,11},{10,... | collective-permute-start | bytes 196616 | tf_op jit(solution)/shard_map/ppermute | solution.py:21
  8.0 7.7 %collective-permute-start.2 = (f32[2,16,512]{2,1,0:T(8,128)}, f32[2,16,512]{2,1,0:T(8,128)S(1)}, u32[]{:S(2)}, u32[]{:S(2)}) collective-permute-start(f32[2,16,512]{2,1,0:T(8,128)} %get-tuple-element.13), channel_id=1, source_target_pairs={{0,4},{1,5},{2,6},{3,7},{4,0},{5,1},{6,2},{7,3},{8,12},{9,13},{10,... | collective-permute-start | bytes 196616 | tf_op jit(solution)/shard_map/ppermute | solution.py:21
  10.6 6.4 %collective-permute-start.3 = (f32[2,16,512]{2,1,0:T(8,128)}, f32[2,16,512]{2,1,0:T(8,128)S(1)}, u32[]{:S(2)}, u32[]{:S(2)}) collective-permute-start(f32[2,16,512]{2,1,0:T(8,128)} %get-tuple-element.14), channel_id=1, source_target_pairs={{0,6},{1,7},{2,4},{3,5},{4,2},{5,3},{6,0},{7,1},{8,14},{9,15},{10,... | collective-permute-start | bytes 196616 | tf_op jit(solution)/shard_map/ppermute | solution.py:21
  17.0 13.3 %copy-start = (f32[8,16,512]{2,1,0:T(8,128)}, f32[8,16,512]{2,1,0:T(8,128)S(1)}, u32[]{:S(2)}) copy-start(f32[8,16,512]{2,1,0:T(8,128)S(1)} %constant_dynamic-update-slice_fusion.refs_0_) | copy-start | bytes 786436
  17.0 10.2 %collective-permute-start.6 = (f32[8,16,512]{2,1,0:T(8,128)S(1)}, f32[8,16,512]{2,1,0:T(8,128)S(1)}, u32[]{:S(2)}, u32[]{:S(2)}) collective-permute-start(f32[8,16,512]{2,1,0:T(8,128)S(1)} %constant_dynamic-update-slice_fusion.refs_0_), channel_id=1, source_target_pairs={{0,24},{8,16},{16,8},{24,0},{1,25},{9,17},{17,9},{25,1},{2,26},{10... | collective-permute-start | bytes 786440 | tf_op jit(solution)/shard_map/ppermute | solution.py:21
  19.5 10.7 %collective-permute-start.5 = (f32[8,16,512]{2,1,0:T(8,128)S(1)}, f32[8,16,512]{2,1,0:T(8,128)S(1)}, u32[]{:S(2)}, u32[]{:S(2)}) collective-permute-start(f32[8,16,512]{2,1,0:T(8,128)S(1)} %constant_dynamic-update-slice_fusion.refs_0_), channel_id=1, source_target_pairs={{0,16},{8,24},{16,0},{24,8},{1,17},{9,25},{17,1},{25,9},{2,18},{10... | collective-permute-start | bytes 786440 | tf_op jit(solution)/shard_map/ppermute | solution.py:21
  20.0 10.3 %collective-permute-start.4 = (f32[8,16,512]{2,1,0:T(8,128)S(1)}, f32[8,16,512]{2,1,0:T(8,128)S(1)}, u32[]{:S(2)}, u32[]{:S(2)}) collective-permute-start(f32[8,16,512]{2,1,0:T(8,128)S(1)} %constant_dynamic-update-slice_fusion.refs_0_), channel_id=1, source_target_pairs={{0,8},{8,0},{16,24},{24,16},{1,9},{9,1},{17,25},{25,17},{2,10},{10... | collective-permute-start | bytes 786440 | tf_op jit(solution)/shard_map/ppermute | solution.py:21
  27.2 3.1 %copy-start.1 = (f32[8,16,512]{2,1,0:T(8,128)}, f32[8,16,512]{2,1,0:T(8,128)S(1)}, u32[]{:S(2)}) copy-start(f32[8,16,512]{2,1,0:T(8,128)S(1)} %collective-permute-done.6.refs_3_) | copy-start | bytes 786436
  30.2 0.7 %copy-start.2 = (f32[8,16,512]{2,1,0:T(8,128)}, f32[8,16,512]{2,1,0:T(8,128)S(1)}, u32[]{:S(2)}) copy-start(f32[8,16,512]{2,1,0:T(8,128)S(1)} %collective-permute-done.5.refs_2_) | copy-start | bytes 786436
  30.9 0.7 %copy-start.3 = (f32[8,16,512]{2,1,0:T(8,128)}, f32[8,16,512]{2,1,0:T(8,128)S(1)}, u32[]{:S(2)}) copy-start(f32[8,16,512]{2,1,0:T(8,128)S(1)} %collective-permute-done.4.refs_1_) | copy-start | bytes 786436
  39.1 1.6 %collective-permute-start.7 = (f32[4,64,128]{2,1,0:T(8,128)}, f32[4,64,128]{2,1,0:T(8,128)S(1)}, u32[]{:S(2)}, u32[]{:S(2)}) collective-permute-start(f32[4,64,128]{2,1,0:T(8,128)} %get-tuple-element.16), channel_id=1, source_target_pairs={{0,1},{1,0},{2,3},{3,2},{4,5},{5,4},{6,7},{7,6},{8,9},{9,8},{10,11... | collective-permute-start | bytes 393224 | tf_op jit(solution)/shard_map/ppermute | solution.py:21
  42.2 6.0 %collective-permute-start.10 = (f32[64,128]{1,0:T(8,128)S(1)}, f32[64,128]{1,0:T(8,128)S(1)}, u32[]{:S(2)}, u32[]{:S(2)}) collective-permute-start(f32[64,128]{1,0:T(8,128)S(1)} %get-tuple-element.20), channel_id=1, source_target_pairs={{0,6},{1,7},{2,4},{3,5},{4,2},{5,3},{6,0},{7,1},{8,14},{9,15},{10,... | collective-permute-start | bytes 98312 | tf_op jit(solution)/shard_map/ppermute | solution.py:21
  43.5 5.1 %collective-permute-start.9 = (f32[64,128]{1,0:T(8,128)S(1)}, f32[64,128]{1,0:T(8,128)S(1)}, u32[]{:S(2)}, u32[]{:S(2)}) collective-permute-start(f32[64,128]{1,0:T(8,128)S(1)} %get-tuple-element.21), channel_id=1, source_target_pairs={{0,4},{1,5},{2,6},{3,7},{4,0},{5,1},{6,2},{7,3},{8,12},{9,13},{10,... | collective-permute-start | bytes 98312 | tf_op jit(solution)/shard_map/ppermute | solution.py:21
  44.9 4.1 %collective-permute-start.8 = (f32[64,128]{1,0:T(8,128)S(1)}, f32[64,128]{1,0:T(8,128)S(1)}, u32[]{:S(2)}, u32[]{:S(2)}) collective-permute-start(f32[64,128]{1,0:T(8,128)S(1)} %get-tuple-element.22), channel_id=1, source_target_pairs={{0,2},{1,3},{2,0},{3,1},{4,6},{5,7},{6,4},{7,5},{8,10},{9,11},{10,... | collective-permute-start | bytes 98312 | tf_op jit(solution)/shard_map/ppermute | solution.py:21
  48.2 0.8 %copy-start.5 = (f32[64,128]{1,0:T(8,128)}, f32[64,128]{1,0:T(8,128)S(1)}, u32[]{:S(2)}) copy-start(f32[64,128]{1,0:T(8,128)S(1)} %collective-permute-done.10.refs_4_) | copy-start | bytes 98308
  48.6 0.6 copy-start.6
  49.0 0.6 copy-start.7
  51.4 1.4 %collective-permute-start.11 = (f32[32,256]{1,0:T(8,128)}, f32[32,256]{1,0:T(8,128)S(1)}, u32[]{:S(2)}, u32[]{:S(2)}) collective-permute-start(f32[32,256]{1,0:T(8,128)} %get-tuple-element.19), channel_id=1, source_target_pairs={{0,1},{1,0},{2,3},{3,2},{4,5},{5,4},{6,7},{7,6},{8,9},{9,8},{10,11... | collective-permute-start | bytes 98312 | tf_op jit(solution)/shard_map/ppermute | solution.py:21
  53.5 5.8 %collective-permute-start.14 = (f32[32,256]{1,0:T(8,128)S(1)}, f32[32,256]{1,0:T(8,128)S(1)}, u32[]{:S(2)}, u32[]{:S(2)}) collective-permute-start(f32[32,256]{1,0:T(8,128)S(1)} %add.30), channel_id=1, source_target_pairs={{0,6},{1,7},{2,4},{3,5},{4,2},{5,3},{6,0},{7,1},{8,14},{9,15},{10,... | collective-permute-start | bytes 98312 | tf_op jit(solution)/shard_map/ppermute | solution.py:21
  55.9 4.8 %collective-permute-start.13 = (f32[32,256]{1,0:T(8,128)S(1)}, f32[32,256]{1,0:T(8,128)S(1)}, u32[]{:S(2)}, u32[]{:S(2)}) collective-permute-start(f32[32,256]{1,0:T(8,128)S(1)} %add.30), channel_id=1, source_target_pairs={{0,4},{1,5},{2,6},{3,7},{4,0},{5,1},{6,2},{7,3},{8,12},{9,13},{10,... | collective-permute-start | bytes 98312 | tf_op jit(solution)/shard_map/ppermute | solution.py:21
  56.5 4.3 %collective-permute-start.12 = (f32[32,256]{1,0:T(8,128)S(1)}, f32[32,256]{1,0:T(8,128)S(1)}, u32[]{:S(2)}, u32[]{:S(2)}) collective-permute-start(f32[32,256]{1,0:T(8,128)S(1)} %add.30), channel_id=1, source_target_pairs={{0,2},{1,3},{2,0},{3,1},{4,6},{5,7},{6,4},{7,5},{8,10},{9,11},{10,... | collective-permute-start | bytes 98312 | tf_op jit(solution)/shard_map/ppermute | solution.py:21
  60.9 5.1 %collective-permute-start.17 = (f32[32,256]{1,0:T(8,128)S(1)}, f32[32,256]{1,0:T(8,128)S(1)}, u32[]{:S(2)}, u32[]{:S(2)}) collective-permute-start(f32[32,256]{1,0:T(8,128)S(1)} %add_add_fusion.1), channel_id=1, source_target_pairs={{0,24},{8,16},{16,8},{24,0},{1,25},{9,17},{17,9},{25,1},{2,26},{10... | collective-permute-start | bytes 98312 | tf_op jit(solution)/shard_map/ppermute | solution.py:21
  62.7 3.9 %collective-permute-start.16 = (f32[32,256]{1,0:T(8,128)S(1)}, f32[32,256]{1,0:T(8,128)S(1)}, u32[]{:S(2)}, u32[]{:S(2)}) collective-permute-start(f32[32,256]{1,0:T(8,128)S(1)} %add_add_fusion.1), channel_id=1, source_target_pairs={{0,16},{8,24},{16,0},{24,8},{1,17},{9,25},{17,1},{25,9},{2,18},{10... | collective-permute-start | bytes 98312 | tf_op jit(solution)/shard_map/ppermute | solution.py:21
  63.9 3.9 %collective-permute-start.15 = (f32[32,256]{1,0:T(8,128)S(1)}, f32[32,256]{1,0:T(8,128)S(1)}, u32[]{:S(2)}, u32[]{:S(2)}) collective-permute-start(f32[32,256]{1,0:T(8,128)S(1)} %add_add_fusion.1), channel_id=1, source_target_pairs={{0,8},{8,0},{16,24},{24,16},{1,9},{9,1},{17,25},{25,17},{2,10},{10... | collective-permute-start | bytes 98312 | tf_op jit(solution)/shard_map/ppermute | solution.py:21
  67.8 1.3 %collective-permute-start.18 = (f32[32,256]{1,0:T(8,128)S(1)}, f32[32,256]{1,0:T(8,128)S(1)}, u32[]{:S(2)}, u32[]{:S(2)}) collective-permute-start(f32[32,256]{1,0:T(8,128)S(1)} %add_add_fusion), channel_id=1, source_target_pairs={{0,1},{1,0},{2,3},{3,2},{4,5},{5,4},{6,7},{7,6},{8,9},{9,8},{10,11... | collective-permute-start | bytes 98312 | tf_op jit(solution)/shard_map/ppermute | solution.py:21

commit v2 on v1

v2 whole, which is shorter than its diff:
```python
import math

import jax
import jax.numpy as jnp
from jax import lax
from jax.experimental import pallas as pl
from jax.experimental.pallas import tpu as pltpu
from jax.sharding import PartitionSpec as P

ROW_BLOCK = 16
COL_BLOCK = 4
LANES = 128
SUBLANES = 8
GROUPS = LANES // ROW_BLOCK
MIB = 1 << 20
IN_SMEM = pl.BlockSpec(memory_space=pltpu.SMEM)
IN_VMEM = pl.BlockSpec(memory_space=pltpu.VMEM)
IN_HBM = pl.BlockSpec(memory_space=pltpu.HBM)


def params(mib):
    return pltpu.CompilerParams(vmem_limit_bytes=mib * MIB)


def swap(value, axis, mask):
    count = lax.axis_size(axis)
    return lax.ppermute(value, axis, [(i, i ^ mask) for i in range(count)])


def tree_sum(terms):
    while len(terms) > 1:
        terms = [terms[i] + terms[i + 1] for i in range(0, len(terms), 2)]
    return terms[0]


def widen_kernel(pos_ref, held_ref, keep_ref, send_ref):
    half = keep_ref.shape[1]
    core = pos_ref[0] & 1
    keep_ref[...] = held_ref[:, pl.ds(pl.multiple_of(core * half, LANES), half)].astype(jnp.float32)
    send_ref[...] = held_ref[:, pl.ds(pl.multiple_of((1 - core) * half, LANES), half)].astype(jnp.float32)


def widen(pos, held):
    rows, columns = held.shape
    half = jax.ShapeDtypeStruct((rows, columns // 2), jnp.float32)
    return pl.pallas_call(
        widen_kernel,
        out_shape=[half, half],
        in_specs=[IN_SMEM, IN_VMEM],
        out_specs=[IN_VMEM, IN_VMEM],
        compiler_params=params(2),
        name="widen",
    )(pos, held)


def split_kernel(space_count, pos_ref, own_ref, other_ref, eig_ref, *out_refs):
    p, q = pos_ref[0], pos_ref[1]
    width = own_ref.shape[0]
    chunk = out_refs[0].shape[2]
    row = lax.broadcasted_iota(jnp.int32, (width, eig_ref.shape[1]), 0)
    mode = lax.broadcasted_iota(jnp.int32, (width, eig_ref.shape[1]), 1)
    mine = (row // COL_BLOCK * space_count + q) * COL_BLOCK + row % COL_BLOCK
    picked = jnp.where(mode == mine, eig_ref[...], 0.0)
    scale = lax.rsqrt(jnp.sum(picked, axis=1, keepdims=True))
    for d, out_ref in enumerate(out_refs):
        start = pl.multiple_of((p ^ (2 * d)) * chunk, LANES)
        out_ref[0] = own_ref[:, pl.ds(start, chunk)] * scale
        out_ref[1] = other_ref[:, pl.ds(start, chunk)] * scale


def split_pieces(pos, own, other, eig, snap_count, space_count):
    width, rows = own.shape
    chunk = rows // snap_count
    piece = jax.ShapeDtypeStruct((2, width, chunk), jnp.float32)
    return pl.pallas_call(
        lambda *refs: split_kernel(space_count, *refs),
        out_shape=[piece] * (snap_count // 2),
        in_specs=[IN_SMEM, IN_VMEM, IN_VMEM, IN_VMEM],
        out_specs=[IN_VMEM] * (snap_count // 2),
        compiler_params=params(4),
        name="split_pieces",
    )(pos, own, other, eig)


def stage_kernel(after_ref, source_ref, target_ref, sem):
    copy = pltpu.make_async_copy(source_ref, target_ref, sem)
    copy.start()
    copy.wait()


def stage(after, snapshots):
    size = snapshots.size * snapshots.dtype.itemsize
    return pl.pallas_call(
        stage_kernel,
        out_shape=jax.ShapeDtypeStruct(snapshots.shape, snapshots.dtype),
        in_specs=[IN_VMEM, IN_HBM],
        out_specs=IN_VMEM,
        scratch_shapes=[pltpu.SemaphoreType.DMA],
        compiler_params=params(12),
        cost_estimate=pl.CostEstimate(flops=0, bytes_accessed=2 * size, transcendentals=0),
        name="stage",
    )(after, snapshots)


def interleave(blocks):
    lane = lax.broadcasted_iota(jnp.int32, blocks[0].shape, 1) // ROW_BLOCK
    step = 1
    while step < GROUPS:
        high = (lane & step) != 0
        mixed = list(blocks)
        for a in range(GROUPS):
            if a & step == 0:
                b = a | step
                low_of_b = pltpu.roll(blocks[b], step * ROW_BLOCK, 1)
                high_of_a = pltpu.roll(blocks[a], LANES - step * ROW_BLOCK, 1)
                mixed[a] = jnp.where(high, low_of_b, blocks[a])
                mixed[b] = jnp.where(high, blocks[b], high_of_a)
        blocks = mixed
        step *= 2
    return blocks


def all_modes(slab_ref, q, slot, t):
    space_count, _, width, _ = slab_ref.shape
    low = lax.broadcasted_iota(jnp.int32, (SUBLANES, LANES), 0) < COL_BLOCK
    pairs = space_count // 2
    tiles = [None] * (space_count * width // SUBLANES)
    lanes = slice(t * LANES, (t + 1) * LANES)
    for u in range(pairs):
        for i in range(width // SUBLANES):
            rows = slice(i * SUBLANES, (i + 1) * SUBLANES)
            even = slab_ref[q ^ (2 * u), slot, rows, lanes]
            odd = slab_ref[q ^ (2 * u + 1), slot, rows, lanes]
            tiles[2 * i * pairs + u] = jnp.where(low, even, pltpu.roll(odd, COL_BLOCK, 0))
            tiles[(2 * i + 1) * pairs + u] = jnp.where(low, pltpu.roll(even, COL_BLOCK, 0), odd)
    return jnp.concatenate(tiles)


def multiply_kernel(pos_ref, slab_ref, snap_ref, out_ref, scaled_ref, cells_ref):
    p, q = pos_ref[0], pos_ref[1]
    _, snap_count, _, chunk = slab_ref.shape
    outer_count = snap_count // GROUPS
    for outer in range(outer_count):
        for t in range(chunk // LANES):
            slots = [p ^ (outer * GROUPS + g) for g in range(GROUPS)]
            for j, block in enumerate(interleave([all_modes(slab_ref, q, slot, t) for slot in slots])):
                tile = (t * GROUPS + j) * outer_count + outer
                scaled_ref[:, tile * LANES : (tile + 1) * LANES] = block.astype(jnp.bfloat16)
    total = lax.dot_general(
        snap_ref[...], scaled_ref[...], (((1,), (1,)), ((), ())), preferred_element_type=jnp.float32
    ).T
    cells = cells_ref.shape[2]
    for owner in range(snap_count):
        cells_ref[owner] = total[:, owner * cells : (owner + 1) * cells]
    for s in range(snap_count):
        out_ref[s] = cells_ref[p ^ s]


def multiply(pos, slab, snapshots):
    space_count, snap_count, width, _ = slab.shape
    cells, depth = snapshots.shape
    modes = width * space_count
    out = (snap_count, modes, cells // snap_count)
    return pl.pallas_call(
        multiply_kernel,
        out_shape=jax.ShapeDtypeStruct(out, jnp.float32),
        in_specs=[IN_SMEM, IN_VMEM, IN_VMEM],
        out_specs=IN_VMEM,
        scratch_shapes=[pltpu.VMEM((modes, depth), jnp.bfloat16), pltpu.VMEM(out, jnp.float32)],
        compiler_params=params(12),
        name="multiply",
    )(pos, slab, snapshots)


def pair_kernel(mine_ref, theirs_ref, *refs):
    held_refs, (coef_ref, *sum_refs) = refs[: len(refs) // 2], refs[len(refs) // 2 :]
    snap_count, modes, _ = mine_ref.shape
    total = jnp.zeros(coef_ref.shape, jnp.float32)
    sums = [mine_ref[s] + theirs_ref[s ^ 1] for s in range(snap_count)]
    for d, sum_ref in enumerate(sum_refs):
        sum_ref[...] = sums[2 * d]
    held = [held_refs[s // 2][s % 2].astype(jnp.bfloat16) for s in range(snap_count)]
    wide = jnp.concatenate(sums, axis=1)
    high = wide.astype(jnp.bfloat16)
    low = (wide - high.astype(jnp.float32)).astype(jnp.bfloat16)
    both = jnp.dot(
        jnp.concatenate([high, low]), jnp.concatenate(held), preferred_element_type=jnp.float32
    )
    coef_ref[...] = both[:modes] + both[modes:]


def pair(mine, theirs, held):
    snap_count, modes, cells = mine.shape
    columns = held[0].shape[2]
    return pl.pallas_call(
        pair_kernel,
        out_shape=[jax.ShapeDtypeStruct((modes, columns), jnp.float32)]
        + [jax.ShapeDtypeStruct((modes, cells), jnp.float32)] * (snap_count // 2),
        in_specs=[IN_VMEM] * (2 + len(held)),
        out_specs=[IN_VMEM] * (1 + snap_count // 2),
        compiler_params=params(6),
        name="pair",
    )(mine, theirs, *held)


def per_device(snapshots, vectors_cyclic, eigen_values, held_out):
    snap_count = lax.axis_size("snap")
    space_count = lax.axis_size("space")
    p, q = lax.axis_index("snap"), lax.axis_index("space")
    pos = jnp.stack([p, q]).astype(jnp.int32)
    chips = range(1, snap_count // 2)

    own = vectors_cyclic.T
    other = swap(own, "snap", 1)
    held_keep, held_send = widen(pos, held_out)
    held = jnp.stack([held_keep, swap(held_send, "snap", 1)])

    pieces = split_pieces(pos, own, other, eigen_values[None, :], snap_count, space_count)
    near = jnp.concatenate([pieces[0]] + [swap(pieces[d], "snap", 2 * d) for d in chips])
    near, held = lax.optimization_barrier((near, held))
    slab = jnp.stack([near] + [swap(near, "space", e) for e in range(1, space_count)])
    held = [held] + [swap(held, "snap", 2 * d) for d in chips]

    mine = multiply(pos, slab, stage(near, snapshots))
    coef, *sums = pair(mine, swap(mine, "snap", 1), held)

    coef = tree_sum([coef] + [swap(coef, "snap", 2 * d) for d in chips])
    coef = tree_sum([coef] + [swap(coef, "space", e) for e in range(1, space_count)])
    far = swap(coef, "snap", 1)
    first = p % 2 == 0
    coefficients = jnp.concatenate([jnp.where(first, coef, far), jnp.where(first, far, coef)], axis=1)

    modes = tree_sum([sums[0]] + [swap(sums[d], "snap", 2 * d) for d in chips])
    total_cells = snapshots.shape[0] * space_count
    return (modes.astype(jnp.bfloat16).T, coefficients / math.sqrt(total_cells))


def solution(mesh):
    return jax.shard_map(
        per_device,
        mesh=mesh,
        in_specs=(P("space", "snap"), P("snap", "space"), P(), P(("space", "snap"), None)),
        out_specs=(P(("space", "snap"), None), P()),
        check_vma=False,
    )
```

time: 70.1 us -> 69.4 us (0.990)
  Pallas kernels: 11.1 us -> 5.22 us
  starting transfers between devices: 22 us -> 26.1 us
  local copies, waits for them, and re-layouts: 4.12 us -> 5.82 us
  other arithmetic: 3.01 us -> 1.49 us
  waiting for transfers between devices: 28.8 us -> 29.8 us
    pallas_call x2 -> x4, Pallas kernels: 9.23 us -> 4.57 us  [the longest x1 3.22 us: multiply(): pl.pallas_call(multiply_kernel, out_shape=jax.ShapeDtypeStruct(out, jnp.f...]
    ppermute x19 -> x22, starting transfers between devices: 22 us -> 26.1 us  [swap(): return lax.ppermute(value, axis, [(i, i ^ mask) for i in range(count)])]
    unnamed x19 -> x8, local copies, waits for them, and re-layouts: 3.49 us -> 5.82 us
    add x2 -> x0, other arithmetic: 1.69 us -> none  [the longest x1 0.93 us: per_device(): paired = keep + swap(send, 'snap', 1)]
    pallas_call x1, Pallas kernels: 1.82 us -> 0.65 us  [split_pieces(): pl.pallas_call(lambda *refs: split_kernel(space_count, *refs), out_shape=...]
    ppermute x19 -> x22, waiting for transfers between devices: 28.8 us -> 29.8 us  [swap(): return lax.ppermute(value, axis, [(i, i ^ mask) for i in range(count)])]
  transfers between devices with their start and end apart: 19 -> 22, of which waited for: 18 -> 10; matrix products, arithmetic and copies ran while one was open for 2% -> 1% of each run, Pallas kernels for 0% -> 3%
where the time goes in v2:
time: 69.4 us; the launch traced here: 69.2 us
  waiting for transfers between devices  29.8 us (43%)
  starting transfers between devices  26.1 us (38%)
  local copies, waits for them, and re-layouts  5.82 us (8%)
  Pallas kernels  5.22 us (8%)
  other arithmetic  1.49 us (2%)
  between operations  0.76 us (1%)
    ppermute x22, waiting for transfers between devices, swap(): return lax.ppermute(value, axis, [(i, i ^ mask) for i in range(count)])  29.8 us
    ppermute x22, starting transfers between devices, swap(): return lax.ppermute(value, axis, [(i, i ^ mask) for i in range(count)])  26.1 us
    unnamed x8, local copies, waits for them, and re-layouts  5.82 us
    pallas_call x1, Pallas kernels, multiply(): pl.pallas_call(multiply_kernel, out_shape=jax.ShapeDtypeStruct(out, jnp.f...  3.22 us
  transfers between devices with their start and end apart: 22, of which 10 were waited for; matrix products, arithmetic and copies ran while one was open for 1% of the time, Pallas kernels for 3%

profile of v2, /device:TPU:0, one launch (start us, length us, event | category | flops | bytes accessed | tf_op | source)
XLA Modules:
  0.0 69.2 jit_solution(4717599239818490569)
XLA Ops:
  1.3 0.8 %copy-done.2 = bf16[128,256]{1,0:T(8,128)(2,1)S(1)} copy-done((bf16[128,256]{1,0:T(8,128)(2,1)S(1)}, bf16[128,256]{1,0:T(8,128)(2,1)}, u32[]{:S(2)}) %copy-start.2) | copy-done | bytes 65560
  2.8 0.9 %copy-done.1 = f32[4096,16]{0,1:T(8,128)S(1)} copy-done((f32[4096,16]{0,1:T(8,128)S(1)}, f32[4096,16]{0,1:T(8,128)}, u32[]{:S(2)}) %copy-start.1) | copy-done | bytes 262168
  3.7 0.7 copy-done.3
  4.4 0.7 split_pieces.1
  5.0 3.1 %collective-permute-start.1 = (f32[2,16,512]{2,1,0:T(8,128)S(1)}, f32[2,16,512]{2,1,0:T(8,128)S(1)}, u32[]{:S(2)}, u32[]{:S(2)}) collective-permute-start(f32[2,16,512]{2,1,0:T(8,128)S(1)} %get-tuple-element.16), channel_id=1, source_target_pairs={{0,2},{1,3},{2,0},{3,1},{4,6},{5,7},{6,4},{7,5},{8,10},{9,11},{10,... | collective-permute-start | bytes 196616 | tf_op jit(solution)/shard_map/ppermute | solution.py:27
  8.1 2.6 %collective-permute-start.2 = (f32[2,16,512]{2,1,0:T(8,128)S(1)}, f32[2,16,512]{2,1,0:T(8,128)S(1)}, u32[]{:S(2)}, u32[]{:S(2)}) collective-permute-start(f32[2,16,512]{2,1,0:T(8,128)S(1)} %get-tuple-element.17), channel_id=1, source_target_pairs={{0,4},{1,5},{2,6},{3,7},{4,0},{5,1},{6,2},{7,3},{8,12},{9,13},{10,... | collective-permute-start | bytes 196616 | tf_op jit(solution)/shard_map/ppermute | solution.py:27
  10.8 4.8 %collective-permute-done.2 = f32[2,16,512]{2,1,0:T(8,128)S(1)} collective-permute-done((f32[2,16,512]{2,1,0:T(8,128)S(1)}, f32[2,16,512]{2,1,0:T(8,128)S(1)}, u32[]{:S(2)}, u32[]{:S(2)}) %collective-permute-start.2) | collective-permute-done | bytes 65568 | tf_op jit(solution)/shard_map/ppermute | solution.py:27
  15.6 1.3 %collective-permute-done.3 = f32[2,16,512]{2,1,0:T(8,128)S(1)} collective-permute-done((f32[2,16,512]{2,1,0:T(8,128)S(1)}, f32[2,16,512]{2,1,0:T(8,128)S(1)}, u32[]{:S(2)}, u32[]{:S(2)}) %collective-permute-start.3) | collective-permute-done | bytes 65568 | tf_op jit(solution)/shard_map/ppermute | solution.py:27
  16.9 1.6 %collective-permute-start.5 = (f32[8,16,512]{2,1,0:T(8,128)S(1)}, f32[8,16,512]{2,1,0:T(8,128)S(1)}, u32[]{:S(2)}, u32[]{:S(2)}) collective-permute-start(f32[8,16,512]{2,1,0:T(8,128)S(1)} %pad_maximum_fusion.1.after_ref), channel_id=1, source_target_pairs={{0,8},{8,0},{16,24},{24,16},{1,9},{9,1},{17,25},{25,17},{2,10},{10... | collective-permute-start | bytes 786440 | tf_op jit(solution)/shard_map/ppermute | solution.py:27
  18.5 1.5 %collective-permute-start.6 = (f32[8,16,512]{2,1,0:T(8,128)S(1)}, f32[8,16,512]{2,1,0:T(8,128)S(1)}, u32[]{:S(2)}, u32[]{:S(2)}) collective-permute-start(f32[8,16,512]{2,1,0:T(8,128)S(1)} %pad_maximum_fusion.1.after_ref), channel_id=1, source_target_pairs={{0,16},{8,24},{16,0},{24,8},{1,17},{9,25},{17,1},{25,9},{2,18},{10... | collective-permute-start | bytes 786440 | tf_op jit(solution)/shard_map/ppermute | solution.py:27
  20.5 3.4 %copy-done = bf16[1024,4096]{1,0:T(8,128)(2,1)S(1)} copy-done((bf16[1024,4096]{1,0:T(8,128)(2,1)S(1)}, bf16[1024,4096]{1,0:T(8,128)(2,1)}, u32[]{:S(2)}) %copy-start) | copy-done | bytes 8388632
  23.8 0.6 stage.1.snap_ref
  24.4 1.7 %collective-permute-done.5 = f32[8,16,512]{2,1,0:T(8,128)S(1)} collective-permute-done((f32[8,16,512]{2,1,0:T(8,128)S(1)}, f32[8,16,512]{2,1,0:T(8,128)S(1)}, u32[]{:S(2)}, u32[]{:S(2)}) %collective-permute-start.5) | collective-permute-done | bytes 262176 | tf_op jit(solution)/shard_map/ppermute | solution.py:27
  26.2 4.2 %collective-permute-done.6 = f32[8,16,512]{2,1,0:T(8,128)S(1)} collective-permute-done((f32[8,16,512]{2,1,0:T(8,128)S(1)}, f32[8,16,512]{2,1,0:T(8,128)S(1)}, u32[]{:S(2)}, u32[]{:S(2)}) %collective-permute-start.6) | collective-permute-done | bytes 262176 | tf_op jit(solution)/shard_map/ppermute | solution.py:27
  30.5 3.2 %multiply.2.mine_ref = f32[8,64,128]{2,1,0:T(8,128)S(1)} custom-call(s32[2]{0:T(128)S(1)} %pad_add_fusion.refs_0_.pos_ref, f32[4,8,16,512]{3,2,1,0:T(8,128)S(1)} %pad_maximum_fusion.slab_ref, bf16[1024,4096]{1,0:T(8,128)(2,1)S(1)} %stage.1.snap_ref), custom_call_target="tpu_custom_call" | custom-call | tf_op jit(solution)/shard_map/multiply/pallas_call | solution.py:164
  33.8 2.1 %collective-permute-start.10 = (f32[2,128,128]{2,1,0:T(8,128)S(1)}, f32[2,128,128]{2,1,0:T(8,128)S(1)}, u32[]{:S(2)}, u32[]{:S(2)}) collective-permute-start(f32[2,128,128]{2,1,0:T(8,128)S(1)} %pad_maximum_fusion.2.refs_0_), channel_id=1, source_target_pairs={{0,4},{1,5},{2,6},{3,7},{4,0},{5,1},{6,2},{7,3},{8,12},{9,13},{10,... | collective-permute-start | bytes 393224 | tf_op jit(solution)/shard_map/ppermute | solution.py:27
  35.9 1.4 %collective-permute-start.11 = (f32[2,128,128]{2,1,0:T(8,128)S(1)}, f32[2,128,128]{2,1,0:T(8,128)S(1)}, u32[]{:S(2)}, u32[]{:S(2)}) collective-permute-start(f32[2,128,128]{2,1,0:T(8,128)S(1)} %pad_maximum_fusion.2.refs_0_), channel_id=1, source_target_pairs={{0,6},{1,7},{2,4},{3,5},{4,2},{5,3},{6,0},{7,1},{8,14},{9,15},{10,... | collective-permute-start | bytes 393224 | tf_op jit(solution)/shard_map/ppermute | solution.py:27
  37.3 9.4 %collective-permute-done.10.refs_2_ = f32[2,128,128]{2,1,0:T(8,128)S(1)} collective-permute-done((f32[2,128,128]{2,1,0:T(8,128)S(1)}, f32[2,128,128]{2,1,0:T(8,128)S(1)}, u32[]{:S(2)}, u32[]{:S(2)}) %collective-permute-start.10) | collective-permute-done | bytes 131104 | tf_op jit(solution)/shard_map/ppermute | solution.py:27
  46.8 0.8 %collective-permute-done.9.refs_1_ = f32[2,128,128]{2,1,0:T(8,128)S(1)} collective-permute-done((f32[2,128,128]{2,1,0:T(8,128)S(1)}, f32[2,128,128]{2,1,0:T(8,128)S(1)}, u32[]{:S(2)}, u32[]{:S(2)}) %collective-permute-start.9) | collective-permute-done | bytes 131104 | tf_op jit(solution)/shard_map/ppermute | solution.py:27
  47.8 2.1 %collective-permute-start.15 = (f32[64,128]{1,0:T(8,128)S(1)}, f32[64,128]{1,0:T(8,128)S(1)}, u32[]{:S(2)}, u32[]{:S(2)}) collective-permute-start(f32[64,128]{1,0:T(8,128)S(1)} %get-tuple-element.27), channel_id=1, source_target_pairs={{0,2},{1,3},{2,0},{3,1},{4,6},{5,7},{6,4},{7,5},{8,10},{9,11},{10,... | collective-permute-start | bytes 98312 | tf_op jit(solution)/shard_map/ppermute | solution.py:27
  49.9 2.4 %collective-permute-start.17 = (f32[64,128]{1,0:T(8,128)S(1)}, f32[64,128]{1,0:T(8,128)S(1)}, u32[]{:S(2)}, u32[]{:S(2)}) collective-permute-start(f32[64,128]{1,0:T(8,128)S(1)} %get-tuple-element.27), channel_id=1, source_target_pairs={{0,6},{1,7},{2,4},{3,5},{4,2},{5,3},{6,0},{7,1},{8,14},{9,15},{10,... | collective-permute-start | bytes 98312 | tf_op jit(solution)/shard_map/ppermute | solution.py:27
  52.3 2.4 %collective-permute-done.16 = f32[64,128]{1,0:T(8,128)S(1)} collective-permute-done((f32[64,128]{1,0:T(8,128)S(1)}, f32[64,128]{1,0:T(8,128)S(1)}, u32[]{:S(2)}, u32[]{:S(2)}) %collective-permute-start.16) | collective-permute-done | bytes 32800 | tf_op jit(solution)/shard_map/ppermute | solution.py:27
  54.7 0.9 %collective-permute-done.17 = f32[64,128]{1,0:T(8,128)S(1)} collective-permute-done((f32[64,128]{1,0:T(8,128)S(1)}, f32[64,128]{1,0:T(8,128)S(1)}, u32[]{:S(2)}, u32[]{:S(2)}) %collective-permute-start.17) | collective-permute-done | bytes 32800 | tf_op jit(solution)/shard_map/ppermute | solution.py:27
  55.6 1.3 %collective-permute-start.18 = (f32[64,128]{1,0:T(8,128)S(1)}, f32[64,128]{1,0:T(8,128)S(1)}, u32[]{:S(2)}, u32[]{:S(2)}) collective-permute-start(f32[64,128]{1,0:T(8,128)S(1)} %add_add_fusion.1), channel_id=1, source_target_pairs={{0,8},{8,0},{16,24},{24,16},{1,9},{9,1},{17,25},{25,17},{2,10},{10... | collective-permute-start | bytes 98312 | tf_op jit(solution)/shard_map/ppermute | solution.py:27
  56.9 0.8 %collective-permute-start.19 = (f32[64,128]{1,0:T(8,128)S(1)}, f32[64,128]{1,0:T(8,128)S(1)}, u32[]{:S(2)}, u32[]{:S(2)}) collective-permute-start(f32[64,128]{1,0:T(8,128)S(1)} %add_add_fusion.1), channel_id=1, source_target_pairs={{0,16},{8,24},{16,0},{24,8},{1,17},{9,25},{17,1},{25,9},{2,18},{10... | collective-permute-start | bytes 98312 | tf_op jit(solution)/shard_map/ppermute | solution.py:27
  57.7 1.4 %collective-permute-start.20 = (f32[64,128]{1,0:T(8,128)S(1)}, f32[64,128]{1,0:T(8,128)S(1)}, u32[]{:S(2)}, u32[]{:S(2)}) collective-permute-start(f32[64,128]{1,0:T(8,128)S(1)} %add_add_fusion.1), channel_id=1, source_target_pairs={{0,24},{8,16},{16,8},{24,0},{1,25},{9,17},{17,9},{25,1},{2,26},{10... | collective-permute-start | bytes 98312 | tf_op jit(solution)/shard_map/ppermute | solution.py:27
  59.2 3.0 %collective-permute-start.13 = (f32[64,128]{1,0:T(8,128)S(1)}, f32[64,128]{1,0:T(8,128)S(1)}, u32[]{:S(2)}, u32[]{:S(2)}) collective-permute-start(f32[64,128]{1,0:T(8,128)S(1)} %get-tuple-element.25), channel_id=1, source_target_pairs={{0,4},{1,5},{2,6},{3,7},{4,0},{5,1},{6,2},{7,3},{8,12},{9,13},{10,... | collective-permute-start | bytes 98312 | tf_op jit(solution)/shard_map/ppermute | solution.py:27
  62.2 1.4 %collective-permute-start.14 = (f32[64,128]{1,0:T(8,128)S(1)}, f32[64,128]{1,0:T(8,128)S(1)}, u32[]{:S(2)}, u32[]{:S(2)}) collective-permute-start(f32[64,128]{1,0:T(8,128)S(1)} %get-tuple-element.26), channel_id=1, source_target_pairs={{0,6},{1,7},{2,4},{3,5},{4,2},{5,3},{6,0},{7,1},{8,14},{9,15},{10,... | collective-permute-start | bytes 98312 | tf_op jit(solution)/shard_map/ppermute | solution.py:27
  63.7 0.6 collective-permute-done.13
  64.2 3.7 %collective-permute-done.14 = f32[64,128]{1,0:T(8,128)S(1)} collective-permute-done((f32[64,128]{1,0:T(8,128)S(1)}, f32[64,128]{1,0:T(8,128)S(1)}, u32[]{:S(2)}, u32[]{:S(2)}) %collective-permute-start.14) | collective-permute-done | bytes 32800 | tf_op jit(solution)/shard_map/ppermute | solution.py:27
  67.9 0.6 fusion
  68.5 0.6 maximum_multiply_fusion
  (34 shorter events, 2.3 us)
Async XLA Ops:
  0.6 2.1 %collective-permute-start = (f32[16,4096]{1,0:T(8,128)}, f32[16,4096]{1,0:T(8,128)S(1)}, u32[]{:S(2)}, u32[]{:S(2)}) collective-permute-start(f32[16,4096]{1,0:T(8,128)} %bitcast.13), channel_id=1, source_target_pairs={{0,1},{1,0},{2,3},{3,2},{4,5},{5,4},{6,7},{7,6},{8,9},{9,8},{10,11... | collective-permute-start | bytes 786440 | tf_op jit(solution)/shard_map/ppermute | solution.py:27
  1.3 0.8 %copy-start.2 = (bf16[128,256]{1,0:T(8,128)(2,1)S(1)}, bf16[128,256]{1,0:T(8,128)(2,1)}, u32[]{:S(2)}) copy-start(bf16[128,256]{1,0:T(8,128)(2,1)} %held_ref.1) | copy-start | bytes 196612
  2.7 8.1 %collective-permute-start.4 = (f32[128,128]{1,0:T(8,128)S(1)}, f32[128,128]{1,0:T(8,128)S(1)}, u32[]{:S(2)}, u32[]{:S(2)}) collective-permute-start(f32[128,128]{1,0:T(8,128)S(1)} %get-tuple-element.20), channel_id=1, source_target_pairs={{0,1},{1,0},{2,3},{3,2},{4,5},{5,4},{6,7},{7,6},{8,9},{9,8},{10,11... | collective-permute-start | bytes 196616 | tf_op jit(solution)/shard_map/ppermute | solution.py:27
  2.8 1.0 %copy-start.1 = (f32[4096,16]{0,1:T(8,128)S(1)}, f32[4096,16]{0,1:T(8,128)}, u32[]{:S(2)}) copy-start(f32[4096,16]{0,1:T(8,128)} %param.5) | copy-start | bytes 786436
  3.7 0.7 copy-start.3
  5.0 5.7 %collective-permute-start.1 = (f32[2,16,512]{2,1,0:T(8,128)S(1)}, f32[2,16,512]{2,1,0:T(8,128)S(1)}, u32[]{:S(2)}, u32[]{:S(2)}) collective-permute-start(f32[2,16,512]{2,1,0:T(8,128)S(1)} %get-tuple-element.16), channel_id=1, source_target_pairs={{0,2},{1,3},{2,0},{3,1},{4,6},{5,7},{6,4},{7,5},{8,10},{9,11},{10,... | collective-permute-start | bytes 196616 | tf_op jit(solution)/shard_map/ppermute | solution.py:27
  8.1 7.5 %collective-permute-start.2 = (f32[2,16,512]{2,1,0:T(8,128)S(1)}, f32[2,16,512]{2,1,0:T(8,128)S(1)}, u32[]{:S(2)}, u32[]{:S(2)}) collective-permute-start(f32[2,16,512]{2,1,0:T(8,128)S(1)} %get-tuple-element.17), channel_id=1, source_target_pairs={{0,4},{1,5},{2,6},{3,7},{4,0},{5,1},{6,2},{7,3},{8,12},{9,13},{10,... | collective-permute-start | bytes 196616 | tf_op jit(solution)/shard_map/ppermute | solution.py:27
  10.7 6.2 %collective-permute-start.3 = (f32[2,16,512]{2,1,0:T(8,128)S(1)}, f32[2,16,512]{2,1,0:T(8,128)S(1)}, u32[]{:S(2)}, u32[]{:S(2)}) collective-permute-start(f32[2,16,512]{2,1,0:T(8,128)S(1)} %get-tuple-element.18), channel_id=1, source_target_pairs={{0,6},{1,7},{2,4},{3,5},{4,2},{5,3},{6,0},{7,1},{8,14},{9,15},{10,... | collective-permute-start | bytes 196616 | tf_op jit(solution)/shard_map/ppermute | solution.py:27
  16.9 9.2 %collective-permute-start.5 = (f32[8,16,512]{2,1,0:T(8,128)S(1)}, f32[8,16,512]{2,1,0:T(8,128)S(1)}, u32[]{:S(2)}, u32[]{:S(2)}) collective-permute-start(f32[8,16,512]{2,1,0:T(8,128)S(1)} %pad_maximum_fusion.1.after_ref), channel_id=1, source_target_pairs={{0,8},{8,0},{16,24},{24,16},{1,9},{9,1},{17,25},{25,17},{2,10},{10... | collective-permute-start | bytes 786440 | tf_op jit(solution)/shard_map/ppermute | solution.py:27
  18.5 11.9 %collective-permute-start.6 = (f32[8,16,512]{2,1,0:T(8,128)S(1)}, f32[8,16,512]{2,1,0:T(8,128)S(1)}, u32[]{:S(2)}, u32[]{:S(2)}) collective-permute-start(f32[8,16,512]{2,1,0:T(8,128)S(1)} %pad_maximum_fusion.1.after_ref), channel_id=1, source_target_pairs={{0,16},{8,24},{16,0},{24,8},{1,17},{9,25},{17,1},{25,9},{2,18},{10... | collective-permute-start | bytes 786440 | tf_op jit(solution)/shard_map/ppermute | solution.py:27
  20.0 10.4 %collective-permute-start.7 = (f32[8,16,512]{2,1,0:T(8,128)S(1)}, f32[8,16,512]{2,1,0:T(8,128)S(1)}, u32[]{:S(2)}, u32[]{:S(2)}) collective-permute-start(f32[8,16,512]{2,1,0:T(8,128)S(1)} %pad_maximum_fusion.1.after_ref), channel_id=1, source_target_pairs={{0,24},{8,16},{16,8},{24,0},{1,25},{9,17},{17,9},{25,1},{2,26},{10... | collective-permute-start | bytes 786440 | tf_op jit(solution)/shard_map/ppermute | solution.py:27
  20.5 3.4 %copy-start = (bf16[1024,4096]{1,0:T(8,128)(2,1)S(1)}, bf16[1024,4096]{1,0:T(8,128)(2,1)}, u32[]{:S(2)}) copy-start(bf16[1024,4096]{1,0:T(8,128)(2,1)} %source_ref.1) | copy-start | bytes 25165828
  33.7 13.9 %collective-permute-start.8 = (f32[8,64,128]{2,1,0:T(8,128)S(1)}, f32[8,64,128]{2,1,0:T(8,128)S(1)}, u32[]{:S(2)}, u32[]{:S(2)}) collective-permute-start(f32[8,64,128]{2,1,0:T(8,128)S(1)} %multiply.2.mine_ref), channel_id=1, source_target_pairs={{0,1},{1,0},{2,3},{3,2},{4,5},{5,4},{6,7},{7,6},{8,9},{9,8},{10,11... | collective-permute-start | bytes 786440 | tf_op jit(solution)/shard_map/ppermute | solution.py:27
  33.8 13.0 %collective-permute-start.10 = (f32[2,128,128]{2,1,0:T(8,128)S(1)}, f32[2,128,128]{2,1,0:T(8,128)S(1)}, u32[]{:S(2)}, u32[]{:S(2)}) collective-permute-start(f32[2,128,128]{2,1,0:T(8,128)S(1)} %pad_maximum_fusion.2.refs_0_), channel_id=1, source_target_pairs={{0,4},{1,5},{2,6},{3,7},{4,0},{5,1},{6,2},{7,3},{8,12},{9,13},{10,... | collective-permute-start | bytes 393224 | tf_op jit(solution)/shard_map/ppermute | solution.py:27
  35.9 10.9 %collective-permute-start.11 = (f32[2,128,128]{2,1,0:T(8,128)S(1)}, f32[2,128,128]{2,1,0:T(8,128)S(1)}, u32[]{:S(2)}, u32[]{:S(2)}) collective-permute-start(f32[2,128,128]{2,1,0:T(8,128)S(1)} %pad_maximum_fusion.2.refs_0_), channel_id=1, source_target_pairs={{0,6},{1,7},{2,4},{3,5},{4,2},{5,3},{6,0},{7,1},{8,14},{9,15},{10,... | collective-permute-start | bytes 393224 | tf_op jit(solution)/shard_map/ppermute | solution.py:27
  37.3 10.2 %collective-permute-start.9 = (f32[2,128,128]{2,1,0:T(8,128)S(1)}, f32[2,128,128]{2,1,0:T(8,128)S(1)}, u32[]{:S(2)}, u32[]{:S(2)}) collective-permute-start(f32[2,128,128]{2,1,0:T(8,128)S(1)} %pad_maximum_fusion.2.refs_0_), channel_id=1, source_target_pairs={{0,2},{1,3},{2,0},{3,1},{4,6},{5,7},{6,4},{7,5},{8,10},{9,11},{10,... | collective-permute-start | bytes 393224 | tf_op jit(solution)/shard_map/ppermute | solution.py:27
  47.8 4.6 %collective-permute-start.15 = (f32[64,128]{1,0:T(8,128)S(1)}, f32[64,128]{1,0:T(8,128)S(1)}, u32[]{:S(2)}, u32[]{:S(2)}) collective-permute-start(f32[64,128]{1,0:T(8,128)S(1)} %get-tuple-element.27), channel_id=1, source_target_pairs={{0,2},{1,3},{2,0},{3,1},{4,6},{5,7},{6,4},{7,5},{8,10},{9,11},{10,... | collective-permute-start | bytes 98312 | tf_op jit(solution)/shard_map/ppermute | solution.py:27
  49.9 4.8 %collective-permute-start.16 = (f32[64,128]{1,0:T(8,128)S(1)}, f32[64,128]{1,0:T(8,128)S(1)}, u32[]{:S(2)}, u32[]{:S(2)}) collective-permute-start(f32[64,128]{1,0:T(8,128)S(1)} %get-tuple-element.27), channel_id=1, source_target_pairs={{0,4},{1,5},{2,6},{3,7},{4,0},{5,1},{6,2},{7,3},{8,12},{9,13},{10,... | collective-permute-start | bytes 98312 | tf_op jit(solution)/shard_map/ppermute | solution.py:27
  49.9 5.7 %collective-permute-start.17 = (f32[64,128]{1,0:T(8,128)S(1)}, f32[64,128]{1,0:T(8,128)S(1)}, u32[]{:S(2)}, u32[]{:S(2)}) collective-permute-start(f32[64,128]{1,0:T(8,128)S(1)} %get-tuple-element.27), channel_id=1, source_target_pairs={{0,6},{1,7},{2,4},{3,5},{4,2},{5,3},{6,0},{7,1},{8,14},{9,15},{10,... | collective-permute-start | bytes 98312 | tf_op jit(solution)/shard_map/ppermute | solution.py:27
  55.6 6.6 %collective-permute-start.18 = (f32[64,128]{1,0:T(8,128)S(1)}, f32[64,128]{1,0:T(8,128)S(1)}, u32[]{:S(2)}, u32[]{:S(2)}) collective-permute-start(f32[64,128]{1,0:T(8,128)S(1)} %add_add_fusion.1), channel_id=1, source_target_pairs={{0,8},{8,0},{16,24},{24,16},{1,9},{9,1},{17,25},{25,17},{2,10},{10... | collective-permute-start | bytes 98312 | tf_op jit(solution)/shard_map/ppermute | solution.py:27
  56.9 6.7 %collective-permute-start.19 = (f32[64,128]{1,0:T(8,128)S(1)}, f32[64,128]{1,0:T(8,128)S(1)}, u32[]{:S(2)}, u32[]{:S(2)}) collective-permute-start(f32[64,128]{1,0:T(8,128)S(1)} %add_add_fusion.1), channel_id=1, source_target_pairs={{0,16},{8,24},{16,0},{24,8},{1,17},{9,25},{17,1},{25,9},{2,18},{10... | collective-permute-start | bytes 98312 | tf_op jit(solution)/shard_map/ppermute | solution.py:27
  57.7 5.8 %collective-permute-start.20 = (f32[64,128]{1,0:T(8,128)S(1)}, f32[64,128]{1,0:T(8,128)S(1)}, u32[]{:S(2)}, u32[]{:S(2)}) collective-permute-start(f32[64,128]{1,0:T(8,128)S(1)} %add_add_fusion.1), channel_id=1, source_target_pairs={{0,24},{8,16},{16,8},{24,0},{1,25},{9,17},{17,9},{25,1},{2,26},{10... | collective-permute-start | bytes 98312 | tf_op jit(solution)/shard_map/ppermute | solution.py:27
  59.2 4.5 %collective-permute-start.12 = (f32[64,128]{1,0:T(8,128)S(1)}, f32[64,128]{1,0:T(8,128)S(1)}, u32[]{:S(2)}, u32[]{:S(2)}) collective-permute-start(f32[64,128]{1,0:T(8,128)S(1)} %get-tuple-element.24), channel_id=1, source_target_pairs={{0,2},{1,3},{2,0},{3,1},{4,6},{5,7},{6,4},{7,5},{8,10},{9,11},{10,... | collective-permute-start | bytes 98312 | tf_op jit(solution)/shard_map/ppermute | solution.py:27
  59.2 5.0 %collective-permute-start.13 = (f32[64,128]{1,0:T(8,128)S(1)}, f32[64,128]{1,0:T(8,128)S(1)}, u32[]{:S(2)}, u32[]{:S(2)}) collective-permute-start(f32[64,128]{1,0:T(8,128)S(1)} %get-tuple-element.25), channel_id=1, source_target_pairs={{0,4},{1,5},{2,6},{3,7},{4,0},{5,1},{6,2},{7,3},{8,12},{9,13},{10,... | collective-permute-start | bytes 98312 | tf_op jit(solution)/shard_map/ppermute | solution.py:27
  62.2 5.7 %collective-permute-start.14 = (f32[64,128]{1,0:T(8,128)S(1)}, f32[64,128]{1,0:T(8,128)S(1)}, u32[]{:S(2)}, u32[]{:S(2)}) collective-permute-start(f32[64,128]{1,0:T(8,128)S(1)} %get-tuple-element.26), channel_id=1, source_target_pairs={{0,6},{1,7},{2,4},{3,5},{4,2},{5,3},{6,0},{7,1},{8,14},{9,15},{10,... | collective-permute-start | bytes 98312 | tf_op jit(solution)/shard_map/ppermute | solution.py:27
  63.6 4.9 %collective-permute-start.21 = (f32[64,128]{1,0:T(8,128)S(1)}, f32[64,128]{1,0:T(8,128)S(1)}, u32[]{:S(2)}, u32[]{:S(2)}) collective-permute-start(f32[64,128]{1,0:T(8,128)S(1)} %add_add_fusion), channel_id=1, source_target_pairs={{0,1},{1,0},{2,3},{3,2},{4,5},{5,4},{6,7},{7,6},{8,9},{9,8},{10,11... | collective-permute-start | bytes 98312 | tf_op jit(solution)/shard_map/ppermute | solution.py:27

commit v3 on v2

--- a/solution.py
+++ b/solution.py
@@ -6,6 +6,7 @@
 from jax.experimental import pallas as pl
 from jax.experimental.pallas import tpu as pltpu
 from jax.sharding import PartitionSpec as P
+
 
 ROW_BLOCK = 16
 COL_BLOCK = 4
@@ -33,53 +34,62 @@
     return terms[0]
 
 
-def widen_kernel(pos_ref, held_ref, keep_ref, send_ref):
+def prepare_kernel(space_count, pos_ref, own_ref, eig_ref, held_ref, scale_ref, keep_ref, send_ref, *own_refs):
+    p, q = pos_ref[0], pos_ref[1]
     half = keep_ref.shape[1]
-    core = pos_ref[0] & 1
+    core = p & 1
     keep_ref[...] = held_ref[:, pl.ds(pl.multiple_of(core * half, LANES), half)].astype(jnp.float32)
     send_ref[...] = held_ref[:, pl.ds(pl.multiple_of((1 - core) * half, LANES), half)].astype(jnp.float32)
-
-
-def widen(pos, held):
-    rows, columns = held.shape
-    half = jax.ShapeDtypeStruct((rows, columns // 2), jnp.float32)
-    return pl.pallas_call(
-        widen_kernel,
-        out_shape=[half, half],
-        in_specs=[IN_SMEM, IN_VMEM],
-        out_specs=[IN_VMEM, IN_VMEM],
-        compiler_params=params(2),
-        name="widen",
-    )(pos, held)
-
-
-def split_kernel(space_count, pos_ref, own_ref, other_ref, eig_ref, *out_refs):
-    p, q = pos_ref[0], pos_ref[1]
     width = own_ref.shape[0]
-    chunk = out_refs[0].shape[2]
     row = lax.broadcasted_iota(jnp.int32, (width, eig_ref.shape[1]), 0)
     mode = lax.broadcasted_iota(jnp.int32, (width, eig_ref.shape[1]), 1)
     mine = (row // COL_BLOCK * space_count + q) * COL_BLOCK + row % COL_BLOCK
     picked = jnp.where(mode == mine, eig_ref[...], 0.0)
     scale = lax.rsqrt(jnp.sum(picked, axis=1, keepdims=True))
-    for d, out_ref in enumerate(out_refs):
+    scale_ref[...] = jnp.broadcast_to(scale, scale_ref.shape)
+    for d, out_ref in enumerate(own_refs):
+        chunk = out_ref.shape[1]
         start = pl.multiple_of((p ^ (2 * d)) * chunk, LANES)
-        out_ref[0] = own_ref[:, pl.ds(start, chunk)] * scale
+        out_ref[...] = own_ref[:, pl.ds(start, chunk)] * scale
+
+
+def prepare(pos, own, eig, held, snap_count, space_count):
+    width, rows = own.shape
+    half = jax.ShapeDtypeStruct((held.shape[0], held.shape[1] // 2), jnp.float32)
+    scale = jax.ShapeDtypeStruct((width, LANES), jnp.float32)
+    piece = jax.ShapeDtypeStruct((width, rows // snap_count), jnp.float32)
+    shapes = [scale, half, half] + [piece] * (snap_count // 2)
+    return pl.pallas_call(
+        lambda *refs: prepare_kernel(space_count, *refs),
+        out_shape=shapes,
+        in_specs=[IN_SMEM, IN_VMEM, IN_VMEM, IN_VMEM],
+        out_specs=[IN_VMEM] * len(shapes),
+        compiler_params=params(4),
+        name="prepare",
+    )(pos, own, eig, held)
+
+
+def join_kernel(pos_ref, scale_ref, other_ref, *refs):
+    p = pos_ref[0]
+    own_refs, out_refs = refs[: len(refs) // 2], refs[len(refs) // 2 :]
+    scale = scale_ref[:, :1]
+    for d, (own_ref, out_ref) in enumerate(zip(own_refs, out_refs)):
+        chunk = own_ref.shape[1]
+        start = pl.multiple_of((p ^ (2 * d)) * chunk, LANES)
+        out_ref[0] = own_ref[...]
         out_ref[1] = other_ref[:, pl.ds(start, chunk)] * scale
 
 
-def split_pieces(pos, own, other, eig, snap_count, space_count):
-    width, rows = own.shape
-    chunk = rows // snap_count
-    piece = jax.ShapeDtypeStruct((2, width, chunk), jnp.float32)
-    return pl.pallas_call(
-        lambda *refs: split_kernel(space_count, *refs),
-        out_shape=[piece] * (snap_count // 2),
-        in_specs=[IN_SMEM, IN_VMEM, IN_VMEM, IN_VMEM],
-        out_specs=[IN_VMEM] * (snap_count // 2),
+def join(pos, scale, other, own_pieces):
+    piece = jax.ShapeDtypeStruct((2, *own_pieces[0].shape), jnp.float32)
+    return pl.pallas_call(
+        join_kernel,
+        out_shape=[piece] * len(own_pieces),
+        in_specs=[IN_SMEM] + [IN_VMEM] * (2 + len(own_pieces)),
+        out_specs=[IN_VMEM] * len(own_pieces),
         compiler_params=params(4),
-        name="split_pieces",
-    )(pos, own, other, eig)
+        name="join",
+    )(pos, scale, other, *own_pieces)
 
 
 def stage_kernel(after_ref, source_ref, target_ref, sem):
@@ -209,23 +219,25 @@
     p, q = lax.axis_index("snap"), lax.axis_index("space")
     pos = jnp.stack([p, q]).astype(jnp.int32)
     chips = range(1, snap_count // 2)
+    others = range(1, space_count)
 
     own = vectors_cyclic.T
     other = swap(own, "snap", 1)
-    held_keep, held_send = widen(pos, held_out)
+    scale, held_keep, held_send, *pieces = prepare(
+        pos, own, eigen_values[None, :], held_out, snap_count, space_count
+    )
     held = jnp.stack([held_keep, swap(held_send, "snap", 1)])
-
-    pieces = split_pieces(pos, own, other, eigen_values[None, :], snap_count, space_count)
+    pieces = join(pos, scale, other, pieces)
     near = jnp.concatenate([pieces[0]] + [swap(pieces[d], "snap", 2 * d) for d in chips])
     near, held = lax.optimization_barrier((near, held))
-    slab = jnp.stack([near] + [swap(near, "space", e) for e in range(1, space_count)])
+    slab = jnp.stack([near] + [swap(near, "space", e) for e in others])
     held = [held] + [swap(held, "snap", 2 * d) for d in chips]
 
     mine = multiply(pos, slab, stage(near, snapshots))
     coef, *sums = pair(mine, swap(mine, "snap", 1), held)
 
     coef = tree_sum([coef] + [swap(coef, "snap", 2 * d) for d in chips])
-    coef = tree_sum([coef] + [swap(coef, "space", e) for e in range(1, space_count)])
+    coef = tree_sum([coef] + [swap(coef, "space", e) for e in others])
     far = swap(coef, "snap", 1)
     first = p % 2 == 0
     coefficients = jnp.concatenate([jnp.where(first, coef, far), jnp.where(first, far, coef)], axis=1)

time: 69.4 us -> 68.5 us (0.987)
  waiting for transfers between devices: 29.8 us -> 28.3 us
    ppermute x22, waiting for transfers between devices: 29.8 us -> 28.3 us  [swap(): return lax.ppermute(value, axis, [(i, i ^ mask) for i in range(count)])]
  transfers between devices with their start and end apart: 22 -> 22, of which waited for: 10 -> 13; matrix products, arithmetic and copies ran while one was open for 1% -> 1% of each run, Pallas kernels for 3% -> 3%
where the time goes in v3:
time: 68.5 us; the launch traced here: 68.2 us
  waiting for transfers between devices  28.3 us (41%)
  starting transfers between devices  26.6 us (39%)
  local copies, waits for them, and re-layouts  5.82 us (8%)
  Pallas kernels  5.27 us (8%)
  other arithmetic  1.49 us (2%)
  between operations  0.73 us (1%)
    ppermute x22, waiting for transfers between devices, swap(): return lax.ppermute(value, axis, [(i, i ^ mask) for i in range(count)])  28.3 us
    ppermute x22, starting transfers between devices, swap(): return lax.ppermute(value, axis, [(i, i ^ mask) for i in range(count)])  26.6 us
    unnamed x8, local copies, waits for them, and re-layouts  5.82 us
    pallas_call x1, Pallas kernels, multiply(): pl.pallas_call(multiply_kernel, out_shape=jax.ShapeDtypeStruct(out, jnp.f...  3.22 us
  transfers between devices with their start and end apart: 22, of which 13 were waited for; matrix products, arithmetic and copies ran while one was open for 1% of the time, Pallas kernels for 3%

profile of v3, /device:TPU:0, one launch (start us, length us, event | category | flops | bytes accessed | tf_op | source)
XLA Modules:
  0.0 68.2 jit_solution(8523645823600042267)
XLA Ops:
  0.6 0.6 collective-permute-start
  1.3 0.9 %copy-done.1 = f32[4096,16]{0,1:T(8,128)S(1)} copy-done((f32[4096,16]{0,1:T(8,128)S(1)}, f32[4096,16]{0,1:T(8,128)}, u32[]{:S(2)}) %copy-start.1) | copy-done | bytes 262168
  2.2 0.8 %copy-done.2 = bf16[128,256]{1,0:T(8,128)(2,1)S(1)} copy-done((bf16[128,256]{1,0:T(8,128)(2,1)S(1)}, bf16[128,256]{1,0:T(8,128)(2,1)}, u32[]{:S(2)}) %copy-start.2) | copy-done | bytes 65560
  3.1 0.7 copy-done.3
  3.7 0.6 prepare.1
  4.4 0.6 join.1
  5.1 5.1 %collective-permute-start.3 = (f32[2,16,512]{2,1,0:T(8,128)S(1)}, f32[2,16,512]{2,1,0:T(8,128)S(1)}, u32[]{:S(2)}, u32[]{:S(2)}) collective-permute-start(f32[2,16,512]{2,1,0:T(8,128)S(1)} %get-tuple-element.28), channel_id=1, source_target_pairs={{0,6},{1,7},{2,4},{3,5},{4,2},{5,3},{6,0},{7,1},{8,14},{9,15},{10,... | collective-permute-start | bytes 196616 | tf_op jit(solution)/shard_map/ppermute | solution.py:28
  10.2 0.6 collective-permute-start.1
  10.9 1.9 %collective-permute-done.3 = f32[2,16,512]{2,1,0:T(8,128)S(1)} collective-permute-done((f32[2,16,512]{2,1,0:T(8,128)S(1)}, f32[2,16,512]{2,1,0:T(8,128)S(1)}, u32[]{:S(2)}, u32[]{:S(2)}) %collective-permute-start.3) | collective-permute-done | bytes 65568 | tf_op jit(solution)/shard_map/ppermute | solution.py:28
  12.7 3.3 %collective-permute-done.2 = f32[2,16,512]{2,1,0:T(8,128)S(1)} collective-permute-done((f32[2,16,512]{2,1,0:T(8,128)S(1)}, f32[2,16,512]{2,1,0:T(8,128)S(1)}, u32[]{:S(2)}, u32[]{:S(2)}) %collective-permute-start.2) | collective-permute-done | bytes 65568 | tf_op jit(solution)/shard_map/ppermute | solution.py:28
  16.0 2.5 %collective-permute-start.7 = (f32[8,16,512]{2,1,0:T(8,128)S(1)}, f32[8,16,512]{2,1,0:T(8,128)S(1)}, u32[]{:S(2)}, u32[]{:S(2)}) collective-permute-start(f32[8,16,512]{2,1,0:T(8,128)S(1)} %pad_maximum_fusion.1.after_ref), channel_id=1, source_target_pairs={{0,24},{8,16},{16,8},{24,0},{1,25},{9,17},{17,9},{25,1},{2,26},{10... | collective-permute-start | bytes 786440 | tf_op jit(solution)/shard_map/ppermute | solution.py:28
  19.6 3.4 %copy-done = bf16[1024,4096]{1,0:T(8,128)(2,1)S(1)} copy-done((bf16[1024,4096]{1,0:T(8,128)(2,1)S(1)}, bf16[1024,4096]{1,0:T(8,128)(2,1)}, u32[]{:S(2)}) %copy-start) | copy-done | bytes 8388632
  23.0 0.6 stage.1.snap_ref
  23.5 2.7 %collective-permute-done.7 = f32[8,16,512]{2,1,0:T(8,128)S(1)} collective-permute-done((f32[8,16,512]{2,1,0:T(8,128)S(1)}, f32[8,16,512]{2,1,0:T(8,128)S(1)}, u32[]{:S(2)}, u32[]{:S(2)}) %collective-permute-start.7) | collective-permute-done | bytes 262176 | tf_op jit(solution)/shard_map/ppermute | solution.py:28
  26.2 4.3 %collective-permute-done.6 = f32[8,16,512]{2,1,0:T(8,128)S(1)} collective-permute-done((f32[8,16,512]{2,1,0:T(8,128)S(1)}, f32[8,16,512]{2,1,0:T(8,128)S(1)}, u32[]{:S(2)}, u32[]{:S(2)}) %collective-permute-start.6) | collective-permute-done | bytes 262176 | tf_op jit(solution)/shard_map/ppermute | solution.py:28
  30.7 3.2 %multiply.2.mine_ref = f32[8,64,128]{2,1,0:T(8,128)S(1)} custom-call(s32[2]{0:T(128)S(1)} %pad_add_fusion.refs_0_.pos_ref, f32[4,8,16,512]{3,2,1,0:T(8,128)S(1)} %pad_maximum_fusion.slab_ref, bf16[1024,4096]{1,0:T(8,128)(2,1)S(1)} %stage.1.snap_ref), custom_call_target="tpu_custom_call" | custom-call | tf_op jit(solution)/shard_map/multiply/pallas_call | solution.py:174
  34.4 2.3 %collective-permute-start.10 = (f32[2,128,128]{2,1,0:T(8,128)S(1)}, f32[2,128,128]{2,1,0:T(8,128)S(1)}, u32[]{:S(2)}, u32[]{:S(2)}) collective-permute-start(f32[2,128,128]{2,1,0:T(8,128)S(1)} %pad_maximum_fusion.2.refs_0_), channel_id=1, source_target_pairs={{0,4},{1,5},{2,6},{3,7},{4,0},{5,1},{6,2},{7,3},{8,12},{9,13},{10,... | collective-permute-start | bytes 393224 | tf_op jit(solution)/shard_map/ppermute | solution.py:28
  36.7 1.8 %collective-permute-start.11 = (f32[2,128,128]{2,1,0:T(8,128)S(1)}, f32[2,128,128]{2,1,0:T(8,128)S(1)}, u32[]{:S(2)}, u32[]{:S(2)}) collective-permute-start(f32[2,128,128]{2,1,0:T(8,128)S(1)} %pad_maximum_fusion.2.refs_0_), channel_id=1, source_target_pairs={{0,6},{1,7},{2,4},{3,5},{4,2},{5,3},{6,0},{7,1},{8,14},{9,15},{10,... | collective-permute-start | bytes 393224 | tf_op jit(solution)/shard_map/ppermute | solution.py:28
  38.5 3.6 %collective-permute-done.9.refs_1_ = f32[2,128,128]{2,1,0:T(8,128)S(1)} collective-permute-done((f32[2,128,128]{2,1,0:T(8,128)S(1)}, f32[2,128,128]{2,1,0:T(8,128)S(1)}, u32[]{:S(2)}, u32[]{:S(2)}) %collective-permute-start.9) | collective-permute-done | bytes 131104 | tf_op jit(solution)/shard_map/ppermute | solution.py:28
  42.0 5.3 %collective-permute-done.10.refs_2_ = f32[2,128,128]{2,1,0:T(8,128)S(1)} collective-permute-done((f32[2,128,128]{2,1,0:T(8,128)S(1)}, f32[2,128,128]{2,1,0:T(8,128)S(1)}, u32[]{:S(2)}, u32[]{:S(2)}) %collective-permute-start.10) | collective-permute-done | bytes 131104 | tf_op jit(solution)/shard_map/ppermute | solution.py:28
  47.5 3.2 %collective-permute-start.16 = (f32[64,128]{1,0:T(8,128)S(1)}, f32[64,128]{1,0:T(8,128)S(1)}, u32[]{:S(2)}, u32[]{:S(2)}) collective-permute-start(f32[64,128]{1,0:T(8,128)S(1)} %get-tuple-element.37), channel_id=1, source_target_pairs={{0,4},{1,5},{2,6},{3,7},{4,0},{5,1},{6,2},{7,3},{8,12},{9,13},{10,... | collective-permute-start | bytes 98312 | tf_op jit(solution)/shard_map/ppermute | solution.py:28
  50.7 1.8 %collective-permute-start.17 = (f32[64,128]{1,0:T(8,128)S(1)}, f32[64,128]{1,0:T(8,128)S(1)}, u32[]{:S(2)}, u32[]{:S(2)}) collective-permute-start(f32[64,128]{1,0:T(8,128)S(1)} %get-tuple-element.37), channel_id=1, source_target_pairs={{0,6},{1,7},{2,4},{3,5},{4,2},{5,3},{6,0},{7,1},{8,14},{9,15},{10,... | collective-permute-start | bytes 98312 | tf_op jit(solution)/shard_map/ppermute | solution.py:28
  53.0 3.6 %collective-permute-done.17 = f32[64,128]{1,0:T(8,128)S(1)} collective-permute-done((f32[64,128]{1,0:T(8,128)S(1)}, f32[64,128]{1,0:T(8,128)S(1)}, u32[]{:S(2)}, u32[]{:S(2)}) %collective-permute-start.17) | collective-permute-done | bytes 32800 | tf_op jit(solution)/shard_map/ppermute | solution.py:28
  56.8 1.5 %collective-permute-start.19 = (f32[64,128]{1,0:T(8,128)S(1)}, f32[64,128]{1,0:T(8,128)S(1)}, u32[]{:S(2)}, u32[]{:S(2)}) collective-permute-start(f32[64,128]{1,0:T(8,128)S(1)} %add_add_fusion.1), channel_id=1, source_target_pairs={{0,16},{8,24},{16,0},{24,8},{1,17},{9,25},{17,1},{25,9},{2,18},{10... | collective-permute-start | bytes 98312 | tf_op jit(solution)/shard_map/ppermute | solution.py:28
  58.3 1.5 %collective-permute-start.20 = (f32[64,128]{1,0:T(8,128)S(1)}, f32[64,128]{1,0:T(8,128)S(1)}, u32[]{:S(2)}, u32[]{:S(2)}) collective-permute-start(f32[64,128]{1,0:T(8,128)S(1)} %add_add_fusion.1), channel_id=1, source_target_pairs={{0,24},{8,16},{16,8},{24,0},{1,25},{9,17},{17,9},{25,1},{2,26},{10... | collective-permute-start | bytes 98312 | tf_op jit(solution)/shard_map/ppermute | solution.py:28
  60.3 0.6 collective-permute-start.13
  60.9 1.8 %collective-permute-start.14 = (f32[64,128]{1,0:T(8,128)S(1)}, f32[64,128]{1,0:T(8,128)S(1)}, u32[]{:S(2)}, u32[]{:S(2)}) collective-permute-start(f32[64,128]{1,0:T(8,128)S(1)} %get-tuple-element.36), channel_id=1, source_target_pairs={{0,6},{1,7},{2,4},{3,5},{4,2},{5,3},{6,0},{7,1},{8,14},{9,15},{10,... | collective-permute-start | bytes 98312 | tf_op jit(solution)/shard_map/ppermute | solution.py:28
  62.7 1.1 %collective-permute-start.12 = (f32[64,128]{1,0:T(8,128)S(1)}, f32[64,128]{1,0:T(8,128)S(1)}, u32[]{:S(2)}, u32[]{:S(2)}) collective-permute-start(f32[64,128]{1,0:T(8,128)S(1)} %get-tuple-element.34), channel_id=1, source_target_pairs={{0,2},{1,3},{2,0},{3,1},{4,6},{5,7},{6,4},{7,5},{8,10},{9,11},{10,... | collective-permute-start | bytes 98312 | tf_op jit(solution)/shard_map/ppermute | solution.py:28
  63.9 1.2 %collective-permute-done.13 = f32[64,128]{1,0:T(8,128)S(1)} collective-permute-done((f32[64,128]{1,0:T(8,128)S(1)}, f32[64,128]{1,0:T(8,128)S(1)}, u32[]{:S(2)}, u32[]{:S(2)}) %collective-permute-start.13) | collective-permute-done | bytes 32800 | tf_op jit(solution)/shard_map/ppermute | solution.py:28
  65.2 1.6 %collective-permute-done.14 = f32[64,128]{1,0:T(8,128)S(1)} collective-permute-done((f32[64,128]{1,0:T(8,128)S(1)}, f32[64,128]{1,0:T(8,128)S(1)}, u32[]{:S(2)}, u32[]{:S(2)}) %collective-permute-start.14) | collective-permute-done | bytes 32800 | tf_op jit(solution)/shard_map/ppermute | solution.py:28
  67.0 0.6 fusion
  67.6 0.6 maximum_multiply_fusion
  (34 shorter events, 3.7 us)
Async XLA Ops:
  0.6 3.8 %collective-permute-start = (f32[16,4096]{1,0:T(8,128)}, f32[16,4096]{1,0:T(8,128)S(1)}, u32[]{:S(2)}, u32[]{:S(2)}) collective-permute-start(f32[16,4096]{1,0:T(8,128)} %bitcast.13), channel_id=1, source_target_pairs={{0,1},{1,0},{2,3},{3,2},{4,5},{5,4},{6,7},{7,6},{8,9},{9,8},{10,11... | collective-permute-start | bytes 786440 | tf_op jit(solution)/shard_map/ppermute | solution.py:28
  1.3 0.9 %copy-start.1 = (f32[4096,16]{0,1:T(8,128)S(1)}, f32[4096,16]{0,1:T(8,128)}, u32[]{:S(2)}) copy-start(f32[4096,16]{0,1:T(8,128)} %param.5) | copy-start | bytes 786436
  2.2 0.8 %copy-start.2 = (bf16[128,256]{1,0:T(8,128)(2,1)S(1)}, bf16[128,256]{1,0:T(8,128)(2,1)}, u32[]{:S(2)}) copy-start(bf16[128,256]{1,0:T(8,128)(2,1)} %refs_3_.1) | copy-start | bytes 196612
  3.1 0.7 copy-start.3
  4.4 6.5 %collective-permute-start.4 = (f32[128,128]{1,0:T(8,128)S(1)}, f32[128,128]{1,0:T(8,128)S(1)}, u32[]{:S(2)}, u32[]{:S(2)}) collective-permute-start(f32[128,128]{1,0:T(8,128)S(1)} %get-tuple-element.30), channel_id=1, source_target_pairs={{0,1},{1,0},{2,3},{3,2},{4,5},{5,4},{6,7},{7,6},{8,9},{9,8},{10,11... | collective-permute-start | bytes 196616 | tf_op jit(solution)/shard_map/ppermute | solution.py:28
  5.1 7.7 %collective-permute-start.3 = (f32[2,16,512]{2,1,0:T(8,128)S(1)}, f32[2,16,512]{2,1,0:T(8,128)S(1)}, u32[]{:S(2)}, u32[]{:S(2)}) collective-permute-start(f32[2,16,512]{2,1,0:T(8,128)S(1)} %get-tuple-element.28), channel_id=1, source_target_pairs={{0,6},{1,7},{2,4},{3,5},{4,2},{5,3},{6,0},{7,1},{8,14},{9,15},{10,... | collective-permute-start | bytes 196616 | tf_op jit(solution)/shard_map/ppermute | solution.py:28
  10.2 5.8 %collective-permute-start.2 = (f32[2,16,512]{2,1,0:T(8,128)S(1)}, f32[2,16,512]{2,1,0:T(8,128)S(1)}, u32[]{:S(2)}, u32[]{:S(2)}) collective-permute-start(f32[2,16,512]{2,1,0:T(8,128)S(1)} %get-tuple-element.27), channel_id=1, source_target_pairs={{0,4},{1,5},{2,6},{3,7},{4,0},{5,1},{6,2},{7,3},{8,12},{9,13},{10,... | collective-permute-start | bytes 196616 | tf_op jit(solution)/shard_map/ppermute | solution.py:28
  10.2 5.8 %collective-permute-start.1 = (f32[2,16,512]{2,1,0:T(8,128)S(1)}, f32[2,16,512]{2,1,0:T(8,128)S(1)}, u32[]{:S(2)}, u32[]{:S(2)}) collective-permute-start(f32[2,16,512]{2,1,0:T(8,128)S(1)} %get-tuple-element.26), channel_id=1, source_target_pairs={{0,2},{1,3},{2,0},{3,1},{4,6},{5,7},{6,4},{7,5},{8,10},{9,11},{10,... | collective-permute-start | bytes 196616 | tf_op jit(solution)/shard_map/ppermute | solution.py:28
  16.0 10.2 %collective-permute-start.7 = (f32[8,16,512]{2,1,0:T(8,128)S(1)}, f32[8,16,512]{2,1,0:T(8,128)S(1)}, u32[]{:S(2)}, u32[]{:S(2)}) collective-permute-start(f32[8,16,512]{2,1,0:T(8,128)S(1)} %pad_maximum_fusion.1.after_ref), channel_id=1, source_target_pairs={{0,24},{8,16},{16,8},{24,0},{1,25},{9,17},{17,9},{25,1},{2,26},{10... | collective-permute-start | bytes 786440 | tf_op jit(solution)/shard_map/ppermute | solution.py:28
  18.5 11.9 %collective-permute-start.6 = (f32[8,16,512]{2,1,0:T(8,128)S(1)}, f32[8,16,512]{2,1,0:T(8,128)S(1)}, u32[]{:S(2)}, u32[]{:S(2)}) collective-permute-start(f32[8,16,512]{2,1,0:T(8,128)S(1)} %pad_maximum_fusion.1.after_ref), channel_id=1, source_target_pairs={{0,16},{8,24},{16,0},{24,8},{1,17},{9,25},{17,1},{25,9},{2,18},{10... | collective-permute-start | bytes 786440 | tf_op jit(solution)/shard_map/ppermute | solution.py:28
  19.0 11.5 %collective-permute-start.5 = (f32[8,16,512]{2,1,0:T(8,128)S(1)}, f32[8,16,512]{2,1,0:T(8,128)S(1)}, u32[]{:S(2)}, u32[]{:S(2)}) collective-permute-start(f32[8,16,512]{2,1,0:T(8,128)S(1)} %pad_maximum_fusion.1.after_ref), channel_id=1, source_target_pairs={{0,8},{8,0},{16,24},{24,16},{1,9},{9,1},{17,25},{25,17},{2,10},{10... | collective-permute-start | bytes 786440 | tf_op jit(solution)/shard_map/ppermute | solution.py:28
  19.6 3.4 %copy-start = (bf16[1024,4096]{1,0:T(8,128)(2,1)S(1)}, bf16[1024,4096]{1,0:T(8,128)(2,1)}, u32[]{:S(2)}) copy-start(bf16[1024,4096]{1,0:T(8,128)(2,1)} %source_ref.1) | copy-start | bytes 25165828
  33.9 13.4 %collective-permute-start.8 = (f32[8,64,128]{2,1,0:T(8,128)S(1)}, f32[8,64,128]{2,1,0:T(8,128)S(1)}, u32[]{:S(2)}, u32[]{:S(2)}) collective-permute-start(f32[8,64,128]{2,1,0:T(8,128)S(1)} %multiply.2.mine_ref), channel_id=1, source_target_pairs={{0,1},{1,0},{2,3},{3,2},{4,5},{5,4},{6,7},{7,6},{8,9},{9,8},{10,11... | collective-permute-start | bytes 786440 | tf_op jit(solution)/shard_map/ppermute | solution.py:28
  34.0 8.0 %collective-permute-start.9 = (f32[2,128,128]{2,1,0:T(8,128)S(1)}, f32[2,128,128]{2,1,0:T(8,128)S(1)}, u32[]{:S(2)}, u32[]{:S(2)}) collective-permute-start(f32[2,128,128]{2,1,0:T(8,128)S(1)} %pad_maximum_fusion.2.refs_0_), channel_id=1, source_target_pairs={{0,2},{1,3},{2,0},{3,1},{4,6},{5,7},{6,4},{7,5},{8,10},{9,11},{10,... | collective-permute-start | bytes 393224 | tf_op jit(solution)/shard_map/ppermute | solution.py:28
  34.4 12.9 %collective-permute-start.10 = (f32[2,128,128]{2,1,0:T(8,128)S(1)}, f32[2,128,128]{2,1,0:T(8,128)S(1)}, u32[]{:S(2)}, u32[]{:S(2)}) collective-permute-start(f32[2,128,128]{2,1,0:T(8,128)S(1)} %pad_maximum_fusion.2.refs_0_), channel_id=1, source_target_pairs={{0,4},{1,5},{2,6},{3,7},{4,0},{5,1},{6,2},{7,3},{8,12},{9,13},{10,... | collective-permute-start | bytes 393224 | tf_op jit(solution)/shard_map/ppermute | solution.py:28
  36.7 10.6 %collective-permute-start.11 = (f32[2,128,128]{2,1,0:T(8,128)S(1)}, f32[2,128,128]{2,1,0:T(8,128)S(1)}, u32[]{:S(2)}, u32[]{:S(2)}) collective-permute-start(f32[2,128,128]{2,1,0:T(8,128)S(1)} %pad_maximum_fusion.2.refs_0_), channel_id=1, source_target_pairs={{0,6},{1,7},{2,4},{3,5},{4,2},{5,3},{6,0},{7,1},{8,14},{9,15},{10,... | collective-permute-start | bytes 393224 | tf_op jit(solution)/shard_map/ppermute | solution.py:28
  47.5 5.4 %collective-permute-start.16 = (f32[64,128]{1,0:T(8,128)S(1)}, f32[64,128]{1,0:T(8,128)S(1)}, u32[]{:S(2)}, u32[]{:S(2)}) collective-permute-start(f32[64,128]{1,0:T(8,128)S(1)} %get-tuple-element.37), channel_id=1, source_target_pairs={{0,4},{1,5},{2,6},{3,7},{4,0},{5,1},{6,2},{7,3},{8,12},{9,13},{10,... | collective-permute-start | bytes 98312 | tf_op jit(solution)/shard_map/ppermute | solution.py:28
  50.7 5.8 %collective-permute-start.17 = (f32[64,128]{1,0:T(8,128)S(1)}, f32[64,128]{1,0:T(8,128)S(1)}, u32[]{:S(2)}, u32[]{:S(2)}) collective-permute-start(f32[64,128]{1,0:T(8,128)S(1)} %get-tuple-element.37), channel_id=1, source_target_pairs={{0,6},{1,7},{2,4},{3,5},{4,2},{5,3},{6,0},{7,1},{8,14},{9,15},{10,... | collective-permute-start | bytes 98312 | tf_op jit(solution)/shard_map/ppermute | solution.py:28
  52.5 4.3 %collective-permute-start.15 = (f32[64,128]{1,0:T(8,128)S(1)}, f32[64,128]{1,0:T(8,128)S(1)}, u32[]{:S(2)}, u32[]{:S(2)}) collective-permute-start(f32[64,128]{1,0:T(8,128)S(1)} %get-tuple-element.37), channel_id=1, source_target_pairs={{0,2},{1,3},{2,0},{3,1},{4,6},{5,7},{6,4},{7,5},{8,10},{9,11},{10,... | collective-permute-start | bytes 98312 | tf_op jit(solution)/shard_map/ppermute | solution.py:28
  56.8 5.9 %collective-permute-start.19 = (f32[64,128]{1,0:T(8,128)S(1)}, f32[64,128]{1,0:T(8,128)S(1)}, u32[]{:S(2)}, u32[]{:S(2)}) collective-permute-start(f32[64,128]{1,0:T(8,128)S(1)} %add_add_fusion.1), channel_id=1, source_target_pairs={{0,16},{8,24},{16,0},{24,8},{1,17},{9,25},{17,1},{25,9},{2,18},{10... | collective-permute-start | bytes 98312 | tf_op jit(solution)/shard_map/ppermute | solution.py:28
  58.3 5.6 %collective-permute-start.20 = (f32[64,128]{1,0:T(8,128)S(1)}, f32[64,128]{1,0:T(8,128)S(1)}, u32[]{:S(2)}, u32[]{:S(2)}) collective-permute-start(f32[64,128]{1,0:T(8,128)S(1)} %add_add_fusion.1), channel_id=1, source_target_pairs={{0,24},{8,16},{16,8},{24,0},{1,25},{9,17},{17,9},{25,1},{2,26},{10... | collective-permute-start | bytes 98312 | tf_op jit(solution)/shard_map/ppermute | solution.py:28
  59.8 4.0 %collective-permute-start.18 = (f32[64,128]{1,0:T(8,128)S(1)}, f32[64,128]{1,0:T(8,128)S(1)}, u32[]{:S(2)}, u32[]{:S(2)}) collective-permute-start(f32[64,128]{1,0:T(8,128)S(1)} %add_add_fusion.1), channel_id=1, source_target_pairs={{0,8},{8,0},{16,24},{24,16},{1,9},{9,1},{17,25},{25,17},{2,10},{10... | collective-permute-start | bytes 98312 | tf_op jit(solution)/shard_map/ppermute | solution.py:28
  60.3 4.8 %collective-permute-start.13 = (f32[64,128]{1,0:T(8,128)S(1)}, f32[64,128]{1,0:T(8,128)S(1)}, u32[]{:S(2)}, u32[]{:S(2)}) collective-permute-start(f32[64,128]{1,0:T(8,128)S(1)} %get-tuple-element.35), channel_id=1, source_target_pairs={{0,4},{1,5},{2,6},{3,7},{4,0},{5,1},{6,2},{7,3},{8,12},{9,13},{10,... | collective-permute-start | bytes 98312 | tf_op jit(solution)/shard_map/ppermute | solution.py:28
  60.9 5.8 %collective-permute-start.14 = (f32[64,128]{1,0:T(8,128)S(1)}, f32[64,128]{1,0:T(8,128)S(1)}, u32[]{:S(2)}, u32[]{:S(2)}) collective-permute-start(f32[64,128]{1,0:T(8,128)S(1)} %get-tuple-element.36), channel_id=1, source_target_pairs={{0,6},{1,7},{2,4},{3,5},{4,2},{5,3},{6,0},{7,1},{8,14},{9,15},{10,... | collective-permute-start | bytes 98312 | tf_op jit(solution)/shard_map/ppermute | solution.py:28
  62.7 4.3 %collective-permute-start.12 = (f32[64,128]{1,0:T(8,128)S(1)}, f32[64,128]{1,0:T(8,128)S(1)}, u32[]{:S(2)}, u32[]{:S(2)}) collective-permute-start(f32[64,128]{1,0:T(8,128)S(1)} %get-tuple-element.34), channel_id=1, source_target_pairs={{0,2},{1,3},{2,0},{3,1},{4,6},{5,7},{6,4},{7,5},{8,10},{9,11},{10,... | collective-permute-start | bytes 98312 | tf_op jit(solution)/shard_map/ppermute | solution.py:28
  63.9 3.7 %collective-permute-start.21 = (f32[64,128]{1,0:T(8,128)S(1)}, f32[64,128]{1,0:T(8,128)S(1)}, u32[]{:S(2)}, u32[]{:S(2)}) collective-permute-start(f32[64,128]{1,0:T(8,128)S(1)} %add_add_fusion), channel_id=1, source_target_pairs={{0,1},{1,0},{2,3},{3,2},{4,5},{5,4},{6,7},{7,6},{8,9},{9,8},{10,11... | collective-permute-start | bytes 98312 | tf_op jit(solution)/shard_map/ppermute | solution.py:28

commit v4 on v3

v4 whole, which is shorter than its diff:
```python
import math

import jax
import jax.numpy as jnp
from jax import lax
from jax.experimental import pallas as pl
from jax.experimental.pallas import tpu as pltpu
from jax.sharding import PartitionSpec as P


ROW_BLOCK = 16
COL_BLOCK = 4
LANES = 128
SUBLANES = 8
GROUPS = LANES // ROW_BLOCK
MIB = 1 << 20
IN_SMEM = pl.BlockSpec(memory_space=pltpu.SMEM)
IN_VMEM = pl.BlockSpec(memory_space=pltpu.VMEM)
IN_HBM = pl.BlockSpec(memory_space=pltpu.HBM)


def params(mib):
    return pltpu.CompilerParams(vmem_limit_bytes=mib * MIB)


def swap(value, axis, mask):
    count = lax.axis_size(axis)
    return lax.ppermute(value, axis, [(i, i ^ mask) for i in range(count)])


def tree_sum(terms):
    while len(terms) > 1:
        terms = [terms[i] + terms[i + 1] for i in range(0, len(terms), 2)]
    return terms[0]


def cut_kernel(pos_ref, source_ref, *out_refs):
    p = pos_ref[0]
    for d, out_ref in enumerate(out_refs):
        chunk = out_ref.shape[1]
        out_ref[...] = source_ref[:, pl.ds(pl.multiple_of((p ^ (2 * d)) * chunk, LANES), chunk)]


def cut(pos, source, snap_count):
    width, rows = source.shape
    piece = jax.ShapeDtypeStruct((width, rows // snap_count), jnp.float32)
    return pl.pallas_call(
        cut_kernel,
        out_shape=[piece] * (snap_count // 2),
        in_specs=[IN_SMEM, IN_VMEM],
        out_specs=[IN_VMEM] * (snap_count // 2),
        compiler_params=params(2),
        name="cut",
    )(pos, source)


def join_kernel(pos_ref, source_ref, *refs):
    p = pos_ref[0]
    own_refs, out_refs = refs[: len(refs) // 2], refs[len(refs) // 2 :]
    for d, (own_ref, out_ref) in enumerate(zip(own_refs, out_refs)):
        chunk = own_ref.shape[1]
        out_ref[0] = own_ref[...]
        out_ref[1] = source_ref[:, pl.ds(pl.multiple_of((p ^ (2 * d)) * chunk, LANES), chunk)]


def join(pos, source, own_pieces):
    piece = jax.ShapeDtypeStruct((2, *own_pieces[0].shape), jnp.float32)
    return pl.pallas_call(
        join_kernel,
        out_shape=[piece] * len(own_pieces),
        in_specs=[IN_SMEM] + [IN_VMEM] * (1 + len(own_pieces)),
        out_specs=[IN_VMEM] * len(own_pieces),
        compiler_params=params(2),
        name="join",
    )(pos, source, *own_pieces)


def stage_kernel(after_ref, source_ref, target_ref, sems):
    rows = source_ref.shape[0] // sems.shape[0]
    parts = [pl.ds(i * rows, rows) for i in range(sems.shape[0])]
    copies = [pltpu.make_async_copy(source_ref.at[r], target_ref.at[r], sems.at[i]) for i, r in enumerate(parts)]
    for copy in copies:
        copy.start()
    for copy in copies:
        copy.wait()


def stage(after, snapshots):
    return pl.pallas_call(
        stage_kernel,
        out_shape=jax.ShapeDtypeStruct(snapshots.shape, snapshots.dtype),
        in_specs=[IN_HBM, IN_HBM],
        out_specs=IN_VMEM,
        scratch_shapes=[pltpu.SemaphoreType.DMA((4,))],
        compiler_params=params(42),
        name="stage",
    )(after, snapshots)


def interleave(blocks):
    lane = lax.broadcasted_iota(jnp.int32, blocks[0].shape, 1) // ROW_BLOCK
    step = 1
    while step < GROUPS:
        high = (lane & step) != 0
        mixed = list(blocks)
        for a in range(GROUPS):
            if a & step == 0:
                b = a | step
                low_of_b = pltpu.roll(blocks[b], step * ROW_BLOCK, 1)
                high_of_a = pltpu.roll(blocks[a], LANES - step * ROW_BLOCK, 1)
                mixed[a] = jnp.where(high, low_of_b, blocks[a])
                mixed[b] = jnp.where(high, blocks[b], high_of_a)
        blocks = mixed
        step *= 2
    return blocks


def all_modes(slab_ref, q, slot, t):
    space_count, _, width, _ = slab_ref.shape
    low = lax.broadcasted_iota(jnp.int32, (SUBLANES, LANES), 0) < COL_BLOCK
    pairs = space_count // 2
    tiles = [None] * (space_count * width // SUBLANES)
    lanes = slice(t * LANES, (t + 1) * LANES)
    for u in range(pairs):
        for i in range(width // SUBLANES):
            rows = slice(i * SUBLANES, (i + 1) * SUBLANES)
            even = slab_ref[q ^ (2 * u), slot, rows, lanes]
            odd = slab_ref[q ^ (2 * u + 1), slot, rows, lanes]
            tiles[2 * i * pairs + u] = jnp.where(low, even, pltpu.roll(odd, COL_BLOCK, 0))
            tiles[(2 * i + 1) * pairs + u] = jnp.where(low, pltpu.roll(even, COL_BLOCK, 0), odd)
    return jnp.concatenate(tiles)


def scale_column(eig):
    modes = eig.shape[1]
    row = lax.broadcasted_iota(jnp.int32, (modes, modes), 0)
    column = lax.broadcasted_iota(jnp.int32, (modes, modes), 1)
    value = jnp.sum(jnp.where(row == column, eig, 0.0), axis=1, keepdims=True)
    return jnp.broadcast_to(lax.rsqrt(value), (modes, LANES))


def multiply_kernel(pos_ref, eig_ref, slab_ref, snap_ref, out_ref, scaled_ref, cells_ref):
    p, q = pos_ref[0], pos_ref[1]
    _, snap_count, _, chunk = slab_ref.shape
    outer_count = snap_count // GROUPS
    scale = scale_column(eig_ref[...])
    for outer in range(outer_count):
        for t in range(chunk // LANES):
            slots = [p ^ (outer * GROUPS + g) for g in range(GROUPS)]
            for j, block in enumerate(interleave([all_modes(slab_ref, q, slot, t) for slot in slots])):
                tile = (t * GROUPS + j) * outer_count + outer
                scaled_ref[:, tile * LANES : (tile + 1) * LANES] = (block * scale).astype(jnp.bfloat16)
    total = lax.dot_general(
        snap_ref[...], scaled_ref[...], (((1,), (1,)), ((), ())), preferred_element_type=jnp.float32
    ).T
    cells = cells_ref.shape[2]
    for owner in range(snap_count):
        cells_ref[owner] = total[:, owner * cells : (owner + 1) * cells]
    for s in range(snap_count):
        out_ref[s] = cells_ref[p ^ s]


def multiply(pos, eig, slab, snapshots):
    space_count, snap_count, width, _ = slab.shape
    cells, depth = snapshots.shape
    modes = width * space_count
    out = (snap_count, modes, cells // snap_count)
    return pl.pallas_call(
        multiply_kernel,
        out_shape=jax.ShapeDtypeStruct(out, jnp.float32),
        in_specs=[IN_SMEM, IN_VMEM, IN_VMEM, IN_VMEM],
        out_specs=IN_VMEM,
        scratch_shapes=[pltpu.VMEM((modes, depth), jnp.bfloat16), pltpu.VMEM(out, jnp.float32)],
        compiler_params=params(12),
        name="multiply",
    )(pos, eig, slab, snapshots)


def pair_kernel(mine_ref, theirs_ref, *refs):
    held_refs, out_refs = refs[: len(refs) // 2], refs[len(refs) // 2 :]
    snap_count, modes, _ = mine_ref.shape
    sums = [mine_ref[s] + theirs_ref[s ^ 1] for s in range(snap_count)]
    held = [held_refs[s // 2][s % 2].astype(jnp.bfloat16) for s in range(snap_count)]
    wide = jnp.concatenate(sums, axis=1)
    high = wide.astype(jnp.bfloat16)
    low = (wide - high.astype(jnp.float32)).astype(jnp.bfloat16)
    both = jnp.dot(jnp.concatenate([high, low]), jnp.concatenate(held), preferred_element_type=jnp.float32)
    coef = both[:modes] + both[modes:]
    for d, out_ref in enumerate(out_refs):
        out_ref[:, : coef.shape[1]] = coef
        out_ref[:, coef.shape[1] :] = sums[2 * d]


def pair(mine, theirs, held):
    snap_count, modes, cells = mine.shape
    out = jax.ShapeDtypeStruct((modes, held[0].shape[2] + cells), jnp.float32)
    return pl.pallas_call(
        pair_kernel,
        out_shape=[out] * (snap_count // 2),
        in_specs=[IN_VMEM] * (2 + len(held)),
        out_specs=[IN_VMEM] * (snap_count // 2),
        compiler_params=params(6),
        name="pair",
    )(mine, theirs, *held)


def per_device(snapshots, vectors_cyclic, eigen_values, held_out):
    snap_count = lax.axis_size("snap")
    space_count = lax.axis_size("space")
    p, q = lax.axis_index("snap"), lax.axis_index("space")
    pos = jnp.stack([p, q]).astype(jnp.int32)
    chips = range(1, snap_count // 2)
    others = range(1, space_count)

    own = vectors_cyclic.T
    other = swap(own, "snap", 1)
    pieces = join(pos, other, cut(pos, own, snap_count))
    near = [pieces[0]] + [swap(pieces[d], "snap", 2 * d) for d in chips]

    first, second = near[0], jnp.concatenate(near[1:])
    firsts = [first] + [swap(first, "space", e) for e in others]
    seconds = [second] + [swap(second, "space", e) for e in others]
    slab = jnp.stack([jnp.concatenate(parts) for parts in zip(firsts, seconds)])

    half = held_out.shape[1] // 2
    wide = held_out.astype(jnp.float32)
    held_keep = lax.dynamic_slice_in_dim(wide, (p & 1) * half, half, 1)
    held_send = lax.dynamic_slice_in_dim(wide, (1 - (p & 1)) * half, half, 1)
    held = jnp.stack([held_keep, swap(held_send, "snap", 1)])
    held = [held] + [swap(held, "snap", 2 * d) for d in chips]

    mine = multiply(pos, eigen_values[None, :], slab, stage(pieces[0], snapshots))
    both = pair(mine, swap(mine, "snap", 1), held)
    both = tree_sum([both[0]] + [swap(both[d], "snap", 2 * d) for d in chips])
    coef, modes = both[:, :half], both[:, half:]
    coef = tree_sum([coef] + [swap(coef, "space", e) for e in others])
    far = swap(coef, "snap", 1)
    even = p % 2 == 0
    coefficients = jnp.concatenate([jnp.where(even, coef, far), jnp.where(even, far, coef)], axis=1)

    total_cells = snapshots.shape[0] * space_count
    return (modes.astype(jnp.bfloat16).T, coefficients / math.sqrt(total_cells))


def solution(mesh):
    return jax.shard_map(
        per_device,
        mesh=mesh,
        in_specs=(P("space", "snap"), P("snap", "space"), P(), P(("space", "snap"), None)),
        out_specs=(P(("space", "snap"), None), P()),
        check_vma=False,
    )
```

time: 68.5 us -> 72.4 us (1.057)
  waiting for transfers between devices: 28.3 us -> 33.3 us
  local copies, waits for them, and re-layouts: 5.82 us -> 1.6 us
  Pallas kernels: 5.27 us -> 8.23 us
    ppermute x22, waiting for transfers between devices: 28.3 us -> 33.3 us  [swap(): return lax.ppermute(value, axis, [(i, i ^ mask) for i in range(count)])]
    unnamed x8 -> x6, local copies, waits for them, and re-layouts: 5.82 us -> 0.97 us
    pallas_call x1, Pallas kernels: 0.57 us -> 3.5 us  [stage(): pl.pallas_call(stage_kernel, out_shape=jax.ShapeDtypeStruct(snapshots.sha...]
    convert_element_type x0 -> x1, other arithmetic: none -> 0.85 us  [per_device(): wide = held_out.astype(jnp.float32)]
  transfers between devices with their start and end apart: 22 -> 22, of which waited for: 13 -> 10; matrix products, arithmetic and copies ran while one was open for 1% -> 2% of each run, Pallas kernels for 3% -> 10%
where the time goes in v4:
time: 72.4 us; the launch traced here: 72.2 us
  waiting for transfers between devices  33.3 us (46%)
  starting transfers between devices  26.6 us (37%)
  Pallas kernels  8.23 us (11%)
  other arithmetic  1.75 us (2%)
  local copies, waits for them, and re-layouts  1.6 us (2%)
  between operations  0.83 us (1%)
    ppermute x22, waiting for transfers between devices, swap(): return lax.ppermute(value, axis, [(i, i ^ mask) for i in range(count)])  33.3 us
    ppermute x22, starting transfers between devices, swap(): return lax.ppermute(value, axis, [(i, i ^ mask) for i in range(count)])  26.6 us
    pallas_call x1, Pallas kernels, stage(): pl.pallas_call(stage_kernel, out_shape=jax.ShapeDtypeStruct(snapshots.sha...  3.5 us
    pallas_call x1, Pallas kernels, multiply(): pl.pallas_call(multiply_kernel, out_shape=jax.ShapeDtypeStruct(out, jnp.f...  3.38 us
  transfers between devices with their start and end apart: 22, of which 10 were waited for; matrix products, arithmetic and copies ran while one was open for 2% of the time, Pallas kernels for 10%

profile of v4, /device:TPU:0, one launch (start us, length us, event | category | flops | bytes accessed | tf_op | source)
XLA Modules:
  0.0 72.2 jit_solution(4574234961724357310)
XLA Ops:
  1.3 0.9 %copy-done = f32[4096,16]{0,1:T(8,128)S(1)} copy-done((f32[4096,16]{0,1:T(8,128)S(1)}, f32[4096,16]{0,1:T(8,128)}, u32[]{:S(2)}) %copy-start) | copy-done | bytes 262168
  2.8 0.6 join.1
  3.4 2.8 %collective-permute-start.1 = (f32[2,16,512]{2,1,0:T(8,128)S(1)}, f32[2,16,512]{2,1,0:T(8,128)S(1)}, u32[]{:S(2)}, u32[]{:S(2)}) collective-permute-start(f32[2,16,512]{2,1,0:T(8,128)S(1)} %get-tuple-element.19), channel_id=1, source_target_pairs={{0,2},{1,3},{2,0},{3,1},{4,6},{5,7},{6,4},{7,5},{8,10},{9,11},{10,... | collective-permute-start | bytes 196616 | tf_op jit(solution)/shard_map/ppermute | solution.py:28
  6.1 0.8 %convert_element_type.4 = f32[128,256]{1,0:T(8,128)S(1)} convert(bf16[128,256]{1,0:T(8,128)(2,1)} %param.7) | non-fusion elementwise | flops 32768 | bytes 196608 | tf_op jit(solution)/shard_map/convert_element_type | solution.py:226
  7.0 2.7 %collective-permute-start.2 = (f32[2,16,512]{2,1,0:T(8,128)S(1)}, f32[2,16,512]{2,1,0:T(8,128)S(1)}, u32[]{:S(2)}, u32[]{:S(2)}) collective-permute-start(f32[2,16,512]{2,1,0:T(8,128)S(1)} %get-tuple-element.20), channel_id=1, source_target_pairs={{0,4},{1,5},{2,6},{3,7},{4,0},{5,1},{6,2},{7,3},{8,12},{9,13},{10,... | collective-permute-start | bytes 196616 | tf_op jit(solution)/shard_map/ppermute | solution.py:28
  9.6 4.2 %collective-permute-done.2 = f32[2,16,512]{2,1,0:T(8,128)S(1)} collective-permute-done((f32[2,16,512]{2,1,0:T(8,128)S(1)}, f32[2,16,512]{2,1,0:T(8,128)S(1)}, u32[]{:S(2)}, u32[]{:S(2)}) %collective-permute-start.2) | collective-permute-done | bytes 65568 | tf_op jit(solution)/shard_map/ppermute | solution.py:28
  13.8 1.9 %collective-permute-done.3 = f32[2,16,512]{2,1,0:T(8,128)S(1)} collective-permute-done((f32[2,16,512]{2,1,0:T(8,128)S(1)}, f32[2,16,512]{2,1,0:T(8,128)S(1)}, u32[]{:S(2)}, u32[]{:S(2)}) %collective-permute-start.3) | collective-permute-done | bytes 65568 | tf_op jit(solution)/shard_map/ppermute | solution.py:28
  15.7 1.5 %collective-permute-start.5 = (f32[6,16,512]{2,1,0:T(8,128)S(1)}, f32[6,16,512]{2,1,0:T(8,128)S(1)}, u32[]{:S(2)}, u32[]{:S(2)}) collective-permute-start(f32[6,16,512]{2,1,0:T(8,128)S(1)} %constant_dynamic-update-slice_fusion), channel_id=1, source_target_pairs={{0,8},{8,0},{16,24},{24,16},{1,9},{9,1},{17,25},{25,17},{2,10},{10... | collective-permute-start | bytes 589832 | tf_op jit(solution)/shard_map/ppermute | solution.py:28
  17.3 0.6 collective-permute-start.4
  17.9 1.5 %collective-permute-start.6 = (f32[2,16,512]{2,1,0:T(8,128)S(1)}, f32[2,16,512]{2,1,0:T(8,128)S(1)}, u32[]{:S(2)}, u32[]{:S(2)}) collective-permute-start(f32[2,16,512]{2,1,0:T(8,128)S(1)} %get-tuple-element.18.after_ref), channel_id=1, source_target_pairs={{0,16},{8,24},{16,0},{24,8},{1,17},{9,25},{17,1},{25,9},{2,18},{10... | collective-permute-start | bytes 196616 | tf_op jit(solution)/shard_map/ppermute | solution.py:28
  19.4 3.5 %stage.1.snap_ref = bf16[1024,4096]{1,0:T(8,128)(2,1)S(1)} custom-call(f32[2,16,512]{2,1,0:T(8,128)S(1)} %get-tuple-element.18.after_ref, bf16[1024,4096]{1,0:T(8,128)(2,1)} %source_ref.1), custom_call_target="tpu_custom_call" | custom-call | tf_op jit(solution)/shard_map/stage/pallas_call | solution.py:89
  22.9 0.6 collective-permute-start.7
  23.5 2.5 %collective-permute-start.8 = (f32[2,16,512]{2,1,0:T(8,128)S(1)}, f32[2,16,512]{2,1,0:T(8,128)S(1)}, u32[]{:S(2)}, u32[]{:S(2)}) collective-permute-start(f32[2,16,512]{2,1,0:T(8,128)S(1)} %get-tuple-element.18.after_ref), channel_id=1, source_target_pairs={{0,24},{8,16},{16,8},{24,0},{1,25},{9,17},{17,9},{25,1},{2,26},{10... | collective-permute-start | bytes 196616 | tf_op jit(solution)/shard_map/ppermute | solution.py:28
  26.6 8.7 %collective-permute-done.7 = f32[6,16,512]{2,1,0:T(8,128)S(1)} collective-permute-done((f32[6,16,512]{2,1,0:T(8,128)S(1)}, f32[6,16,512]{2,1,0:T(8,128)S(1)}, u32[]{:S(2)}, u32[]{:S(2)}) %collective-permute-start.7) | collective-permute-done | bytes 196640 | tf_op jit(solution)/shard_map/ppermute | solution.py:28
  35.4 3.4 %multiply.2.mine_ref = f32[8,64,128]{2,1,0:T(8,128)S(1)} custom-call(s32[2]{0:T(128)S(1)} %pad_add_fusion.pos_ref, f32[1,64]{1,0:T(1,128)S(1)} %bitcast.19, f32[4,8,16,512]{3,2,1,0:T(8,128)S(1)} %pad_maximum_fusion.slab_ref, bf16[1024,4096]{1,0:T(8,128)(2,1)S(1)} %stage.1.snap_ref), custom_call_target="tpu_custom_call" | custom-call | tf_op jit(solution)/shard_map/multiply/pallas_call | solution.py:168
  38.9 1.1 %collective-permute-start.12 = (f32[2,128,128]{2,1,0:T(8,128)S(1)}, f32[2,128,128]{2,1,0:T(8,128)S(1)}, u32[]{:S(2)}, u32[]{:S(2)}) collective-permute-start(f32[2,128,128]{2,1,0:T(8,128)S(1)} %pad_maximum_fusion.1.refs_0_), channel_id=1, source_target_pairs={{0,2},{1,3},{2,0},{3,1},{4,6},{5,7},{6,4},{7,5},{8,10},{9,11},{10,... | collective-permute-start | bytes 393224 | tf_op jit(solution)/shard_map/ppermute | solution.py:28
  40.0 1.9 %collective-permute-start.13 = (f32[2,128,128]{2,1,0:T(8,128)S(1)}, f32[2,128,128]{2,1,0:T(8,128)S(1)}, u32[]{:S(2)}, u32[]{:S(2)}) collective-permute-start(f32[2,128,128]{2,1,0:T(8,128)S(1)} %pad_maximum_fusion.1.refs_0_), channel_id=1, source_target_pairs={{0,4},{1,5},{2,6},{3,7},{4,0},{5,1},{6,2},{7,3},{8,12},{9,13},{10,... | collective-permute-start | bytes 393224 | tf_op jit(solution)/shard_map/ppermute | solution.py:28
  42.0 1.4 %collective-permute-start.14 = (f32[2,128,128]{2,1,0:T(8,128)S(1)}, f32[2,128,128]{2,1,0:T(8,128)S(1)}, u32[]{:S(2)}, u32[]{:S(2)}) collective-permute-start(f32[2,128,128]{2,1,0:T(8,128)S(1)} %pad_maximum_fusion.1.refs_0_), channel_id=1, source_target_pairs={{0,6},{1,7},{2,4},{3,5},{4,2},{5,3},{6,0},{7,1},{8,14},{9,15},{10,... | collective-permute-start | bytes 393224 | tf_op jit(solution)/shard_map/ppermute | solution.py:28
  43.4 3.9 %collective-permute-done.12.refs_1_ = f32[2,128,128]{2,1,0:T(8,128)S(1)} collective-permute-done((f32[2,128,128]{2,1,0:T(8,128)S(1)}, f32[2,128,128]{2,1,0:T(8,128)S(1)}, u32[]{:S(2)}, u32[]{:S(2)}) %collective-permute-start.12) | collective-permute-done | bytes 131104 | tf_op jit(solution)/shard_map/ppermute | solution.py:28
  47.3 5.7 %collective-permute-done.13.refs_2_ = f32[2,128,128]{2,1,0:T(8,128)S(1)} collective-permute-done((f32[2,128,128]{2,1,0:T(8,128)S(1)}, f32[2,128,128]{2,1,0:T(8,128)S(1)}, u32[]{:S(2)}, u32[]{:S(2)}) %collective-permute-start.13) | collective-permute-done | bytes 131104 | tf_op jit(solution)/shard_map/ppermute | solution.py:28
  53.2 2.7 %collective-permute-start.15 = (f32[64,256]{1,0:T(8,128)S(1)}, f32[64,256]{1,0:T(8,128)S(1)}, u32[]{:S(2)}, u32[]{:S(2)}) collective-permute-start(f32[64,256]{1,0:T(8,128)S(1)} %get-tuple-element.23), channel_id=1, source_target_pairs={{0,2},{1,3},{2,0},{3,1},{4,6},{5,7},{6,4},{7,5},{8,10},{9,11},{10,... | collective-permute-start | bytes 196616 | tf_op jit(solution)/shard_map/ppermute | solution.py:28
  55.9 1.1 %collective-permute-start.16 = (f32[64,256]{1,0:T(8,128)S(1)}, f32[64,256]{1,0:T(8,128)S(1)}, u32[]{:S(2)}, u32[]{:S(2)}) collective-permute-start(f32[64,256]{1,0:T(8,128)S(1)} %get-tuple-element.24), channel_id=1, source_target_pairs={{0,4},{1,5},{2,6},{3,7},{4,0},{5,1},{6,2},{7,3},{8,12},{9,13},{10,... | collective-permute-start | bytes 196616 | tf_op jit(solution)/shard_map/ppermute | solution.py:28
  57.0 1.4 %collective-permute-start.17 = (f32[64,256]{1,0:T(8,128)S(1)}, f32[64,256]{1,0:T(8,128)S(1)}, u32[]{:S(2)}, u32[]{:S(2)}) collective-permute-start(f32[64,256]{1,0:T(8,128)S(1)} %get-tuple-element.25), channel_id=1, source_target_pairs={{0,6},{1,7},{2,4},{3,5},{4,2},{5,3},{6,0},{7,1},{8,14},{9,15},{10,... | collective-permute-start | bytes 196616 | tf_op jit(solution)/shard_map/ppermute | solution.py:28
  58.4 5.0 %collective-permute-done.16 = f32[64,256]{1,0:T(8,128)S(1)} collective-permute-done((f32[64,256]{1,0:T(8,128)S(1)}, f32[64,256]{1,0:T(8,128)S(1)}, u32[]{:S(2)}, u32[]{:S(2)}) %collective-permute-start.16) | collective-permute-done | bytes 65568 | tf_op jit(solution)/shard_map/ppermute | solution.py:28
  63.4 1.6 %collective-permute-start.18 = (f32[64,128]{1,0:T(8,128)S(1)}, f32[64,128]{1,0:T(8,128)S(1)}, u32[]{:S(2)}, u32[]{:S(2)}) collective-permute-start(f32[64,128]{1,0:T(8,128)S(1)} %slice.10), channel_id=1, source_target_pairs={{0,8},{8,0},{16,24},{24,16},{1,9},{9,1},{17,25},{25,17},{2,10},{10... | collective-permute-start | bytes 98312 | tf_op jit(solution)/shard_map/ppermute | solution.py:28
  65.5 1.5 %collective-permute-start.20 = (f32[64,128]{1,0:T(8,128)S(1)}, f32[64,128]{1,0:T(8,128)S(1)}, u32[]{:S(2)}, u32[]{:S(2)}) collective-permute-start(f32[64,128]{1,0:T(8,128)S(1)} %slice.10), channel_id=1, source_target_pairs={{0,24},{8,16},{16,8},{24,0},{1,25},{9,17},{17,9},{25,1},{2,26},{10... | collective-permute-start | bytes 98312 | tf_op jit(solution)/shard_map/ppermute | solution.py:28
  67.0 0.6 collective-permute-done.18
  67.6 1.3 %collective-permute-done.19 = f32[64,128]{1,0:T(8,128)S(1)} collective-permute-done((f32[64,128]{1,0:T(8,128)S(1)}, f32[64,128]{1,0:T(8,128)S(1)}, u32[]{:S(2)}, u32[]{:S(2)}) %collective-permute-start.19) | collective-permute-done | bytes 32800 | tf_op jit(solution)/shard_map/ppermute | solution.py:28
  68.9 1.4 %collective-permute-done.20 = f32[64,128]{1,0:T(8,128)S(1)} collective-permute-done((f32[64,128]{1,0:T(8,128)S(1)}, f32[64,128]{1,0:T(8,128)S(1)}, u32[]{:S(2)}, u32[]{:S(2)}) %collective-permute-start.20) | collective-permute-done | bytes 32800 | tf_op jit(solution)/shard_map/ppermute | solution.py:28
  70.4 0.6 fusion
  71.0 0.6 collective-permute-done.21
  71.6 0.6 maximum_multiply_fusion
  (39 shorter events, 2.9 us)
Async XLA Ops:
  0.6 2.1 %collective-permute-start = (f32[16,4096]{1,0:T(8,128)}, f32[16,4096]{1,0:T(8,128)S(1)}, u32[]{:S(2)}, u32[]{:S(2)}) collective-permute-start(f32[16,4096]{1,0:T(8,128)} %bitcast.17), channel_id=1, source_target_pairs={{0,1},{1,0},{2,3},{3,2},{4,5},{5,4},{6,7},{7,6},{8,9},{9,8},{10,11... | collective-permute-start | bytes 786440 | tf_op jit(solution)/shard_map/ppermute | solution.py:28
  1.3 0.9 %copy-start = (f32[4096,16]{0,1:T(8,128)S(1)}, f32[4096,16]{0,1:T(8,128)}, u32[]{:S(2)}) copy-start(f32[4096,16]{0,1:T(8,128)} %param.5) | copy-start | bytes 786436
  3.4 6.3 %collective-permute-start.1 = (f32[2,16,512]{2,1,0:T(8,128)S(1)}, f32[2,16,512]{2,1,0:T(8,128)S(1)}, u32[]{:S(2)}, u32[]{:S(2)}) collective-permute-start(f32[2,16,512]{2,1,0:T(8,128)S(1)} %get-tuple-element.19), channel_id=1, source_target_pairs={{0,2},{1,3},{2,0},{3,1},{4,6},{5,7},{6,4},{7,5},{8,10},{9,11},{10,... | collective-permute-start | bytes 196616 | tf_op jit(solution)/shard_map/ppermute | solution.py:28
  7.0 6.8 %collective-permute-start.2 = (f32[2,16,512]{2,1,0:T(8,128)S(1)}, f32[2,16,512]{2,1,0:T(8,128)S(1)}, u32[]{:S(2)}, u32[]{:S(2)}) collective-permute-start(f32[2,16,512]{2,1,0:T(8,128)S(1)} %get-tuple-element.20), channel_id=1, source_target_pairs={{0,4},{1,5},{2,6},{3,7},{4,0},{5,1},{6,2},{7,3},{8,12},{9,13},{10,... | collective-permute-start | bytes 196616 | tf_op jit(solution)/shard_map/ppermute | solution.py:28
  9.6 6.1 %collective-permute-start.3 = (f32[2,16,512]{2,1,0:T(8,128)S(1)}, f32[2,16,512]{2,1,0:T(8,128)S(1)}, u32[]{:S(2)}, u32[]{:S(2)}) collective-permute-start(f32[2,16,512]{2,1,0:T(8,128)S(1)} %get-tuple-element.21), channel_id=1, source_target_pairs={{0,6},{1,7},{2,4},{3,5},{4,2},{5,3},{6,0},{7,1},{8,14},{9,15},{10,... | collective-permute-start | bytes 196616 | tf_op jit(solution)/shard_map/ppermute | solution.py:28
  15.7 10.3 %collective-permute-start.5 = (f32[6,16,512]{2,1,0:T(8,128)S(1)}, f32[6,16,512]{2,1,0:T(8,128)S(1)}, u32[]{:S(2)}, u32[]{:S(2)}) collective-permute-start(f32[6,16,512]{2,1,0:T(8,128)S(1)} %constant_dynamic-update-slice_fusion), channel_id=1, source_target_pairs={{0,8},{8,0},{16,24},{24,16},{1,9},{9,1},{17,25},{25,17},{2,10},{10... | collective-permute-start | bytes 589832 | tf_op jit(solution)/shard_map/ppermute | solution.py:28
  17.2 21.7 %collective-permute-start.11 = (f32[128,128]{1,0:T(8,128)S(1)}, f32[128,128]{1,0:T(8,128)S(1)}, u32[]{:S(2)}, u32[]{:S(2)}) collective-permute-start(f32[128,128]{1,0:T(8,128)S(1)} %get-tuple-element.27), channel_id=1, source_target_pairs={{0,1},{1,0},{2,3},{3,2},{4,5},{5,4},{6,7},{7,6},{8,9},{9,8},{10,11... | collective-permute-start | bytes 196616 | tf_op jit(solution)/shard_map/ppermute | solution.py:28
  17.3 18.1 %copy-start.1 = (f32[64]{0:T(128)S(1)}, f32[64]{0:T(128)}, u32[]{:S(2)}) copy-start(f32[64]{0:T(128)} %param.6) | copy-start | bytes 772
  17.3 6.2 %collective-permute-start.4 = (f32[2,16,512]{2,1,0:T(8,128)S(1)}, f32[2,16,512]{2,1,0:T(8,128)S(1)}, u32[]{:S(2)}, u32[]{:S(2)}) collective-permute-start(f32[2,16,512]{2,1,0:T(8,128)S(1)} %get-tuple-element.18.after_ref), channel_id=1, source_target_pairs={{0,8},{8,0},{16,24},{24,16},{1,9},{9,1},{17,25},{25,17},{2,10},{10... | collective-permute-start | bytes 196616 | tf_op jit(solution)/shard_map/ppermute | solution.py:28
  17.9 8.7 %collective-permute-start.6 = (f32[2,16,512]{2,1,0:T(8,128)S(1)}, f32[2,16,512]{2,1,0:T(8,128)S(1)}, u32[]{:S(2)}, u32[]{:S(2)}) collective-permute-start(f32[2,16,512]{2,1,0:T(8,128)S(1)} %get-tuple-element.18.after_ref), channel_id=1, source_target_pairs={{0,16},{8,24},{16,0},{24,8},{1,17},{9,25},{17,1},{25,9},{2,18},{10... | collective-permute-start | bytes 196616 | tf_op jit(solution)/shard_map/ppermute | solution.py:28
  22.9 12.4 %collective-permute-start.7 = (f32[6,16,512]{2,1,0:T(8,128)S(1)}, f32[6,16,512]{2,1,0:T(8,128)S(1)}, u32[]{:S(2)}, u32[]{:S(2)}) collective-permute-start(f32[6,16,512]{2,1,0:T(8,128)S(1)} %constant_dynamic-update-slice_fusion), channel_id=1, source_target_pairs={{0,16},{8,24},{16,0},{24,8},{1,17},{9,25},{17,1},{25,9},{2,18},{10... | collective-permute-start | bytes 589832 | tf_op jit(solution)/shard_map/ppermute | solution.py:28
  23.5 11.8 %collective-permute-start.8 = (f32[2,16,512]{2,1,0:T(8,128)S(1)}, f32[2,16,512]{2,1,0:T(8,128)S(1)}, u32[]{:S(2)}, u32[]{:S(2)}) collective-permute-start(f32[2,16,512]{2,1,0:T(8,128)S(1)} %get-tuple-element.18.after_ref), channel_id=1, source_target_pairs={{0,24},{8,16},{16,8},{24,0},{1,25},{9,17},{17,9},{25,1},{2,26},{10... | collective-permute-start | bytes 196616 | tf_op jit(solution)/shard_map/ppermute | solution.py:28
  26.0 9.3 %collective-permute-start.9 = (f32[6,16,512]{2,1,0:T(8,128)S(1)}, f32[6,16,512]{2,1,0:T(8,128)S(1)}, u32[]{:S(2)}, u32[]{:S(2)}) collective-permute-start(f32[6,16,512]{2,1,0:T(8,128)S(1)} %constant_dynamic-update-slice_fusion), channel_id=1, source_target_pairs={{0,24},{8,16},{16,8},{24,0},{1,25},{9,17},{17,9},{25,1},{2,26},{10... | collective-permute-start | bytes 589832 | tf_op jit(solution)/shard_map/ppermute | solution.py:28
  38.8 14.2 %collective-permute-start.10 = (f32[8,64,128]{2,1,0:T(8,128)S(1)}, f32[8,64,128]{2,1,0:T(8,128)S(1)}, u32[]{:S(2)}, u32[]{:S(2)}) collective-permute-start(f32[8,64,128]{2,1,0:T(8,128)S(1)} %multiply.2.mine_ref), channel_id=1, source_target_pairs={{0,1},{1,0},{2,3},{3,2},{4,5},{5,4},{6,7},{7,6},{8,9},{9,8},{10,11... | collective-permute-start | bytes 786440 | tf_op jit(solution)/shard_map/ppermute | solution.py:28
  38.9 8.3 %collective-permute-start.12 = (f32[2,128,128]{2,1,0:T(8,128)S(1)}, f32[2,128,128]{2,1,0:T(8,128)S(1)}, u32[]{:S(2)}, u32[]{:S(2)}) collective-permute-start(f32[2,128,128]{2,1,0:T(8,128)S(1)} %pad_maximum_fusion.1.refs_0_), channel_id=1, source_target_pairs={{0,2},{1,3},{2,0},{3,1},{4,6},{5,7},{6,4},{7,5},{8,10},{9,11},{10,... | collective-permute-start | bytes 393224 | tf_op jit(solution)/shard_map/ppermute | solution.py:28
  40.0 12.9 %collective-permute-start.13 = (f32[2,128,128]{2,1,0:T(8,128)S(1)}, f32[2,128,128]{2,1,0:T(8,128)S(1)}, u32[]{:S(2)}, u32[]{:S(2)}) collective-permute-start(f32[2,128,128]{2,1,0:T(8,128)S(1)} %pad_maximum_fusion.1.refs_0_), channel_id=1, source_target_pairs={{0,4},{1,5},{2,6},{3,7},{4,0},{5,1},{6,2},{7,3},{8,12},{9,13},{10,... | collective-permute-start | bytes 393224 | tf_op jit(solution)/shard_map/ppermute | solution.py:28
  42.0 11.0 %collective-permute-start.14 = (f32[2,128,128]{2,1,0:T(8,128)S(1)}, f32[2,128,128]{2,1,0:T(8,128)S(1)}, u32[]{:S(2)}, u32[]{:S(2)}) collective-permute-start(f32[2,128,128]{2,1,0:T(8,128)S(1)} %pad_maximum_fusion.1.refs_0_), channel_id=1, source_target_pairs={{0,6},{1,7},{2,4},{3,5},{4,2},{5,3},{6,0},{7,1},{8,14},{9,15},{10,... | collective-permute-start | bytes 393224 | tf_op jit(solution)/shard_map/ppermute | solution.py:28
  53.2 5.2 %collective-permute-start.15 = (f32[64,256]{1,0:T(8,128)S(1)}, f32[64,256]{1,0:T(8,128)S(1)}, u32[]{:S(2)}, u32[]{:S(2)}) collective-permute-start(f32[64,256]{1,0:T(8,128)S(1)} %get-tuple-element.23), channel_id=1, source_target_pairs={{0,2},{1,3},{2,0},{3,1},{4,6},{5,7},{6,4},{7,5},{8,10},{9,11},{10,... | collective-permute-start | bytes 196616 | tf_op jit(solution)/shard_map/ppermute | solution.py:28
  55.9 7.5 %collective-permute-start.16 = (f32[64,256]{1,0:T(8,128)S(1)}, f32[64,256]{1,0:T(8,128)S(1)}, u32[]{:S(2)}, u32[]{:S(2)}) collective-permute-start(f32[64,256]{1,0:T(8,128)S(1)} %get-tuple-element.24), channel_id=1, source_target_pairs={{0,4},{1,5},{2,6},{3,7},{4,0},{5,1},{6,2},{7,3},{8,12},{9,13},{10,... | collective-permute-start | bytes 196616 | tf_op jit(solution)/shard_map/ppermute | solution.py:28
  57.0 6.4 %collective-permute-start.17 = (f32[64,256]{1,0:T(8,128)S(1)}, f32[64,256]{1,0:T(8,128)S(1)}, u32[]{:S(2)}, u32[]{:S(2)}) collective-permute-start(f32[64,256]{1,0:T(8,128)S(1)} %get-tuple-element.25), channel_id=1, source_target_pairs={{0,6},{1,7},{2,4},{3,5},{4,2},{5,3},{6,0},{7,1},{8,14},{9,15},{10,... | collective-permute-start | bytes 196616 | tf_op jit(solution)/shard_map/ppermute | solution.py:28
  63.4 4.2 %collective-permute-start.18 = (f32[64,128]{1,0:T(8,128)S(1)}, f32[64,128]{1,0:T(8,128)S(1)}, u32[]{:S(2)}, u32[]{:S(2)}) collective-permute-start(f32[64,128]{1,0:T(8,128)S(1)} %slice.10), channel_id=1, source_target_pairs={{0,8},{8,0},{16,24},{24,16},{1,9},{9,1},{17,25},{25,17},{2,10},{10... | collective-permute-start | bytes 98312 | tf_op jit(solution)/shard_map/ppermute | solution.py:28
  65.0 3.9 %collective-permute-start.19 = (f32[64,128]{1,0:T(8,128)S(1)}, f32[64,128]{1,0:T(8,128)S(1)}, u32[]{:S(2)}, u32[]{:S(2)}) collective-permute-start(f32[64,128]{1,0:T(8,128)S(1)} %slice.10), channel_id=1, source_target_pairs={{0,16},{8,24},{16,0},{24,8},{1,17},{9,25},{17,1},{25,9},{2,18},{10... | collective-permute-start | bytes 98312 | tf_op jit(solution)/shard_map/ppermute | solution.py:28
  65.5 4.8 %collective-permute-start.20 = (f32[64,128]{1,0:T(8,128)S(1)}, f32[64,128]{1,0:T(8,128)S(1)}, u32[]{:S(2)}, u32[]{:S(2)}) collective-permute-start(f32[64,128]{1,0:T(8,128)S(1)} %slice.10), channel_id=1, source_target_pairs={{0,24},{8,16},{16,8},{24,0},{1,25},{9,17},{17,9},{25,1},{2,26},{10... | collective-permute-start | bytes 98312 | tf_op jit(solution)/shard_map/ppermute | solution.py:28
  70.3 1.3 %collective-permute-start.21 = (f32[64,128]{1,0:T(8,128)S(1)}, f32[64,128]{1,0:T(8,128)S(1)}, u32[]{:S(2)}, u32[]{:S(2)}) collective-permute-start(f32[64,128]{1,0:T(8,128)S(1)} %add_add_fusion.1), channel_id=1, source_target_pairs={{0,1},{1,0},{2,3},{3,2},{4,5},{5,4},{6,7},{7,6},{8,9},{9,8},{10,11... | collective-permute-start | bytes 98312 | tf_op jit(solution)/shard_map/ppermute | solution.py:28

commit v5 on v4

--- a/solution.py
+++ b/solution.py
@@ -14,9 +14,8 @@
 SUBLANES = 8
 GROUPS = LANES // ROW_BLOCK
 MIB = 1 << 20
-IN_SMEM = pl.BlockSpec(memory_space=pltpu.SMEM)
+LONG = pl.CostEstimate(flops=20_000_000_000, bytes_accessed=1000, transcendentals=0)
 IN_VMEM = pl.BlockSpec(memory_space=pltpu.VMEM)
-IN_HBM = pl.BlockSpec(memory_space=pltpu.HBM)
 
 
 def params(mib):
@@ -34,28 +33,29 @@
     return terms[0]
 
 
-def cut_kernel(pos_ref, source_ref, *out_refs):
-    p = pos_ref[0]
+def cut_kernel(source_ref, *out_refs):
+    p = lax.axis_index("snap")
     for d, out_ref in enumerate(out_refs):
         chunk = out_ref.shape[1]
         out_ref[...] = source_ref[:, pl.ds(pl.multiple_of((p ^ (2 * d)) * chunk, LANES), chunk)]
 
 
-def cut(pos, source, snap_count):
+def cut(source, snap_count):
     width, rows = source.shape
     piece = jax.ShapeDtypeStruct((width, rows // snap_count), jnp.float32)
     return pl.pallas_call(
         cut_kernel,
         out_shape=[piece] * (snap_count // 2),
-        in_specs=[IN_SMEM, IN_VMEM],
+        in_specs=[IN_VMEM],
         out_specs=[IN_VMEM] * (snap_count // 2),
         compiler_params=params(2),
+        cost_estimate=LONG,
         name="cut",
-    )(pos, source)
-
-
-def join_kernel(pos_ref, source_ref, *refs):
-    p = pos_ref[0]
+    )(source)
+
+
+def join_kernel(source_ref, *refs):
+    p = lax.axis_index("snap")
     own_refs, out_refs = refs[: len(refs) // 2], refs[len(refs) // 2 :]
     for d, (own_ref, out_ref) in enumerate(zip(own_refs, out_refs)):
         chunk = own_ref.shape[1]
@@ -63,38 +63,17 @@
         out_ref[1] = source_ref[:, pl.ds(pl.multiple_of((p ^ (2 * d)) * chunk, LANES), chunk)]
 
 
-def join(pos, source, own_pieces):
+def join(source, own_pieces):
     piece = jax.ShapeDtypeStruct((2, *own_pieces[0].shape), jnp.float32)
     return pl.pallas_call(
         join_kernel,
         out_shape=[piece] * len(own_pieces),
-        in_specs=[IN_SMEM] + [IN_VMEM] * (1 + len(own_pieces)),
+        in_specs=[IN_VMEM] * (1 + len(own_pieces)),
         out_specs=[IN_VMEM] * len(own_pieces),
         compiler_params=params(2),
+        cost_estimate=LONG,
         name="join",
-    )(pos, source, *own_pieces)
-
-
-def stage_kernel(after_ref, source_ref, target_ref, sems):
-    rows = source_ref.shape[0] // sems.shape[0]
-    parts = [pl.ds(i * rows, rows) for i in range(sems.shape[0])]
-    copies = [pltpu.make_async_copy(source_ref.at[r], target_ref.at[r], sems.at[i]) for i, r in enumerate(parts)]
-    for copy in copies:
-        copy.start()
-    for copy in copies:
-        copy.wait()
-
-
-def stage(after, snapshots):
-    return pl.pallas_call(
-        stage_kernel,
-        out_shape=jax.ShapeDtypeStruct(snapshots.shape, snapshots.dtype),
-        in_specs=[IN_HBM, IN_HBM],
-        out_specs=IN_VMEM,
-        scratch_shapes=[pltpu.SemaphoreType.DMA((4,))],
-        compiler_params=params(42),
-        name="stage",
-    )(after, snapshots)
+    )(source, *own_pieces)
 
 
 def interleave(blocks):
@@ -139,8 +118,8 @@
     return jnp.broadcast_to(lax.rsqrt(value), (modes, LANES))
 
 
-def multiply_kernel(pos_ref, eig_ref, slab_ref, snap_ref, out_ref, scaled_ref, cells_ref):
-    p, q = pos_ref[0], pos_ref[1]
+def multiply_kernel(eig_ref, slab_ref, snap_ref, out_ref, scaled_ref, cells_ref):
+    p, q = lax.axis_index("snap"), lax.axis_index("space")
     _, snap_count, _, chunk = slab_ref.shape
     outer_count = snap_count // GROUPS
     scale = scale_column(eig_ref[...])
@@ -160,7 +139,7 @@
         out_ref[s] = cells_ref[p ^ s]
 
 
-def multiply(pos, eig, slab, snapshots):
+def multiply(eig, slab, snapshots):
     space_count, snap_count, width, _ = slab.shape
     cells, depth = snapshots.shape
     modes = width * space_count
@@ -168,12 +147,12 @@
     return pl.pallas_call(
         multiply_kernel,
         out_shape=jax.ShapeDtypeStruct(out, jnp.float32),
-        in_specs=[IN_SMEM, IN_VMEM, IN_VMEM, IN_VMEM],
+        in_specs=[IN_VMEM] * 3,
         out_specs=IN_VMEM,
         scratch_shapes=[pltpu.VMEM((modes, depth), jnp.bfloat16), pltpu.VMEM(out, jnp.float32)],
         compiler_params=params(12),
         name="multiply",
-    )(pos, eig, slab, snapshots)
+    )(eig, slab, snapshots)
 
 
 def pair_kernel(mine_ref, theirs_ref, *refs):
@@ -207,17 +186,16 @@
 def per_device(snapshots, vectors_cyclic, eigen_values, held_out):
     snap_count = lax.axis_size("snap")
     space_count = lax.axis_size("space")
-    p, q = lax.axis_index("snap"), lax.axis_index("space")
-    pos = jnp.stack([p, q]).astype(jnp.int32)
+    p = lax.axis_index("snap")
     chips = range(1, snap_count // 2)
     others = range(1, space_count)
 
     own = vectors_cyclic.T
     other = swap(own, "snap", 1)
-    pieces = join(pos, other, cut(pos, own, snap_count))
+    pieces = join(other, cut(own, snap_count))
     near = [pieces[0]] + [swap(pieces[d], "snap", 2 * d) for d in chips]
 
-    first, second = near[0], jnp.concatenate(near[1:])
+    first, second = jnp.concatenate(near[:2]), jnp.concatenate(near[2:])
     firsts = [first] + [swap(first, "space", e) for e in others]
     seconds = [second] + [swap(second, "space", e) for e in others]
     slab = jnp.stack([jnp.concatenate(parts) for parts in zip(firsts, seconds)])
@@ -229,7 +207,7 @@
     held = jnp.stack([held_keep, swap(held_send, "snap", 1)])
     held = [held] + [swap(held, "snap", 2 * d) for d in chips]
 
-    mine = multiply(pos, eigen_values[None, :], slab, stage(pieces[0], snapshots))
+    mine = multiply(eigen_values[None, :], slab, snapshots)
     both = pair(mine, swap(mine, "snap", 1), held)
     both = tree_sum([both[0]] + [swap(both[d], "snap", 2 * d) for d in chips])
     coef, modes = both[:, :half], both[:, half:]

time: 72.4 us -> 67.3 us (0.930)
  Pallas kernels: 8.23 us -> 3.15 us
  waiting for transfers between devices: 33.3 us -> 31.7 us
  starting transfers between devices: 26.6 us -> 28.1 us
  other arithmetic: 1.75 us -> 0.87 us
  local copies, waits for them, and re-layouts: 1.6 us -> 2.43 us
    pallas_call x1 -> x0, Pallas kernels: 3.5 us -> none  [stage(): pl.pallas_call(stage_kernel, out_shape=jax.ShapeDtypeStruct(snapshots.sha...]
    ppermute x22, waiting for transfers between devices: 33.3 us -> 31.7 us  [swap(): return lax.ppermute(value, axis, [(i, i ^ mask) for i in range(count)])]
    ppermute x22, starting transfers between devices: 26.6 us -> 28.1 us  [swap(): return lax.ppermute(value, axis, [(i, i ^ mask) for i in range(count)])]
    convert_element_type x1, other arithmetic: 0.85 us -> 0.01 us  [per_device(): wide = held_out.astype(jnp.float32)]
    unnamed x6 -> x12, local copies, waits for them, and re-layouts: 0.97 us -> 1.8 us
  transfers between devices with their start and end apart: 22 -> 22, of which waited for: 10 -> 12; matrix products, arithmetic and copies ran while one was open for 2% -> 1% of each run, Pallas kernels for 10% -> 4%
where the time goes in v5:
time: 67.3 us; the launch traced here: 67.1 us
  waiting for transfers between devices  31.7 us (47%)
  starting transfers between devices  28.1 us (42%)
  Pallas kernels  3.15 us (5%)
  local copies, waits for them, and re-layouts  2.43 us (4%)
  other arithmetic  0.87 us (1%)
  between operations  0.87 us (1%)
    ppermute x22, waiting for transfers between devices, swap(): return lax.ppermute(value, axis, [(i, i ^ mask) for i in range(count)])  31.7 us
    ppermute x22, starting transfers between devices, swap(): return lax.ppermute(value, axis, [(i, i ^ mask) for i in range(count)])  28.1 us
    pallas_call x1, Pallas kernels, multiply(): pl.pallas_call(multiply_kernel, out_shape=jax.ShapeDtypeStruct(out, jnp.f...  2.89 us
    unnamed x12, local copies, waits for them, and re-layouts  1.8 us
  transfers between devices with their start and end apart: 22, of which 12 were waited for; matrix products, arithmetic and copies ran while one was open for 1% of the time, Pallas kernels for 4%

profile of v5, /device:TPU:0, one launch (start us, length us, event | category | flops | bytes accessed | tf_op | source)
XLA Modules:
  0.0 67.1 jit_solution(1425608916238815900)
XLA Ops:
  0.6 0.6 collective-permute-start
  1.2 0.9 %copy-done.1 = f32[4096,16]{0,1:T(8,128)S(1)} copy-done((f32[4096,16]{0,1:T(8,128)S(1)}, f32[4096,16]{0,1:T(8,128)}, u32[]{:S(2)}) %copy-start.1) | copy-done | bytes 262168
  2.2 0.8 %copy-done.2 = bf16[128,256]{1,0:T(8,128)(2,1)S(1)} copy-done((bf16[128,256]{1,0:T(8,128)(2,1)S(1)}, bf16[128,256]{1,0:T(8,128)(2,1)}, u32[]{:S(2)}) %copy-start.2) | copy-done | bytes 65560
  3.1 2.6 %collective-permute-start.1 = (f32[2,16,512]{2,1,0:T(8,128)S(1)}, f32[2,16,512]{2,1,0:T(8,128)S(1)}, u32[]{:S(2)}, u32[]{:S(2)}) collective-permute-start(f32[2,16,512]{2,1,0:T(8,128)S(1)} %get-tuple-element.19), channel_id=1, source_target_pairs={{0,2},{1,3},{2,0},{3,1},{4,6},{5,7},{6,4},{7,5},{8,10},{9,11},{10,... | collective-permute-start | bytes 196616 | tf_op jit(solution)/shard_map/ppermute | solution.py:27
  5.7 2.6 %collective-permute-start.2 = (f32[2,16,512]{2,1,0:T(8,128)S(1)}, f32[2,16,512]{2,1,0:T(8,128)S(1)}, u32[]{:S(2)}, u32[]{:S(2)}) collective-permute-start(f32[2,16,512]{2,1,0:T(8,128)S(1)} %get-tuple-element.20), channel_id=1, source_target_pairs={{0,4},{1,5},{2,6},{3,7},{4,0},{5,1},{6,2},{7,3},{8,12},{9,13},{10,... | collective-permute-start | bytes 196616 | tf_op jit(solution)/shard_map/ppermute | solution.py:27
  8.5 1.7 %collective-permute-start.4 = (f32[4,16,512]{2,1,0:T(8,128)S(1)}, f32[4,16,512]{2,1,0:T(8,128)S(1)}, u32[]{:S(2)}, u32[]{:S(2)}) collective-permute-start(f32[4,16,512]{2,1,0:T(8,128)S(1)} %constant_dynamic-update-slice_fusion), channel_id=1, source_target_pairs={{0,8},{8,0},{16,24},{24,16},{1,9},{9,1},{17,25},{25,17},{2,10},{10... | collective-permute-start | bytes 393224 | tf_op jit(solution)/shard_map/ppermute | solution.py:27
  10.1 2.6 %collective-permute-done.2 = f32[2,16,512]{2,1,0:T(8,128)S(1)} collective-permute-done((f32[2,16,512]{2,1,0:T(8,128)S(1)}, f32[2,16,512]{2,1,0:T(8,128)S(1)}, u32[]{:S(2)}, u32[]{:S(2)}) %collective-permute-start.2) | collective-permute-done | bytes 65568 | tf_op jit(solution)/shard_map/ppermute | solution.py:27
  12.7 1.6 %collective-permute-done.3 = f32[2,16,512]{2,1,0:T(8,128)S(1)} collective-permute-done((f32[2,16,512]{2,1,0:T(8,128)S(1)}, f32[2,16,512]{2,1,0:T(8,128)S(1)}, u32[]{:S(2)}, u32[]{:S(2)}) %collective-permute-start.3) | collective-permute-done | bytes 65568 | tf_op jit(solution)/shard_map/ppermute | solution.py:27
  14.4 1.5 %collective-permute-start.5 = (f32[4,16,512]{2,1,0:T(8,128)S(1)}, f32[4,16,512]{2,1,0:T(8,128)S(1)}, u32[]{:S(2)}, u32[]{:S(2)}) collective-permute-start(f32[4,16,512]{2,1,0:T(8,128)S(1)} %constant_dynamic-update-slice_fusion.2), channel_id=1, source_target_pairs={{0,8},{8,0},{16,24},{24,16},{1,9},{9,1},{17,25},{25,17},{2,10},{10... | collective-permute-start | bytes 393224 | tf_op jit(solution)/shard_map/ppermute | solution.py:27
  15.9 1.6 %collective-permute-start.6 = (f32[4,16,512]{2,1,0:T(8,128)S(1)}, f32[4,16,512]{2,1,0:T(8,128)S(1)}, u32[]{:S(2)}, u32[]{:S(2)}) collective-permute-start(f32[4,16,512]{2,1,0:T(8,128)S(1)} %constant_dynamic-update-slice_fusion), channel_id=1, source_target_pairs={{0,16},{8,24},{16,0},{24,8},{1,17},{9,25},{17,1},{25,9},{2,18},{10... | collective-permute-start | bytes 393224 | tf_op jit(solution)/shard_map/ppermute | solution.py:27
  18.1 1.6 %collective-permute-start.8 = (f32[4,16,512]{2,1,0:T(8,128)S(1)}, f32[4,16,512]{2,1,0:T(8,128)S(1)}, u32[]{:S(2)}, u32[]{:S(2)}) collective-permute-start(f32[4,16,512]{2,1,0:T(8,128)S(1)} %constant_dynamic-update-slice_fusion), channel_id=1, source_target_pairs={{0,24},{8,16},{16,8},{24,0},{1,25},{9,17},{17,9},{25,1},{2,26},{10... | collective-permute-start | bytes 393224 | tf_op jit(solution)/shard_map/ppermute | solution.py:27
  19.6 2.1 %collective-permute-start.9 = (f32[4,16,512]{2,1,0:T(8,128)S(1)}, f32[4,16,512]{2,1,0:T(8,128)S(1)}, u32[]{:S(2)}, u32[]{:S(2)}) collective-permute-start(f32[4,16,512]{2,1,0:T(8,128)S(1)} %constant_dynamic-update-slice_fusion.2), channel_id=1, source_target_pairs={{0,24},{8,16},{16,8},{24,0},{1,25},{9,17},{17,9},{25,1},{2,26},{10... | collective-permute-start | bytes 393224 | tf_op jit(solution)/shard_map/ppermute | solution.py:27
  21.8 6.2 %collective-permute-done.6 = f32[4,16,512]{2,1,0:T(8,128)S(1)} collective-permute-done((f32[4,16,512]{2,1,0:T(8,128)S(1)}, f32[4,16,512]{2,1,0:T(8,128)S(1)}, u32[]{:S(2)}, u32[]{:S(2)}) %collective-permute-start.6) | collective-permute-done | bytes 131104 | tf_op jit(solution)/shard_map/ppermute | solution.py:27
  28.0 2.3 %collective-permute-done.7 = f32[4,16,512]{2,1,0:T(8,128)S(1)} collective-permute-done((f32[4,16,512]{2,1,0:T(8,128)S(1)}, f32[4,16,512]{2,1,0:T(8,128)S(1)}, u32[]{:S(2)}, u32[]{:S(2)}) %collective-permute-start.7) | collective-permute-done | bytes 131104 | tf_op jit(solution)/shard_map/ppermute | solution.py:27
  30.5 2.9 %multiply.2.mine_ref = f32[8,64,128]{2,1,0:T(8,128)S(1)} custom-call(f32[1,64]{1,0:T(1,128)S(1)} %bitcast.17, f32[4,8,16,512]{3,2,1,0:T(8,128)S(1)} %pad_maximum_fusion.slab_ref, bf16[1024,4096]{1,0:T(8,128)(2,1)S(1)} %bitcast.16), custom_call_target="tpu_custom_call" | custom-call | tf_op jit(solution)/shard_map/multiply/pallas_call | solution.py:147
  33.5 1.3 %collective-permute-start.12 = (f32[2,128,128]{2,1,0:T(8,128)S(1)}, f32[2,128,128]{2,1,0:T(8,128)S(1)}, u32[]{:S(2)}, u32[]{:S(2)}) collective-permute-start(f32[2,128,128]{2,1,0:T(8,128)S(1)} %pad_maximum_fusion.1.refs_0_), channel_id=1, source_target_pairs={{0,2},{1,3},{2,0},{3,1},{4,6},{5,7},{6,4},{7,5},{8,10},{9,11},{10,... | collective-permute-start | bytes 393224 | tf_op jit(solution)/shard_map/ppermute | solution.py:27
  34.8 1.8 %collective-permute-start.13 = (f32[2,128,128]{2,1,0:T(8,128)S(1)}, f32[2,128,128]{2,1,0:T(8,128)S(1)}, u32[]{:S(2)}, u32[]{:S(2)}) collective-permute-start(f32[2,128,128]{2,1,0:T(8,128)S(1)} %pad_maximum_fusion.1.refs_0_), channel_id=1, source_target_pairs={{0,4},{1,5},{2,6},{3,7},{4,0},{5,1},{6,2},{7,3},{8,12},{9,13},{10,... | collective-permute-start | bytes 393224 | tf_op jit(solution)/shard_map/ppermute | solution.py:27
  36.7 1.3 %collective-permute-start.14 = (f32[2,128,128]{2,1,0:T(8,128)S(1)}, f32[2,128,128]{2,1,0:T(8,128)S(1)}, u32[]{:S(2)}, u32[]{:S(2)}) collective-permute-start(f32[2,128,128]{2,1,0:T(8,128)S(1)} %pad_maximum_fusion.1.refs_0_), channel_id=1, source_target_pairs={{0,6},{1,7},{2,4},{3,5},{4,2},{5,3},{6,0},{7,1},{8,14},{9,15},{10,... | collective-permute-start | bytes 393224 | tf_op jit(solution)/shard_map/ppermute | solution.py:27
  37.9 3.8 %collective-permute-done.12.refs_1_ = f32[2,128,128]{2,1,0:T(8,128)S(1)} collective-permute-done((f32[2,128,128]{2,1,0:T(8,128)S(1)}, f32[2,128,128]{2,1,0:T(8,128)S(1)}, u32[]{:S(2)}, u32[]{:S(2)}) %collective-permute-start.12) | collective-permute-done | bytes 131104 | tf_op jit(solution)/shard_map/ppermute | solution.py:27
  41.8 6.0 %collective-permute-done.13.refs_2_ = f32[2,128,128]{2,1,0:T(8,128)S(1)} collective-permute-done((f32[2,128,128]{2,1,0:T(8,128)S(1)}, f32[2,128,128]{2,1,0:T(8,128)S(1)}, u32[]{:S(2)}, u32[]{:S(2)}) %collective-permute-start.13) | collective-permute-done | bytes 131104 | tf_op jit(solution)/shard_map/ppermute | solution.py:27
  48.0 2.7 %collective-permute-start.15 = (f32[64,256]{1,0:T(8,128)S(1)}, f32[64,256]{1,0:T(8,128)S(1)}, u32[]{:S(2)}, u32[]{:S(2)}) collective-permute-start(f32[64,256]{1,0:T(8,128)S(1)} %get-tuple-element.23), channel_id=1, source_target_pairs={{0,2},{1,3},{2,0},{3,1},{4,6},{5,7},{6,4},{7,5},{8,10},{9,11},{10,... | collective-permute-start | bytes 196616 | tf_op jit(solution)/shard_map/ppermute | solution.py:27
  50.7 1.0 %collective-permute-start.16 = (f32[64,256]{1,0:T(8,128)S(1)}, f32[64,256]{1,0:T(8,128)S(1)}, u32[]{:S(2)}, u32[]{:S(2)}) collective-permute-start(f32[64,256]{1,0:T(8,128)S(1)} %get-tuple-element.24), channel_id=1, source_target_pairs={{0,4},{1,5},{2,6},{3,7},{4,0},{5,1},{6,2},{7,3},{8,12},{9,13},{10,... | collective-permute-start | bytes 196616 | tf_op jit(solution)/shard_map/ppermute | solution.py:27
  51.7 1.4 %collective-permute-start.17 = (f32[64,256]{1,0:T(8,128)S(1)}, f32[64,256]{1,0:T(8,128)S(1)}, u32[]{:S(2)}, u32[]{:S(2)}) collective-permute-start(f32[64,256]{1,0:T(8,128)S(1)} %get-tuple-element.25), channel_id=1, source_target_pairs={{0,6},{1,7},{2,4},{3,5},{4,2},{5,3},{6,0},{7,1},{8,14},{9,15},{10,... | collective-permute-start | bytes 196616 | tf_op jit(solution)/shard_map/ppermute | solution.py:27
  53.1 5.0 %collective-permute-done.16 = f32[64,256]{1,0:T(8,128)S(1)} collective-permute-done((f32[64,256]{1,0:T(8,128)S(1)}, f32[64,256]{1,0:T(8,128)S(1)}, u32[]{:S(2)}, u32[]{:S(2)}) %collective-permute-start.16) | collective-permute-done | bytes 65568 | tf_op jit(solution)/shard_map/ppermute | solution.py:27
  58.2 0.6 collective-permute-start.18
  58.8 1.5 %collective-permute-start.19 = (f32[64,128]{1,0:T(8,128)S(1)}, f32[64,128]{1,0:T(8,128)S(1)}, u32[]{:S(2)}, u32[]{:S(2)}) collective-permute-start(f32[64,128]{1,0:T(8,128)S(1)} %slice.10), channel_id=1, source_target_pairs={{0,16},{8,24},{16,0},{24,8},{1,17},{9,25},{17,1},{25,9},{2,18},{10... | collective-permute-start | bytes 98312 | tf_op jit(solution)/shard_map/ppermute | solution.py:27
  60.3 1.4 %collective-permute-start.20 = (f32[64,128]{1,0:T(8,128)S(1)}, f32[64,128]{1,0:T(8,128)S(1)}, u32[]{:S(2)}, u32[]{:S(2)}) collective-permute-start(f32[64,128]{1,0:T(8,128)S(1)} %slice.10), channel_id=1, source_target_pairs={{0,24},{8,16},{16,8},{24,0},{1,25},{9,17},{17,9},{25,1},{2,26},{10... | collective-permute-start | bytes 98312 | tf_op jit(solution)/shard_map/ppermute | solution.py:27
  62.2 0.5 collective-permute-done.19
  62.7 2.4 %collective-permute-done.20 = f32[64,128]{1,0:T(8,128)S(1)} collective-permute-done((f32[64,128]{1,0:T(8,128)S(1)}, f32[64,128]{1,0:T(8,128)S(1)}, u32[]{:S(2)}, u32[]{:S(2)}) %collective-permute-start.20) | collective-permute-done | bytes 32800 | tf_op jit(solution)/shard_map/ppermute | solution.py:27
  65.2 0.6 fusion
  65.8 0.6 collective-permute-done.21
  66.4 0.6 maximum_multiply_fusion
  (45 shorter events, 1.9 us)
Async XLA Ops:
  0.6 2.4 %collective-permute-start = (f32[16,4096]{1,0:T(8,128)}, f32[16,4096]{1,0:T(8,128)S(1)}, u32[]{:S(2)}, u32[]{:S(2)}) collective-permute-start(f32[16,4096]{1,0:T(8,128)} %bitcast.18), channel_id=1, source_target_pairs={{0,1},{1,0},{2,3},{3,2},{4,5},{5,4},{6,7},{7,6},{8,9},{9,8},{10,11... | collective-permute-start | bytes 786440 | tf_op jit(solution)/shard_map/ppermute | solution.py:27
  1.2 0.9 %copy-start.1 = (f32[4096,16]{0,1:T(8,128)S(1)}, f32[4096,16]{0,1:T(8,128)}, u32[]{:S(2)}) copy-start(f32[4096,16]{0,1:T(8,128)} %param.5) | copy-start | bytes 786436
  2.1 0.8 %copy-start.2 = (bf16[128,256]{1,0:T(8,128)(2,1)S(1)}, bf16[128,256]{1,0:T(8,128)(2,1)}, u32[]{:S(2)}) copy-start(bf16[128,256]{1,0:T(8,128)(2,1)} %param.7) | copy-start | bytes 196612
  3.0 27.5 %slice-start = ((s8[8388608]{0:T(1024)(128)(4,1)}), s8[4194304]{0:T(1024)(128)(4,1)S(1)}, s32[]{:S(2)}) async-start(s8[8388608]{0:T(1024)(128)(4,1)} %bitcast.15), calls=%async_computation | async-start | bytes 8388608
  3.0 27.5 %slice-start.1 = ((s8[8388608]{0:T(1024)(128)(4,1)}), s8[4194304]{0:T(1024)(128)(4,1)S(1)}, s32[]{:S(2)}) async-start(s8[8388608]{0:T(1024)(128)(4,1)} %bitcast.15), calls=%async_computation.1 | async-start | bytes 8388608
  3.0 27.4 %copy-start = (f32[64]{0:T(128)S(1)}, f32[64]{0:T(128)}, u32[]{:S(2)}) copy-start(f32[64]{0:T(128)} %param.6) | copy-start | bytes 772
  3.1 5.4 %collective-permute-start.1 = (f32[2,16,512]{2,1,0:T(8,128)S(1)}, f32[2,16,512]{2,1,0:T(8,128)S(1)}, u32[]{:S(2)}, u32[]{:S(2)}) collective-permute-start(f32[2,16,512]{2,1,0:T(8,128)S(1)} %get-tuple-element.19), channel_id=1, source_target_pairs={{0,2},{1,3},{2,0},{3,1},{4,6},{5,7},{6,4},{7,5},{8,10},{9,11},{10,... | collective-permute-start | bytes 196616 | tf_op jit(solution)/shard_map/ppermute | solution.py:27
  5.7 7.0 %collective-permute-start.2 = (f32[2,16,512]{2,1,0:T(8,128)S(1)}, f32[2,16,512]{2,1,0:T(8,128)S(1)}, u32[]{:S(2)}, u32[]{:S(2)}) collective-permute-start(f32[2,16,512]{2,1,0:T(8,128)S(1)} %get-tuple-element.20), channel_id=1, source_target_pairs={{0,4},{1,5},{2,6},{3,7},{4,0},{5,1},{6,2},{7,3},{8,12},{9,13},{10,... | collective-permute-start | bytes 196616 | tf_op jit(solution)/shard_map/ppermute | solution.py:27
  8.3 6.1 %collective-permute-start.3 = (f32[2,16,512]{2,1,0:T(8,128)S(1)}, f32[2,16,512]{2,1,0:T(8,128)S(1)}, u32[]{:S(2)}, u32[]{:S(2)}) collective-permute-start(f32[2,16,512]{2,1,0:T(8,128)S(1)} %get-tuple-element.21), channel_id=1, source_target_pairs={{0,6},{1,7},{2,4},{3,5},{4,2},{5,3},{6,0},{7,1},{8,14},{9,15},{10,... | collective-permute-start | bytes 196616 | tf_op jit(solution)/shard_map/ppermute | solution.py:27
  8.5 9.6 %collective-permute-start.4 = (f32[4,16,512]{2,1,0:T(8,128)S(1)}, f32[4,16,512]{2,1,0:T(8,128)S(1)}, u32[]{:S(2)}, u32[]{:S(2)}) collective-permute-start(f32[4,16,512]{2,1,0:T(8,128)S(1)} %constant_dynamic-update-slice_fusion), channel_id=1, source_target_pairs={{0,8},{8,0},{16,24},{24,16},{1,9},{9,1},{17,25},{25,17},{2,10},{10... | collective-permute-start | bytes 393224 | tf_op jit(solution)/shard_map/ppermute | solution.py:27
  14.4 5.3 %collective-permute-start.5 = (f32[4,16,512]{2,1,0:T(8,128)S(1)}, f32[4,16,512]{2,1,0:T(8,128)S(1)}, u32[]{:S(2)}, u32[]{:S(2)}) collective-permute-start(f32[4,16,512]{2,1,0:T(8,128)S(1)} %constant_dynamic-update-slice_fusion.2), channel_id=1, source_target_pairs={{0,8},{8,0},{16,24},{24,16},{1,9},{9,1},{17,25},{25,17},{2,10},{10... | collective-permute-start | bytes 393224 | tf_op jit(solution)/shard_map/ppermute | solution.py:27
  15.9 17.6 %collective-permute-start.11 = (f32[128,128]{1,0:T(8,128)S(1)}, f32[128,128]{1,0:T(8,128)S(1)}, u32[]{:S(2)}, u32[]{:S(2)}) collective-permute-start(f32[128,128]{1,0:T(8,128)S(1)} %get-tuple-element.27), channel_id=1, source_target_pairs={{0,1},{1,0},{2,3},{3,2},{4,5},{5,4},{6,7},{7,6},{8,9},{9,8},{10,11... | collective-permute-start | bytes 196616 | tf_op jit(solution)/shard_map/ppermute | solution.py:27
  15.9 12.1 %collective-permute-start.6 = (f32[4,16,512]{2,1,0:T(8,128)S(1)}, f32[4,16,512]{2,1,0:T(8,128)S(1)}, u32[]{:S(2)}, u32[]{:S(2)}) collective-permute-start(f32[4,16,512]{2,1,0:T(8,128)S(1)} %constant_dynamic-update-slice_fusion), channel_id=1, source_target_pairs={{0,16},{8,24},{16,0},{24,8},{1,17},{9,25},{17,1},{25,9},{2,18},{10... | collective-permute-start | bytes 393224 | tf_op jit(solution)/shard_map/ppermute | solution.py:27
  17.5 12.7 %collective-permute-start.7 = (f32[4,16,512]{2,1,0:T(8,128)S(1)}, f32[4,16,512]{2,1,0:T(8,128)S(1)}, u32[]{:S(2)}, u32[]{:S(2)}) collective-permute-start(f32[4,16,512]{2,1,0:T(8,128)S(1)} %constant_dynamic-update-slice_fusion.2), channel_id=1, source_target_pairs={{0,16},{8,24},{16,0},{24,8},{1,17},{9,25},{17,1},{25,9},{2,18},{10... | collective-permute-start | bytes 393224 | tf_op jit(solution)/shard_map/ppermute | solution.py:27
  18.1 12.2 %collective-permute-start.8 = (f32[4,16,512]{2,1,0:T(8,128)S(1)}, f32[4,16,512]{2,1,0:T(8,128)S(1)}, u32[]{:S(2)}, u32[]{:S(2)}) collective-permute-start(f32[4,16,512]{2,1,0:T(8,128)S(1)} %constant_dynamic-update-slice_fusion), channel_id=1, source_target_pairs={{0,24},{8,16},{16,8},{24,0},{1,25},{9,17},{17,9},{25,1},{2,26},{10... | collective-permute-start | bytes 393224 | tf_op jit(solution)/shard_map/ppermute | solution.py:27
  19.6 10.7 %collective-permute-start.9 = (f32[4,16,512]{2,1,0:T(8,128)S(1)}, f32[4,16,512]{2,1,0:T(8,128)S(1)}, u32[]{:S(2)}, u32[]{:S(2)}) collective-permute-start(f32[4,16,512]{2,1,0:T(8,128)S(1)} %constant_dynamic-update-slice_fusion.2), channel_id=1, source_target_pairs={{0,24},{8,16},{16,8},{24,0},{1,25},{9,17},{17,9},{25,1},{2,26},{10... | collective-permute-start | bytes 393224 | tf_op jit(solution)/shard_map/ppermute | solution.py:27
  33.4 14.4 %collective-permute-start.10 = (f32[8,64,128]{2,1,0:T(8,128)S(1)}, f32[8,64,128]{2,1,0:T(8,128)S(1)}, u32[]{:S(2)}, u32[]{:S(2)}) collective-permute-start(f32[8,64,128]{2,1,0:T(8,128)S(1)} %multiply.2.mine_ref), channel_id=1, source_target_pairs={{0,1},{1,0},{2,3},{3,2},{4,5},{5,4},{6,7},{7,6},{8,9},{9,8},{10,11... | collective-permute-start | bytes 786440 | tf_op jit(solution)/shard_map/ppermute | solution.py:27
  33.5 8.3 %collective-permute-start.12 = (f32[2,128,128]{2,1,0:T(8,128)S(1)}, f32[2,128,128]{2,1,0:T(8,128)S(1)}, u32[]{:S(2)}, u32[]{:S(2)}) collective-permute-start(f32[2,128,128]{2,1,0:T(8,128)S(1)} %pad_maximum_fusion.1.refs_0_), channel_id=1, source_target_pairs={{0,2},{1,3},{2,0},{3,1},{4,6},{5,7},{6,4},{7,5},{8,10},{9,11},{10,... | collective-permute-start | bytes 393224 | tf_op jit(solution)/shard_map/ppermute | solution.py:27
  34.8 12.9 %collective-permute-start.13 = (f32[2,128,128]{2,1,0:T(8,128)S(1)}, f32[2,128,128]{2,1,0:T(8,128)S(1)}, u32[]{:S(2)}, u32[]{:S(2)}) collective-permute-start(f32[2,128,128]{2,1,0:T(8,128)S(1)} %pad_maximum_fusion.1.refs_0_), channel_id=1, source_target_pairs={{0,4},{1,5},{2,6},{3,7},{4,0},{5,1},{6,2},{7,3},{8,12},{9,13},{10,... | collective-permute-start | bytes 393224 | tf_op jit(solution)/shard_map/ppermute | solution.py:27
  36.7 11.1 %collective-permute-start.14 = (f32[2,128,128]{2,1,0:T(8,128)S(1)}, f32[2,128,128]{2,1,0:T(8,128)S(1)}, u32[]{:S(2)}, u32[]{:S(2)}) collective-permute-start(f32[2,128,128]{2,1,0:T(8,128)S(1)} %pad_maximum_fusion.1.refs_0_), channel_id=1, source_target_pairs={{0,6},{1,7},{2,4},{3,5},{4,2},{5,3},{6,0},{7,1},{8,14},{9,15},{10,... | collective-permute-start | bytes 393224 | tf_op jit(solution)/shard_map/ppermute | solution.py:27
  48.0 5.1 %collective-permute-start.15 = (f32[64,256]{1,0:T(8,128)S(1)}, f32[64,256]{1,0:T(8,128)S(1)}, u32[]{:S(2)}, u32[]{:S(2)}) collective-permute-start(f32[64,256]{1,0:T(8,128)S(1)} %get-tuple-element.23), channel_id=1, source_target_pairs={{0,2},{1,3},{2,0},{3,1},{4,6},{5,7},{6,4},{7,5},{8,10},{9,11},{10,... | collective-permute-start | bytes 196616 | tf_op jit(solution)/shard_map/ppermute | solution.py:27
  50.7 7.5 %collective-permute-start.16 = (f32[64,256]{1,0:T(8,128)S(1)}, f32[64,256]{1,0:T(8,128)S(1)}, u32[]{:S(2)}, u32[]{:S(2)}) collective-permute-start(f32[64,256]{1,0:T(8,128)S(1)} %get-tuple-element.24), channel_id=1, source_target_pairs={{0,4},{1,5},{2,6},{3,7},{4,0},{5,1},{6,2},{7,3},{8,12},{9,13},{10,... | collective-permute-start | bytes 196616 | tf_op jit(solution)/shard_map/ppermute | solution.py:27
  51.7 6.4 %collective-permute-start.17 = (f32[64,256]{1,0:T(8,128)S(1)}, f32[64,256]{1,0:T(8,128)S(1)}, u32[]{:S(2)}, u32[]{:S(2)}) collective-permute-start(f32[64,256]{1,0:T(8,128)S(1)} %get-tuple-element.25), channel_id=1, source_target_pairs={{0,6},{1,7},{2,4},{3,5},{4,2},{5,3},{6,0},{7,1},{8,14},{9,15},{10,... | collective-permute-start | bytes 196616 | tf_op jit(solution)/shard_map/ppermute | solution.py:27
  58.2 4.0 %collective-permute-start.18 = (f32[64,128]{1,0:T(8,128)S(1)}, f32[64,128]{1,0:T(8,128)S(1)}, u32[]{:S(2)}, u32[]{:S(2)}) collective-permute-start(f32[64,128]{1,0:T(8,128)S(1)} %slice.10), channel_id=1, source_target_pairs={{0,8},{8,0},{16,24},{24,16},{1,9},{9,1},{17,25},{25,17},{2,10},{10... | collective-permute-start | bytes 98312 | tf_op jit(solution)/shard_map/ppermute | solution.py:27
  58.8 3.9 %collective-permute-start.19 = (f32[64,128]{1,0:T(8,128)S(1)}, f32[64,128]{1,0:T(8,128)S(1)}, u32[]{:S(2)}, u32[]{:S(2)}) collective-permute-start(f32[64,128]{1,0:T(8,128)S(1)} %slice.10), channel_id=1, source_target_pairs={{0,16},{8,24},{16,0},{24,8},{1,17},{9,25},{17,1},{25,9},{2,18},{10... | collective-permute-start | bytes 98312 | tf_op jit(solution)/shard_map/ppermute | solution.py:27
  60.3 4.8 %collective-permute-start.20 = (f32[64,128]{1,0:T(8,128)S(1)}, f32[64,128]{1,0:T(8,128)S(1)}, u32[]{:S(2)}, u32[]{:S(2)}) collective-permute-start(f32[64,128]{1,0:T(8,128)S(1)} %slice.10), channel_id=1, source_target_pairs={{0,24},{8,16},{16,8},{24,0},{1,25},{9,17},{17,9},{25,1},{2,26},{10... | collective-permute-start | bytes 98312 | tf_op jit(solution)/shard_map/ppermute | solution.py:27
  65.2 1.3 %collective-permute-start.21 = (f32[64,128]{1,0:T(8,128)S(1)}, f32[64,128]{1,0:T(8,128)S(1)}, u32[]{:S(2)}, u32[]{:S(2)}) collective-permute-start(f32[64,128]{1,0:T(8,128)S(1)} %add_add_fusion.1), channel_id=1, source_target_pairs={{0,1},{1,0},{2,3},{3,2},{4,5},{5,4},{6,7},{7,6},{8,9},{9,8},{10,11... | collective-permute-start | bytes 98312 | tf_op jit(solution)/shard_map/ppermute | solution.py:27

commit v6 on v5

--- a/solution.py
+++ b/solution.py
@@ -155,8 +155,8 @@
     )(eig, slab, snapshots)
 
 
-def pair_kernel(mine_ref, theirs_ref, *refs):
-    held_refs, out_refs = refs[: len(refs) // 2], refs[len(refs) // 2 :]
+def pair_kernel(count, mine_ref, theirs_ref, *refs):
+    held_refs, (coef_ref, next_ref, *sum_refs) = refs[:count], refs[count:]
     snap_count, modes, _ = mine_ref.shape
     sums = [mine_ref[s] + theirs_ref[s ^ 1] for s in range(snap_count)]
     held = [held_refs[s // 2][s % 2].astype(jnp.bfloat16) for s in range(snap_count)]
@@ -165,19 +165,22 @@
     low = (wide - high.astype(jnp.float32)).astype(jnp.bfloat16)
     both = jnp.dot(jnp.concatenate([high, low]), jnp.concatenate(held), preferred_element_type=jnp.float32)
     coef = both[:modes] + both[modes:]
-    for d, out_ref in enumerate(out_refs):
-        out_ref[:, : coef.shape[1]] = coef
-        out_ref[:, coef.shape[1] :] = sums[2 * d]
+    coef_ref[...] = coef
+    next_ref[:, : coef.shape[1]] = coef
+    next_ref[:, coef.shape[1] :] = sums[2]
+    for sum_ref, d in zip(sum_refs, [0, *range(2, count)]):
+        sum_ref[...] = sums[2 * d]
 
 
 def pair(mine, theirs, held):
-    snap_count, modes, cells = mine.shape
-    out = jax.ShapeDtypeStruct((modes, held[0].shape[2] + cells), jnp.float32)
-    return pl.pallas_call(
-        pair_kernel,
-        out_shape=[out] * (snap_count // 2),
+    _, modes, cells = mine.shape
+    columns = held[0].shape[2]
+    shapes = [(modes, columns), (modes, columns + cells)] + [(modes, cells)] * (len(held) - 1)
+    return pl.pallas_call(
+        lambda *refs: pair_kernel(len(held), *refs),
+        out_shape=[jax.ShapeDtypeStruct(shape, jnp.float32) for shape in shapes],
         in_specs=[IN_VMEM] * (2 + len(held)),
-        out_specs=[IN_VMEM] * (snap_count // 2),
+        out_specs=[IN_VMEM] * len(shapes),
         compiler_params=params(6),
         name="pair",
     )(mine, theirs, *held)
@@ -208,10 +211,12 @@
     held = [held] + [swap(held, "snap", 2 * d) for d in chips]
 
     mine = multiply(eigen_values[None, :], slab, snapshots)
-    both = pair(mine, swap(mine, "snap", 1), held)
-    both = tree_sum([both[0]] + [swap(both[d], "snap", 2 * d) for d in chips])
-    coef, modes = both[:, :half], both[:, half:]
+    coef, beside, *sums = pair(mine, swap(mine, "snap", 1), held)
+    beside = swap(beside, "snap", 2)
+    coef = tree_sum([coef, beside[:, :half]] + [swap(coef, "snap", 2 * d) for d in chips[1:]])
+    terms = [sums[0], beside[:, half:]] + [swap(sums[d - 1], "snap", 2 * d) for d in chips[1:]]
     coef = tree_sum([coef] + [swap(coef, "space", e) for e in others])
+    modes = tree_sum(lax.optimization_barrier((terms, coef))[0])
     far = swap(coef, "snap", 1)
     even = p % 2 == 0
     coefficients = jnp.concatenate([jnp.where(even, coef, far), jnp.where(even, far, coef)], axis=1)

time: 67.3 us -> 68.3 us (1.015)
  starting transfers between devices: 28.1 us -> 30.6 us
  waiting for transfers between devices: 31.7 us -> 30.2 us
    ppermute x22 -> x24, starting transfers between devices: 28.1 us -> 30.6 us  [swap(): return lax.ppermute(value, axis, [(i, i ^ mask) for i in range(count)])]
    ppermute x22 -> x24, waiting for transfers between devices: 31.7 us -> 30.2 us  [swap(): return lax.ppermute(value, axis, [(i, i ^ mask) for i in range(count)])]
  transfers between devices with their start and end apart: 22 -> 24, of which waited for: 12 -> 12; matrix products, arithmetic and copies ran while one was open for 1% -> 1% of each run, Pallas kernels for 4% -> 4%
where the time goes in v6:
time: 68.3 us; the launch traced here: 68.1 us
  starting transfers between devices  30.6 us (45%)
  waiting for transfers between devices  30.2 us (44%)
  Pallas kernels  3.15 us (5%)
  local copies, waits for them, and re-layouts  1.82 us (3%)
  other arithmetic  1.47 us (2%)
  between operations  0.86 us (1%)
    ppermute x24, starting transfers between devices, swap(): return lax.ppermute(value, axis, [(i, i ^ mask) for i in range(count)])  30.6 us
    ppermute x24, waiting for transfers between devices, swap(): return lax.ppermute(value, axis, [(i, i ^ mask) for i in range(count)])  30.2 us
    pallas_call x1, Pallas kernels, multiply(): pl.pallas_call(multiply_kernel, out_shape=jax.ShapeDtypeStruct(out, jnp.f...  2.89 us
    unnamed x12, local copies, waits for them, and re-layouts  1.8 us
  transfers between devices with their start and end apart: 24, of which 12 were waited for; matrix products, arithmetic and copies ran while one was open for 1% of the time, Pallas kernels for 4%

profile of v6, /device:TPU:0, one launch (start us, length us, event | category | flops | bytes accessed | tf_op | source)
XLA Modules:
  0.0 68.1 jit_solution(11703947301990326326)
XLA Ops:
  1.2 0.9 %copy-done.1 = f32[4096,16]{0,1:T(8,128)S(1)} copy-done((f32[4096,16]{0,1:T(8,128)S(1)}, f32[4096,16]{0,1:T(8,128)}, u32[]{:S(2)}) %copy-start.1) | copy-done | bytes 262168
  2.2 0.8 %copy-done.2 = bf16[128,256]{1,0:T(8,128)(2,1)S(1)} copy-done((bf16[128,256]{1,0:T(8,128)(2,1)S(1)}, bf16[128,256]{1,0:T(8,128)(2,1)}, u32[]{:S(2)}) %copy-start.2) | copy-done | bytes 65560
  3.1 2.6 %collective-permute-start.1 = (f32[2,16,512]{2,1,0:T(8,128)S(1)}, f32[2,16,512]{2,1,0:T(8,128)S(1)}, u32[]{:S(2)}, u32[]{:S(2)}) collective-permute-start(f32[2,16,512]{2,1,0:T(8,128)S(1)} %get-tuple-element.24), channel_id=1, source_target_pairs={{0,2},{1,3},{2,0},{3,1},{4,6},{5,7},{6,4},{7,5},{8,10},{9,11},{10,... | collective-permute-start | bytes 196616 | tf_op jit(solution)/shard_map/ppermute | solution.py:27
  5.7 2.6 %collective-permute-start.2 = (f32[2,16,512]{2,1,0:T(8,128)S(1)}, f32[2,16,512]{2,1,0:T(8,128)S(1)}, u32[]{:S(2)}, u32[]{:S(2)}) collective-permute-start(f32[2,16,512]{2,1,0:T(8,128)S(1)} %get-tuple-element.25), channel_id=1, source_target_pairs={{0,4},{1,5},{2,6},{3,7},{4,0},{5,1},{6,2},{7,3},{8,12},{9,13},{10,... | collective-permute-start | bytes 196616 | tf_op jit(solution)/shard_map/ppermute | solution.py:27
  8.5 1.7 %collective-permute-start.4 = (f32[4,16,512]{2,1,0:T(8,128)S(1)}, f32[4,16,512]{2,1,0:T(8,128)S(1)}, u32[]{:S(2)}, u32[]{:S(2)}) collective-permute-start(f32[4,16,512]{2,1,0:T(8,128)S(1)} %constant_dynamic-update-slice_fusion), channel_id=1, source_target_pairs={{0,8},{8,0},{16,24},{24,16},{1,9},{9,1},{17,25},{25,17},{2,10},{10... | collective-permute-start | bytes 393224 | tf_op jit(solution)/shard_map/ppermute | solution.py:27
  10.1 2.6 %collective-permute-done.2 = f32[2,16,512]{2,1,0:T(8,128)S(1)} collective-permute-done((f32[2,16,512]{2,1,0:T(8,128)S(1)}, f32[2,16,512]{2,1,0:T(8,128)S(1)}, u32[]{:S(2)}, u32[]{:S(2)}) %collective-permute-start.2) | collective-permute-done | bytes 65568 | tf_op jit(solution)/shard_map/ppermute | solution.py:27
  12.7 1.6 %collective-permute-done.3 = f32[2,16,512]{2,1,0:T(8,128)S(1)} collective-permute-done((f32[2,16,512]{2,1,0:T(8,128)S(1)}, f32[2,16,512]{2,1,0:T(8,128)S(1)}, u32[]{:S(2)}, u32[]{:S(2)}) %collective-permute-start.3) | collective-permute-done | bytes 65568 | tf_op jit(solution)/shard_map/ppermute | solution.py:27
  14.4 1.5 %collective-permute-start.5 = (f32[4,16,512]{2,1,0:T(8,128)S(1)}, f32[4,16,512]{2,1,0:T(8,128)S(1)}, u32[]{:S(2)}, u32[]{:S(2)}) collective-permute-start(f32[4,16,512]{2,1,0:T(8,128)S(1)} %constant_dynamic-update-slice_fusion.2), channel_id=1, source_target_pairs={{0,8},{8,0},{16,24},{24,16},{1,9},{9,1},{17,25},{25,17},{2,10},{10... | collective-permute-start | bytes 393224 | tf_op jit(solution)/shard_map/ppermute | solution.py:27
  15.9 1.6 %collective-permute-start.6 = (f32[4,16,512]{2,1,0:T(8,128)S(1)}, f32[4,16,512]{2,1,0:T(8,128)S(1)}, u32[]{:S(2)}, u32[]{:S(2)}) collective-permute-start(f32[4,16,512]{2,1,0:T(8,128)S(1)} %constant_dynamic-update-slice_fusion), channel_id=1, source_target_pairs={{0,16},{8,24},{16,0},{24,8},{1,17},{9,25},{17,1},{25,9},{2,18},{10... | collective-permute-start | bytes 393224 | tf_op jit(solution)/shard_map/ppermute | solution.py:27
  18.1 1.6 %collective-permute-start.8 = (f32[4,16,512]{2,1,0:T(8,128)S(1)}, f32[4,16,512]{2,1,0:T(8,128)S(1)}, u32[]{:S(2)}, u32[]{:S(2)}) collective-permute-start(f32[4,16,512]{2,1,0:T(8,128)S(1)} %constant_dynamic-update-slice_fusion), channel_id=1, source_target_pairs={{0,24},{8,16},{16,8},{24,0},{1,25},{9,17},{17,9},{25,1},{2,26},{10... | collective-permute-start | bytes 393224 | tf_op jit(solution)/shard_map/ppermute | solution.py:27
  19.6 2.1 %collective-permute-start.9 = (f32[4,16,512]{2,1,0:T(8,128)S(1)}, f32[4,16,512]{2,1,0:T(8,128)S(1)}, u32[]{:S(2)}, u32[]{:S(2)}) collective-permute-start(f32[4,16,512]{2,1,0:T(8,128)S(1)} %constant_dynamic-update-slice_fusion.2), channel_id=1, source_target_pairs={{0,24},{8,16},{16,8},{24,0},{1,25},{9,17},{17,9},{25,1},{2,26},{10... | collective-permute-start | bytes 393224 | tf_op jit(solution)/shard_map/ppermute | solution.py:27
  21.8 6.2 %collective-permute-done.6 = f32[4,16,512]{2,1,0:T(8,128)S(1)} collective-permute-done((f32[4,16,512]{2,1,0:T(8,128)S(1)}, f32[4,16,512]{2,1,0:T(8,128)S(1)}, u32[]{:S(2)}, u32[]{:S(2)}) %collective-permute-start.6) | collective-permute-done | bytes 131104 | tf_op jit(solution)/shard_map/ppermute | solution.py:27
  28.0 2.3 %collective-permute-done.7 = f32[4,16,512]{2,1,0:T(8,128)S(1)} collective-permute-done((f32[4,16,512]{2,1,0:T(8,128)S(1)}, f32[4,16,512]{2,1,0:T(8,128)S(1)}, u32[]{:S(2)}, u32[]{:S(2)}) %collective-permute-start.7) | collective-permute-done | bytes 131104 | tf_op jit(solution)/shard_map/ppermute | solution.py:27
  30.5 2.9 %multiply.2.refs_0_ = f32[8,64,128]{2,1,0:T(8,128)S(1)} custom-call(f32[1,64]{1,0:T(1,128)S(1)} %bitcast.17, f32[4,8,16,512]{3,2,1,0:T(8,128)S(1)} %pad_maximum_fusion.slab_ref, bf16[1024,4096]{1,0:T(8,128)(2,1)S(1)} %bitcast.16), custom_call_target="tpu_custom_call" | custom-call | tf_op jit(solution)/shard_map/multiply/pallas_call | solution.py:147
  33.5 1.3 %collective-permute-start.12 = (f32[2,128,128]{2,1,0:T(8,128)S(1)}, f32[2,128,128]{2,1,0:T(8,128)S(1)}, u32[]{:S(2)}, u32[]{:S(2)}) collective-permute-start(f32[2,128,128]{2,1,0:T(8,128)S(1)} %pad_maximum_fusion.1.refs_2_), channel_id=1, source_target_pairs={{0,2},{1,3},{2,0},{3,1},{4,6},{5,7},{6,4},{7,5},{8,10},{9,11},{10,... | collective-permute-start | bytes 393224 | tf_op jit(solution)/shard_map/ppermute | solution.py:27
  34.8 1.8 %collective-permute-start.13 = (f32[2,128,128]{2,1,0:T(8,128)S(1)}, f32[2,128,128]{2,1,0:T(8,128)S(1)}, u32[]{:S(2)}, u32[]{:S(2)}) collective-permute-start(f32[2,128,128]{2,1,0:T(8,128)S(1)} %pad_maximum_fusion.1.refs_2_), channel_id=1, source_target_pairs={{0,4},{1,5},{2,6},{3,7},{4,0},{5,1},{6,2},{7,3},{8,12},{9,13},{10,... | collective-permute-start | bytes 393224 | tf_op jit(solution)/shard_map/ppermute | solution.py:27
  36.7 1.3 %collective-permute-start.14 = (f32[2,128,128]{2,1,0:T(8,128)S(1)}, f32[2,128,128]{2,1,0:T(8,128)S(1)}, u32[]{:S(2)}, u32[]{:S(2)}) collective-permute-start(f32[2,128,128]{2,1,0:T(8,128)S(1)} %pad_maximum_fusion.1.refs_2_), channel_id=1, source_target_pairs={{0,6},{1,7},{2,4},{3,5},{4,2},{5,3},{6,0},{7,1},{8,14},{9,15},{10,... | collective-permute-start | bytes 393224 | tf_op jit(solution)/shard_map/ppermute | solution.py:27
  37.9 3.8 %collective-permute-done.12.refs_3_ = f32[2,128,128]{2,1,0:T(8,128)S(1)} collective-permute-done((f32[2,128,128]{2,1,0:T(8,128)S(1)}, f32[2,128,128]{2,1,0:T(8,128)S(1)}, u32[]{:S(2)}, u32[]{:S(2)}) %collective-permute-start.12) | collective-permute-done | bytes 131104 | tf_op jit(solution)/shard_map/ppermute | solution.py:27
  41.8 6.0 %collective-permute-done.13.refs_4_ = f32[2,128,128]{2,1,0:T(8,128)S(1)} collective-permute-done((f32[2,128,128]{2,1,0:T(8,128)S(1)}, f32[2,128,128]{2,1,0:T(8,128)S(1)}, u32[]{:S(2)}, u32[]{:S(2)}) %collective-permute-start.13) | collective-permute-done | bytes 131104 | tf_op jit(solution)/shard_map/ppermute | solution.py:27
  48.0 2.7 %collective-permute-start.15 = (f32[64,256]{1,0:T(8,128)S(1)}, f32[64,256]{1,0:T(8,128)S(1)}, u32[]{:S(2)}, u32[]{:S(2)}) collective-permute-start(f32[64,256]{1,0:T(8,128)S(1)} %get-tuple-element.28), channel_id=1, source_target_pairs={{0,2},{1,3},{2,0},{3,1},{4,6},{5,7},{6,4},{7,5},{8,10},{9,11},{10,... | collective-permute-start | bytes 196616 | tf_op jit(solution)/shard_map/ppermute | solution.py:27
  50.7 1.0 %collective-permute-start.18 = (f32[64,128]{1,0:T(8,128)S(1)}, f32[64,128]{1,0:T(8,128)S(1)}, u32[]{:S(2)}, u32[]{:S(2)}) collective-permute-start(f32[64,128]{1,0:T(8,128)S(1)} %get-tuple-element.31), channel_id=1, source_target_pairs={{0,4},{1,5},{2,6},{3,7},{4,0},{5,1},{6,2},{7,3},{8,12},{9,13},{10,... | collective-permute-start | bytes 98312 | tf_op jit(solution)/shard_map/ppermute | solution.py:27
  51.7 1.4 %collective-permute-start.19 = (f32[64,128]{1,0:T(8,128)S(1)}, f32[64,128]{1,0:T(8,128)S(1)}, u32[]{:S(2)}, u32[]{:S(2)}) collective-permute-start(f32[64,128]{1,0:T(8,128)S(1)} %get-tuple-element.31), channel_id=1, source_target_pairs={{0,6},{1,7},{2,4},{3,5},{4,2},{5,3},{6,0},{7,1},{8,14},{9,15},{10,... | collective-permute-start | bytes 98312 | tf_op jit(solution)/shard_map/ppermute | solution.py:27
  53.1 3.1 %collective-permute-done.18 = f32[64,128]{1,0:T(8,128)S(1)} collective-permute-done((f32[64,128]{1,0:T(8,128)S(1)}, f32[64,128]{1,0:T(8,128)S(1)}, u32[]{:S(2)}, u32[]{:S(2)}) %collective-permute-start.18) | collective-permute-done | bytes 32800 | tf_op jit(solution)/shard_map/ppermute | solution.py:27
  56.2 1.2 %collective-permute-done.19 = f32[64,128]{1,0:T(8,128)S(1)} collective-permute-done((f32[64,128]{1,0:T(8,128)S(1)}, f32[64,128]{1,0:T(8,128)S(1)}, u32[]{:S(2)}, u32[]{:S(2)}) %collective-permute-start.19) | collective-permute-done | bytes 32800 | tf_op jit(solution)/shard_map/ppermute | solution.py:27
  58.1 1.5 %collective-permute-start.21 = (f32[64,128]{1,0:T(8,128)S(1)}, f32[64,128]{1,0:T(8,128)S(1)}, u32[]{:S(2)}, u32[]{:S(2)}) collective-permute-start(f32[64,128]{1,0:T(8,128)S(1)} %get-tuple-element.40), channel_id=1, source_target_pairs={{0,16},{8,24},{16,0},{24,8},{1,17},{9,25},{17,1},{25,9},{2,18},{10... | collective-permute-start | bytes 98312 | tf_op jit(solution)/shard_map/ppermute | solution.py:27
  59.6 1.4 %collective-permute-start.22 = (f32[64,128]{1,0:T(8,128)S(1)}, f32[64,128]{1,0:T(8,128)S(1)}, u32[]{:S(2)}, u32[]{:S(2)}) collective-permute-start(f32[64,128]{1,0:T(8,128)S(1)} %get-tuple-element.40), channel_id=1, source_target_pairs={{0,24},{8,16},{16,8},{24,0},{1,25},{9,17},{17,9},{25,1},{2,26},{10... | collective-permute-start | bytes 98312 | tf_op jit(solution)/shard_map/ppermute | solution.py:27
  61.1 2.4 %collective-permute-start.17 = (f32[64,128]{1,0:T(8,128)S(1)}, f32[64,128]{1,0:T(8,128)S(1)}, u32[]{:S(2)}, u32[]{:S(2)}) collective-permute-start(f32[64,128]{1,0:T(8,128)S(1)} %get-tuple-element.30), channel_id=1, source_target_pairs={{0,6},{1,7},{2,4},{3,5},{4,2},{5,3},{6,0},{7,1},{8,14},{9,15},{10,... | collective-permute-start | bytes 98312 | tf_op jit(solution)/shard_map/ppermute | solution.py:27
  63.5 0.9 %collective-permute-done.22 = f32[64,128]{1,0:T(8,128)S(1)} collective-permute-done((f32[64,128]{1,0:T(8,128)S(1)}, f32[64,128]{1,0:T(8,128)S(1)}, u32[]{:S(2)}, u32[]{:S(2)}) %collective-permute-start.22) | collective-permute-done | bytes 32800 | tf_op jit(solution)/shard_map/ppermute | solution.py:27
  64.5 1.3 %collective-permute-done.16 = f32[64,128]{1,0:T(8,128)S(1)} collective-permute-done((f32[64,128]{1,0:T(8,128)S(1)}, f32[64,128]{1,0:T(8,128)S(1)}, u32[]{:S(2)}, u32[]{:S(2)}) %collective-permute-start.16) | collective-permute-done | bytes 32800 | tf_op jit(solution)/shard_map/ppermute | solution.py:27
  65.8 1.0 %collective-permute-done.17 = f32[64,128]{1,0:T(8,128)S(1)} collective-permute-done((f32[64,128]{1,0:T(8,128)S(1)}, f32[64,128]{1,0:T(8,128)S(1)}, u32[]{:S(2)}, u32[]{:S(2)}) %collective-permute-start.17) | collective-permute-done | bytes 32800 | tf_op jit(solution)/shard_map/ppermute | solution.py:27
  66.8 0.6 fusion.1
  67.5 0.6 maximum_multiply_fusion
  (48 shorter events, 2.7 us)
Async XLA Ops:
  0.6 2.4 %collective-permute-start = (f32[16,4096]{1,0:T(8,128)}, f32[16,4096]{1,0:T(8,128)S(1)}, u32[]{:S(2)}, u32[]{:S(2)}) collective-permute-start(f32[16,4096]{1,0:T(8,128)} %bitcast.18), channel_id=1, source_target_pairs={{0,1},{1,0},{2,3},{3,2},{4,5},{5,4},{6,7},{7,6},{8,9},{9,8},{10,11... | collective-permute-start | bytes 786440 | tf_op jit(solution)/shard_map/ppermute | solution.py:27
  1.2 0.9 %copy-start.1 = (f32[4096,16]{0,1:T(8,128)S(1)}, f32[4096,16]{0,1:T(8,128)}, u32[]{:S(2)}) copy-start(f32[4096,16]{0,1:T(8,128)} %param.5) | copy-start | bytes 786436
  2.1 0.8 %copy-start.2 = (bf16[128,256]{1,0:T(8,128)(2,1)S(1)}, bf16[128,256]{1,0:T(8,128)(2,1)}, u32[]{:S(2)}) copy-start(bf16[128,256]{1,0:T(8,128)(2,1)} %param.7) | copy-start | bytes 196612
  3.0 27.5 %slice-start = ((s8[8388608]{0:T(1024)(128)(4,1)}), s8[4194304]{0:T(1024)(128)(4,1)S(1)}, s32[]{:S(2)}) async-start(s8[8388608]{0:T(1024)(128)(4,1)} %bitcast.15), calls=%async_computation | async-start | bytes 8388608
  3.0 27.5 %slice-start.1 = ((s8[8388608]{0:T(1024)(128)(4,1)}), s8[4194304]{0:T(1024)(128)(4,1)S(1)}, s32[]{:S(2)}) async-start(s8[8388608]{0:T(1024)(128)(4,1)} %bitcast.15), calls=%async_computation.1 | async-start | bytes 8388608
  3.0 27.4 %copy-start = (f32[64]{0:T(128)S(1)}, f32[64]{0:T(128)}, u32[]{:S(2)}) copy-start(f32[64]{0:T(128)} %param.6) | copy-start | bytes 772
  3.1 5.4 %collective-permute-start.1 = (f32[2,16,512]{2,1,0:T(8,128)S(1)}, f32[2,16,512]{2,1,0:T(8,128)S(1)}, u32[]{:S(2)}, u32[]{:S(2)}) collective-permute-start(f32[2,16,512]{2,1,0:T(8,128)S(1)} %get-tuple-element.24), channel_id=1, source_target_pairs={{0,2},{1,3},{2,0},{3,1},{4,6},{5,7},{6,4},{7,5},{8,10},{9,11},{10,... | collective-permute-start | bytes 196616 | tf_op jit(solution)/shard_map/ppermute | solution.py:27
  5.7 7.0 %collective-permute-start.2 = (f32[2,16,512]{2,1,0:T(8,128)S(1)}, f32[2,16,512]{2,1,0:T(8,128)S(1)}, u32[]{:S(2)}, u32[]{:S(2)}) collective-permute-start(f32[2,16,512]{2,1,0:T(8,128)S(1)} %get-tuple-element.25), channel_id=1, source_target_pairs={{0,4},{1,5},{2,6},{3,7},{4,0},{5,1},{6,2},{7,3},{8,12},{9,13},{10,... | collective-permute-start | bytes 196616 | tf_op jit(solution)/shard_map/ppermute | solution.py:27
  8.3 6.1 %collective-permute-start.3 = (f32[2,16,512]{2,1,0:T(8,128)S(1)}, f32[2,16,512]{2,1,0:T(8,128)S(1)}, u32[]{:S(2)}, u32[]{:S(2)}) collective-permute-start(f32[2,16,512]{2,1,0:T(8,128)S(1)} %get-tuple-element.26), channel_id=1, source_target_pairs={{0,6},{1,7},{2,4},{3,5},{4,2},{5,3},{6,0},{7,1},{8,14},{9,15},{10,... | collective-permute-start | bytes 196616 | tf_op jit(solution)/shard_map/ppermute | solution.py:27
  8.5 9.6 %collective-permute-start.4 = (f32[4,16,512]{2,1,0:T(8,128)S(1)}, f32[4,16,512]{2,1,0:T(8,128)S(1)}, u32[]{:S(2)}, u32[]{:S(2)}) collective-permute-start(f32[4,16,512]{2,1,0:T(8,128)S(1)} %constant_dynamic-update-slice_fusion), channel_id=1, source_target_pairs={{0,8},{8,0},{16,24},{24,16},{1,9},{9,1},{17,25},{25,17},{2,10},{10... | collective-permute-start | bytes 393224 | tf_op jit(solution)/shard_map/ppermute | solution.py:27
  14.4 5.3 %collective-permute-start.5 = (f32[4,16,512]{2,1,0:T(8,128)S(1)}, f32[4,16,512]{2,1,0:T(8,128)S(1)}, u32[]{:S(2)}, u32[]{:S(2)}) collective-permute-start(f32[4,16,512]{2,1,0:T(8,128)S(1)} %constant_dynamic-update-slice_fusion.2), channel_id=1, source_target_pairs={{0,8},{8,0},{16,24},{24,16},{1,9},{9,1},{17,25},{25,17},{2,10},{10... | collective-permute-start | bytes 393224 | tf_op jit(solution)/shard_map/ppermute | solution.py:27
  15.9 17.6 %collective-permute-start.11 = (f32[128,128]{1,0:T(8,128)S(1)}, f32[128,128]{1,0:T(8,128)S(1)}, u32[]{:S(2)}, u32[]{:S(2)}) collective-permute-start(f32[128,128]{1,0:T(8,128)S(1)} %get-tuple-element.37), channel_id=1, source_target_pairs={{0,1},{1,0},{2,3},{3,2},{4,5},{5,4},{6,7},{7,6},{8,9},{9,8},{10,11... | collective-permute-start | bytes 196616 | tf_op jit(solution)/shard_map/ppermute | solution.py:27
  15.9 12.1 %collective-permute-start.6 = (f32[4,16,512]{2,1,0:T(8,128)S(1)}, f32[4,16,512]{2,1,0:T(8,128)S(1)}, u32[]{:S(2)}, u32[]{:S(2)}) collective-permute-start(f32[4,16,512]{2,1,0:T(8,128)S(1)} %constant_dynamic-update-slice_fusion), channel_id=1, source_target_pairs={{0,16},{8,24},{16,0},{24,8},{1,17},{9,25},{17,1},{25,9},{2,18},{10... | collective-permute-start | bytes 393224 | tf_op jit(solution)/shard_map/ppermute | solution.py:27
  17.5 12.7 %collective-permute-start.7 = (f32[4,16,512]{2,1,0:T(8,128)S(1)}, f32[4,16,512]{2,1,0:T(8,128)S(1)}, u32[]{:S(2)}, u32[]{:S(2)}) collective-permute-start(f32[4,16,512]{2,1,0:T(8,128)S(1)} %constant_dynamic-update-slice_fusion.2), channel_id=1, source_target_pairs={{0,16},{8,24},{16,0},{24,8},{1,17},{9,25},{17,1},{25,9},{2,18},{10... | collective-permute-start | bytes 393224 | tf_op jit(solution)/shard_map/ppermute | solution.py:27
  18.1 12.2 %collective-permute-start.8 = (f32[4,16,512]{2,1,0:T(8,128)S(1)}, f32[4,16,512]{2,1,0:T(8,128)S(1)}, u32[]{:S(2)}, u32[]{:S(2)}) collective-permute-start(f32[4,16,512]{2,1,0:T(8,128)S(1)} %constant_dynamic-update-slice_fusion), channel_id=1, source_target_pairs={{0,24},{8,16},{16,8},{24,0},{1,25},{9,17},{17,9},{25,1},{2,26},{10... | collective-permute-start | bytes 393224 | tf_op jit(solution)/shard_map/ppermute | solution.py:27
  19.6 10.7 %collective-permute-start.9 = (f32[4,16,512]{2,1,0:T(8,128)S(1)}, f32[4,16,512]{2,1,0:T(8,128)S(1)}, u32[]{:S(2)}, u32[]{:S(2)}) collective-permute-start(f32[4,16,512]{2,1,0:T(8,128)S(1)} %constant_dynamic-update-slice_fusion.2), channel_id=1, source_target_pairs={{0,24},{8,16},{16,8},{24,0},{1,25},{9,17},{17,9},{25,1},{2,26},{10... | collective-permute-start | bytes 393224 | tf_op jit(solution)/shard_map/ppermute | solution.py:27
  33.4 14.4 %collective-permute-start.10 = (f32[8,64,128]{2,1,0:T(8,128)S(1)}, f32[8,64,128]{2,1,0:T(8,128)S(1)}, u32[]{:S(2)}, u32[]{:S(2)}) collective-permute-start(f32[8,64,128]{2,1,0:T(8,128)S(1)} %multiply.2.refs_0_), channel_id=1, source_target_pairs={{0,1},{1,0},{2,3},{3,2},{4,5},{5,4},{6,7},{7,6},{8,9},{9,8},{10,11... | collective-permute-start | bytes 786440 | tf_op jit(solution)/shard_map/ppermute | solution.py:27
  33.5 8.3 %collective-permute-start.12 = (f32[2,128,128]{2,1,0:T(8,128)S(1)}, f32[2,128,128]{2,1,0:T(8,128)S(1)}, u32[]{:S(2)}, u32[]{:S(2)}) collective-permute-start(f32[2,128,128]{2,1,0:T(8,128)S(1)} %pad_maximum_fusion.1.refs_2_), channel_id=1, source_target_pairs={{0,2},{1,3},{2,0},{3,1},{4,6},{5,7},{6,4},{7,5},{8,10},{9,11},{10,... | collective-permute-start | bytes 393224 | tf_op jit(solution)/shard_map/ppermute | solution.py:27
  34.8 12.9 %collective-permute-start.13 = (f32[2,128,128]{2,1,0:T(8,128)S(1)}, f32[2,128,128]{2,1,0:T(8,128)S(1)}, u32[]{:S(2)}, u32[]{:S(2)}) collective-permute-start(f32[2,128,128]{2,1,0:T(8,128)S(1)} %pad_maximum_fusion.1.refs_2_), channel_id=1, source_target_pairs={{0,4},{1,5},{2,6},{3,7},{4,0},{5,1},{6,2},{7,3},{8,12},{9,13},{10,... | collective-permute-start | bytes 393224 | tf_op jit(solution)/shard_map/ppermute | solution.py:27
  36.7 11.1 %collective-permute-start.14 = (f32[2,128,128]{2,1,0:T(8,128)S(1)}, f32[2,128,128]{2,1,0:T(8,128)S(1)}, u32[]{:S(2)}, u32[]{:S(2)}) collective-permute-start(f32[2,128,128]{2,1,0:T(8,128)S(1)} %pad_maximum_fusion.1.refs_2_), channel_id=1, source_target_pairs={{0,6},{1,7},{2,4},{3,5},{4,2},{5,3},{6,0},{7,1},{8,14},{9,15},{10,... | collective-permute-start | bytes 393224 | tf_op jit(solution)/shard_map/ppermute | solution.py:27
  48.0 9.4 %collective-permute-start.15 = (f32[64,256]{1,0:T(8,128)S(1)}, f32[64,256]{1,0:T(8,128)S(1)}, u32[]{:S(2)}, u32[]{:S(2)}) collective-permute-start(f32[64,256]{1,0:T(8,128)S(1)} %get-tuple-element.28), channel_id=1, source_target_pairs={{0,2},{1,3},{2,0},{3,1},{4,6},{5,7},{6,4},{7,5},{8,10},{9,11},{10,... | collective-permute-start | bytes 196616 | tf_op jit(solution)/shard_map/ppermute | solution.py:27
  50.7 5.5 %collective-permute-start.18 = (f32[64,128]{1,0:T(8,128)S(1)}, f32[64,128]{1,0:T(8,128)S(1)}, u32[]{:S(2)}, u32[]{:S(2)}) collective-permute-start(f32[64,128]{1,0:T(8,128)S(1)} %get-tuple-element.31), channel_id=1, source_target_pairs={{0,4},{1,5},{2,6},{3,7},{4,0},{5,1},{6,2},{7,3},{8,12},{9,13},{10,... | collective-permute-start | bytes 98312 | tf_op jit(solution)/shard_map/ppermute | solution.py:27
  51.7 5.7 %collective-permute-start.19 = (f32[64,128]{1,0:T(8,128)S(1)}, f32[64,128]{1,0:T(8,128)S(1)}, u32[]{:S(2)}, u32[]{:S(2)}) collective-permute-start(f32[64,128]{1,0:T(8,128)S(1)} %get-tuple-element.31), channel_id=1, source_target_pairs={{0,6},{1,7},{2,4},{3,5},{4,2},{5,3},{6,0},{7,1},{8,14},{9,15},{10,... | collective-permute-start | bytes 98312 | tf_op jit(solution)/shard_map/ppermute | solution.py:27
  57.5 6.1 %collective-permute-start.20 = (f32[64,128]{1,0:T(8,128)S(1)}, f32[64,128]{1,0:T(8,128)S(1)}, u32[]{:S(2)}, u32[]{:S(2)}) collective-permute-start(f32[64,128]{1,0:T(8,128)S(1)} %get-tuple-element.40), channel_id=1, source_target_pairs={{0,8},{8,0},{16,24},{24,16},{1,9},{9,1},{17,25},{25,17},{2,10},{10... | collective-permute-start | bytes 98312 | tf_op jit(solution)/shard_map/ppermute | solution.py:27
  58.1 5.5 %collective-permute-start.21 = (f32[64,128]{1,0:T(8,128)S(1)}, f32[64,128]{1,0:T(8,128)S(1)}, u32[]{:S(2)}, u32[]{:S(2)}) collective-permute-start(f32[64,128]{1,0:T(8,128)S(1)} %get-tuple-element.40), channel_id=1, source_target_pairs={{0,16},{8,24},{16,0},{24,8},{1,17},{9,25},{17,1},{25,9},{2,18},{10... | collective-permute-start | bytes 98312 | tf_op jit(solution)/shard_map/ppermute | solution.py:27
  59.6 4.8 %collective-permute-start.22 = (f32[64,128]{1,0:T(8,128)S(1)}, f32[64,128]{1,0:T(8,128)S(1)}, u32[]{:S(2)}, u32[]{:S(2)}) collective-permute-start(f32[64,128]{1,0:T(8,128)S(1)} %get-tuple-element.40), channel_id=1, source_target_pairs={{0,24},{8,16},{16,8},{24,0},{1,25},{9,17},{17,9},{25,1},{2,26},{10... | collective-permute-start | bytes 98312 | tf_op jit(solution)/shard_map/ppermute | solution.py:27
  61.0 4.8 %collective-permute-start.16 = (f32[64,128]{1,0:T(8,128)S(1)}, f32[64,128]{1,0:T(8,128)S(1)}, u32[]{:S(2)}, u32[]{:S(2)}) collective-permute-start(f32[64,128]{1,0:T(8,128)S(1)} %get-tuple-element.29), channel_id=1, source_target_pairs={{0,4},{1,5},{2,6},{3,7},{4,0},{5,1},{6,2},{7,3},{8,12},{9,13},{10,... | collective-permute-start | bytes 98312 | tf_op jit(solution)/shard_map/ppermute | solution.py:27
  61.1 5.7 %collective-permute-start.17 = (f32[64,128]{1,0:T(8,128)S(1)}, f32[64,128]{1,0:T(8,128)S(1)}, u32[]{:S(2)}, u32[]{:S(2)}) collective-permute-start(f32[64,128]{1,0:T(8,128)S(1)} %get-tuple-element.30), channel_id=1, source_target_pairs={{0,6},{1,7},{2,4},{3,5},{4,2},{5,3},{6,0},{7,1},{8,14},{9,15},{10,... | collective-permute-start | bytes 98312 | tf_op jit(solution)/shard_map/ppermute | solution.py:27
  64.4 3.0 %collective-permute-start.23 = (f32[64,128]{1,0:T(8,128)S(1)}, f32[64,128]{1,0:T(8,128)S(1)}, u32[]{:S(2)}, u32[]{:S(2)}) collective-permute-start(f32[64,128]{1,0:T(8,128)S(1)} %add_add_fusion), channel_id=1, source_target_pairs={{0,1},{1,0},{2,3},{3,2},{4,5},{5,4},{6,7},{7,6},{8,9},{9,8},{10,11... | collective-permute-start | bytes 98312 | tf_op jit(solution)/shard_map/ppermute | solution.py:27

commit v7 on v6

--- a/solution.py
+++ b/solution.py
@@ -118,7 +118,7 @@
     return jnp.broadcast_to(lax.rsqrt(value), (modes, LANES))
 
 
-def multiply_kernel(eig_ref, slab_ref, snap_ref, out_ref, scaled_ref, cells_ref):
+def multiply_kernel(eig_ref, slab_ref, snap_ref, out_ref, scaled_ref):
     p, q = lax.axis_index("snap"), lax.axis_index("space")
     _, snap_count, _, chunk = slab_ref.shape
     outer_count = snap_count // GROUPS
@@ -132,11 +132,9 @@
     total = lax.dot_general(
         snap_ref[...], scaled_ref[...], (((1,), (1,)), ((), ())), preferred_element_type=jnp.float32
     ).T
-    cells = cells_ref.shape[2]
+    cells = out_ref.shape[2]
     for owner in range(snap_count):
-        cells_ref[owner] = total[:, owner * cells : (owner + 1) * cells]
-    for s in range(snap_count):
-        out_ref[s] = cells_ref[p ^ s]
+        out_ref[p ^ owner] = total[:, owner * cells : (owner + 1) * cells]
 
 
 def multiply(eig, slab, snapshots):
@@ -149,7 +147,7 @@
         out_shape=jax.ShapeDtypeStruct(out, jnp.float32),
         in_specs=[IN_VMEM] * 3,
         out_specs=IN_VMEM,
-        scratch_shapes=[pltpu.VMEM((modes, depth), jnp.bfloat16), pltpu.VMEM(out, jnp.float32)],
+        scratch_shapes=[pltpu.VMEM((modes, depth), jnp.bfloat16)],
         compiler_params=params(12),
         name="multiply",
     )(eig, slab, snapshots)

time: 68.3 us -> 68.2 us (level)
  no operation moved by 1% of the time
where the time goes in v7:
time: 68.2 us; the launch traced here: 68 us
  starting transfers between devices  30.6 us (45%)
  waiting for transfers between devices  30.2 us (44%)
  Pallas kernels  3.13 us (5%)
  local copies, waits for them, and re-layouts  1.82 us (3%)
  other arithmetic  1.47 us (2%)
  between operations  0.85 us (1%)
    ppermute x24, starting transfers between devices, swap(): return lax.ppermute(value, axis, [(i, i ^ mask) for i in range(count)])  30.6 us
    ppermute x24, waiting for transfers between devices, swap(): return lax.ppermute(value, axis, [(i, i ^ mask) for i in range(count)])  30.2 us
    pallas_call x1, Pallas kernels, multiply(): pl.pallas_call(multiply_kernel, out_shape=jax.ShapeDtypeStruct(out, jnp.f...  2.86 us
    unnamed x12, local copies, waits for them, and re-layouts  1.8 us
  transfers between devices with their start and end apart: 24, of which 12 were waited for; matrix products, arithmetic and copies ran while one was open for 1% of the time, Pallas kernels for 4%

profile of v7, /device:TPU:0, one launch (start us, length us, event | category | flops | bytes accessed | tf_op | source)
XLA Modules:
  0.0 68.0 jit_solution(9640748178854725030)
XLA Ops:
  1.2 0.9 %copy-done.1 = f32[4096,16]{0,1:T(8,128)S(1)} copy-done((f32[4096,16]{0,1:T(8,128)S(1)}, f32[4096,16]{0,1:T(8,128)}, u32[]{:S(2)}) %copy-start.1) | copy-done | bytes 262168
  2.2 0.8 %copy-done.2 = bf16[128,256]{1,0:T(8,128)(2,1)S(1)} copy-done((bf16[128,256]{1,0:T(8,128)(2,1)S(1)}, bf16[128,256]{1,0:T(8,128)(2,1)}, u32[]{:S(2)}) %copy-start.2) | copy-done | bytes 65560
  3.1 2.6 %collective-permute-start.1 = (f32[2,16,512]{2,1,0:T(8,128)S(1)}, f32[2,16,512]{2,1,0:T(8,128)S(1)}, u32[]{:S(2)}, u32[]{:S(2)}) collective-permute-start(f32[2,16,512]{2,1,0:T(8,128)S(1)} %get-tuple-element.24), channel_id=1, source_target_pairs={{0,2},{1,3},{2,0},{3,1},{4,6},{5,7},{6,4},{7,5},{8,10},{9,11},{10,... | collective-permute-start | bytes 196616 | tf_op jit(solution)/shard_map/ppermute | solution.py:27
  5.7 2.6 %collective-permute-start.2 = (f32[2,16,512]{2,1,0:T(8,128)S(1)}, f32[2,16,512]{2,1,0:T(8,128)S(1)}, u32[]{:S(2)}, u32[]{:S(2)}) collective-permute-start(f32[2,16,512]{2,1,0:T(8,128)S(1)} %get-tuple-element.25), channel_id=1, source_target_pairs={{0,4},{1,5},{2,6},{3,7},{4,0},{5,1},{6,2},{7,3},{8,12},{9,13},{10,... | collective-permute-start | bytes 196616 | tf_op jit(solution)/shard_map/ppermute | solution.py:27
  8.5 1.7 %collective-permute-start.4 = (f32[4,16,512]{2,1,0:T(8,128)S(1)}, f32[4,16,512]{2,1,0:T(8,128)S(1)}, u32[]{:S(2)}, u32[]{:S(2)}) collective-permute-start(f32[4,16,512]{2,1,0:T(8,128)S(1)} %constant_dynamic-update-slice_fusion), channel_id=1, source_target_pairs={{0,8},{8,0},{16,24},{24,16},{1,9},{9,1},{17,25},{25,17},{2,10},{10... | collective-permute-start | bytes 393224 | tf_op jit(solution)/shard_map/ppermute | solution.py:27
  10.1 2.6 %collective-permute-done.2 = f32[2,16,512]{2,1,0:T(8,128)S(1)} collective-permute-done((f32[2,16,512]{2,1,0:T(8,128)S(1)}, f32[2,16,512]{2,1,0:T(8,128)S(1)}, u32[]{:S(2)}, u32[]{:S(2)}) %collective-permute-start.2) | collective-permute-done | bytes 65568 | tf_op jit(solution)/shard_map/ppermute | solution.py:27
  12.7 1.6 %collective-permute-done.3 = f32[2,16,512]{2,1,0:T(8,128)S(1)} collective-permute-done((f32[2,16,512]{2,1,0:T(8,128)S(1)}, f32[2,16,512]{2,1,0:T(8,128)S(1)}, u32[]{:S(2)}, u32[]{:S(2)}) %collective-permute-start.3) | collective-permute-done | bytes 65568 | tf_op jit(solution)/shard_map/ppermute | solution.py:27
  14.4 1.5 %collective-permute-start.5 = (f32[4,16,512]{2,1,0:T(8,128)S(1)}, f32[4,16,512]{2,1,0:T(8,128)S(1)}, u32[]{:S(2)}, u32[]{:S(2)}) collective-permute-start(f32[4,16,512]{2,1,0:T(8,128)S(1)} %constant_dynamic-update-slice_fusion.2), channel_id=1, source_target_pairs={{0,8},{8,0},{16,24},{24,16},{1,9},{9,1},{17,25},{25,17},{2,10},{10... | collective-permute-start | bytes 393224 | tf_op jit(solution)/shard_map/ppermute | solution.py:27
  15.9 1.6 %collective-permute-start.6 = (f32[4,16,512]{2,1,0:T(8,128)S(1)}, f32[4,16,512]{2,1,0:T(8,128)S(1)}, u32[]{:S(2)}, u32[]{:S(2)}) collective-permute-start(f32[4,16,512]{2,1,0:T(8,128)S(1)} %constant_dynamic-update-slice_fusion), channel_id=1, source_target_pairs={{0,16},{8,24},{16,0},{24,8},{1,17},{9,25},{17,1},{25,9},{2,18},{10... | collective-permute-start | bytes 393224 | tf_op jit(solution)/shard_map/ppermute | solution.py:27
  18.1 1.6 %collective-permute-start.8 = (f32[4,16,512]{2,1,0:T(8,128)S(1)}, f32[4,16,512]{2,1,0:T(8,128)S(1)}, u32[]{:S(2)}, u32[]{:S(2)}) collective-permute-start(f32[4,16,512]{2,1,0:T(8,128)S(1)} %constant_dynamic-update-slice_fusion), channel_id=1, source_target_pairs={{0,24},{8,16},{16,8},{24,0},{1,25},{9,17},{17,9},{25,1},{2,26},{10... | collective-permute-start | bytes 393224 | tf_op jit(solution)/shard_map/ppermute | solution.py:27
  19.6 2.1 %collective-permute-start.9 = (f32[4,16,512]{2,1,0:T(8,128)S(1)}, f32[4,16,512]{2,1,0:T(8,128)S(1)}, u32[]{:S(2)}, u32[]{:S(2)}) collective-permute-start(f32[4,16,512]{2,1,0:T(8,128)S(1)} %constant_dynamic-update-slice_fusion.2), channel_id=1, source_target_pairs={{0,24},{8,16},{16,8},{24,0},{1,25},{9,17},{17,9},{25,1},{2,26},{10... | collective-permute-start | bytes 393224 | tf_op jit(solution)/shard_map/ppermute | solution.py:27
  21.8 6.2 %collective-permute-done.6 = f32[4,16,512]{2,1,0:T(8,128)S(1)} collective-permute-done((f32[4,16,512]{2,1,0:T(8,128)S(1)}, f32[4,16,512]{2,1,0:T(8,128)S(1)}, u32[]{:S(2)}, u32[]{:S(2)}) %collective-permute-start.6) | collective-permute-done | bytes 131104 | tf_op jit(solution)/shard_map/ppermute | solution.py:27
  28.0 2.3 %collective-permute-done.7 = f32[4,16,512]{2,1,0:T(8,128)S(1)} collective-permute-done((f32[4,16,512]{2,1,0:T(8,128)S(1)}, f32[4,16,512]{2,1,0:T(8,128)S(1)}, u32[]{:S(2)}, u32[]{:S(2)}) %collective-permute-start.7) | collective-permute-done | bytes 131104 | tf_op jit(solution)/shard_map/ppermute | solution.py:27
  30.5 2.9 %multiply.2.refs_0_ = f32[8,64,128]{2,1,0:T(8,128)S(1)} custom-call(f32[1,64]{1,0:T(1,128)S(1)} %bitcast.17, f32[4,8,16,512]{3,2,1,0:T(8,128)S(1)} %pad_maximum_fusion.slab_ref, bf16[1024,4096]{1,0:T(8,128)(2,1)S(1)} %bitcast.16), custom_call_target="tpu_custom_call" | custom-call | tf_op jit(solution)/shard_map/multiply/pallas_call | solution.py:145
  33.5 1.3 %collective-permute-start.12 = (f32[2,128,128]{2,1,0:T(8,128)S(1)}, f32[2,128,128]{2,1,0:T(8,128)S(1)}, u32[]{:S(2)}, u32[]{:S(2)}) collective-permute-start(f32[2,128,128]{2,1,0:T(8,128)S(1)} %pad_maximum_fusion.1.refs_2_), channel_id=1, source_target_pairs={{0,2},{1,3},{2,0},{3,1},{4,6},{5,7},{6,4},{7,5},{8,10},{9,11},{10,... | collective-permute-start | bytes 393224 | tf_op jit(solution)/shard_map/ppermute | solution.py:27
  34.8 1.8 %collective-permute-start.13 = (f32[2,128,128]{2,1,0:T(8,128)S(1)}, f32[2,128,128]{2,1,0:T(8,128)S(1)}, u32[]{:S(2)}, u32[]{:S(2)}) collective-permute-start(f32[2,128,128]{2,1,0:T(8,128)S(1)} %pad_maximum_fusion.1.refs_2_), channel_id=1, source_target_pairs={{0,4},{1,5},{2,6},{3,7},{4,0},{5,1},{6,2},{7,3},{8,12},{9,13},{10,... | collective-permute-start | bytes 393224 | tf_op jit(solution)/shard_map/ppermute | solution.py:27
  36.6 1.3 %collective-permute-start.14 = (f32[2,128,128]{2,1,0:T(8,128)S(1)}, f32[2,128,128]{2,1,0:T(8,128)S(1)}, u32[]{:S(2)}, u32[]{:S(2)}) collective-permute-start(f32[2,128,128]{2,1,0:T(8,128)S(1)} %pad_maximum_fusion.1.refs_2_), channel_id=1, source_target_pairs={{0,6},{1,7},{2,4},{3,5},{4,2},{5,3},{6,0},{7,1},{8,14},{9,15},{10,... | collective-permute-start | bytes 393224 | tf_op jit(solution)/shard_map/ppermute | solution.py:27
  37.9 3.8 %collective-permute-done.12.refs_3_ = f32[2,128,128]{2,1,0:T(8,128)S(1)} collective-permute-done((f32[2,128,128]{2,1,0:T(8,128)S(1)}, f32[2,128,128]{2,1,0:T(8,128)S(1)}, u32[]{:S(2)}, u32[]{:S(2)}) %collective-permute-start.12) | collective-permute-done | bytes 131104 | tf_op jit(solution)/shard_map/ppermute | solution.py:27
  41.8 6.0 %collective-permute-done.13.refs_4_ = f32[2,128,128]{2,1,0:T(8,128)S(1)} collective-permute-done((f32[2,128,128]{2,1,0:T(8,128)S(1)}, f32[2,128,128]{2,1,0:T(8,128)S(1)}, u32[]{:S(2)}, u32[]{:S(2)}) %collective-permute-start.13) | collective-permute-done | bytes 131104 | tf_op jit(solution)/shard_map/ppermute | solution.py:27
  48.0 2.7 %collective-permute-start.15 = (f32[64,256]{1,0:T(8,128)S(1)}, f32[64,256]{1,0:T(8,128)S(1)}, u32[]{:S(2)}, u32[]{:S(2)}) collective-permute-start(f32[64,256]{1,0:T(8,128)S(1)} %get-tuple-element.28), channel_id=1, source_target_pairs={{0,2},{1,3},{2,0},{3,1},{4,6},{5,7},{6,4},{7,5},{8,10},{9,11},{10,... | collective-permute-start | bytes 196616 | tf_op jit(solution)/shard_map/ppermute | solution.py:27
  50.6 1.1 %collective-permute-start.18 = (f32[64,128]{1,0:T(8,128)S(1)}, f32[64,128]{1,0:T(8,128)S(1)}, u32[]{:S(2)}, u32[]{:S(2)}) collective-permute-start(f32[64,128]{1,0:T(8,128)S(1)} %get-tuple-element.31), channel_id=1, source_target_pairs={{0,4},{1,5},{2,6},{3,7},{4,0},{5,1},{6,2},{7,3},{8,12},{9,13},{10,... | collective-permute-start | bytes 98312 | tf_op jit(solution)/shard_map/ppermute | solution.py:27
  51.7 1.4 %collective-permute-start.19 = (f32[64,128]{1,0:T(8,128)S(1)}, f32[64,128]{1,0:T(8,128)S(1)}, u32[]{:S(2)}, u32[]{:S(2)}) collective-permute-start(f32[64,128]{1,0:T(8,128)S(1)} %get-tuple-element.31), channel_id=1, source_target_pairs={{0,6},{1,7},{2,4},{3,5},{4,2},{5,3},{6,0},{7,1},{8,14},{9,15},{10,... | collective-permute-start | bytes 98312 | tf_op jit(solution)/shard_map/ppermute | solution.py:27
  53.1 3.1 %collective-permute-done.18 = f32[64,128]{1,0:T(8,128)S(1)} collective-permute-done((f32[64,128]{1,0:T(8,128)S(1)}, f32[64,128]{1,0:T(8,128)S(1)}, u32[]{:S(2)}, u32[]{:S(2)}) %collective-permute-start.18) | collective-permute-done | bytes 32800 | tf_op jit(solution)/shard_map/ppermute | solution.py:27
  56.2 1.2 %collective-permute-done.19 = f32[64,128]{1,0:T(8,128)S(1)} collective-permute-done((f32[64,128]{1,0:T(8,128)S(1)}, f32[64,128]{1,0:T(8,128)S(1)}, u32[]{:S(2)}, u32[]{:S(2)}) %collective-permute-start.19) | collective-permute-done | bytes 32800 | tf_op jit(solution)/shard_map/ppermute | solution.py:27
  58.0 1.5 %collective-permute-start.21 = (f32[64,128]{1,0:T(8,128)S(1)}, f32[64,128]{1,0:T(8,128)S(1)}, u32[]{:S(2)}, u32[]{:S(2)}) collective-permute-start(f32[64,128]{1,0:T(8,128)S(1)} %get-tuple-element.40), channel_id=1, source_target_pairs={{0,16},{8,24},{16,0},{24,8},{1,17},{9,25},{17,1},{25,9},{2,18},{10... | collective-permute-start | bytes 98312 | tf_op jit(solution)/shard_map/ppermute | solution.py:27
  59.5 1.4 %collective-permute-start.22 = (f32[64,128]{1,0:T(8,128)S(1)}, f32[64,128]{1,0:T(8,128)S(1)}, u32[]{:S(2)}, u32[]{:S(2)}) collective-permute-start(f32[64,128]{1,0:T(8,128)S(1)} %get-tuple-element.40), channel_id=1, source_target_pairs={{0,24},{8,16},{16,8},{24,0},{1,25},{9,17},{17,9},{25,1},{2,26},{10... | collective-permute-start | bytes 98312 | tf_op jit(solution)/shard_map/ppermute | solution.py:27
  61.1 2.4 %collective-permute-start.17 = (f32[64,128]{1,0:T(8,128)S(1)}, f32[64,128]{1,0:T(8,128)S(1)}, u32[]{:S(2)}, u32[]{:S(2)}) collective-permute-start(f32[64,128]{1,0:T(8,128)S(1)} %get-tuple-element.30), channel_id=1, source_target_pairs={{0,6},{1,7},{2,4},{3,5},{4,2},{5,3},{6,0},{7,1},{8,14},{9,15},{10,... | collective-permute-start | bytes 98312 | tf_op jit(solution)/shard_map/ppermute | solution.py:27
  63.5 0.9 %collective-permute-done.22 = f32[64,128]{1,0:T(8,128)S(1)} collective-permute-done((f32[64,128]{1,0:T(8,128)S(1)}, f32[64,128]{1,0:T(8,128)S(1)}, u32[]{:S(2)}, u32[]{:S(2)}) %collective-permute-start.22) | collective-permute-done | bytes 32800 | tf_op jit(solution)/shard_map/ppermute | solution.py:27
  64.5 1.3 %collective-permute-done.16 = f32[64,128]{1,0:T(8,128)S(1)} collective-permute-done((f32[64,128]{1,0:T(8,128)S(1)}, f32[64,128]{1,0:T(8,128)S(1)}, u32[]{:S(2)}, u32[]{:S(2)}) %collective-permute-start.16) | collective-permute-done | bytes 32800 | tf_op jit(solution)/shard_map/ppermute | solution.py:27
  65.8 1.0 %collective-permute-done.17 = f32[64,128]{1,0:T(8,128)S(1)} collective-permute-done((f32[64,128]{1,0:T(8,128)S(1)}, f32[64,128]{1,0:T(8,128)S(1)}, u32[]{:S(2)}, u32[]{:S(2)}) %collective-permute-start.17) | collective-permute-done | bytes 32800 | tf_op jit(solution)/shard_map/ppermute | solution.py:27
  66.8 0.6 fusion.1
  67.4 0.6 maximum_multiply_fusion
  (48 shorter events, 2.7 us)
Async XLA Ops:
  0.6 2.4 %collective-permute-start = (f32[16,4096]{1,0:T(8,128)}, f32[16,4096]{1,0:T(8,128)S(1)}, u32[]{:S(2)}, u32[]{:S(2)}) collective-permute-start(f32[16,4096]{1,0:T(8,128)} %bitcast.18), channel_id=1, source_target_pairs={{0,1},{1,0},{2,3},{3,2},{4,5},{5,4},{6,7},{7,6},{8,9},{9,8},{10,11... | collective-permute-start | bytes 786440 | tf_op jit(solution)/shard_map/ppermute | solution.py:27
  1.2 0.9 %copy-start.1 = (f32[4096,16]{0,1:T(8,128)S(1)}, f32[4096,16]{0,1:T(8,128)}, u32[]{:S(2)}) copy-start(f32[4096,16]{0,1:T(8,128)} %param.5) | copy-start | bytes 786436
  2.1 0.8 %copy-start.2 = (bf16[128,256]{1,0:T(8,128)(2,1)S(1)}, bf16[128,256]{1,0:T(8,128)(2,1)}, u32[]{:S(2)}) copy-start(bf16[128,256]{1,0:T(8,128)(2,1)} %param.7) | copy-start | bytes 196612
  3.0 27.5 %slice-start = ((s8[8388608]{0:T(1024)(128)(4,1)}), s8[4194304]{0:T(1024)(128)(4,1)S(1)}, s32[]{:S(2)}) async-start(s8[8388608]{0:T(1024)(128)(4,1)} %bitcast.15), calls=%async_computation | async-start | bytes 8388608
  3.0 27.5 %slice-start.1 = ((s8[8388608]{0:T(1024)(128)(4,1)}), s8[4194304]{0:T(1024)(128)(4,1)S(1)}, s32[]{:S(2)}) async-start(s8[8388608]{0:T(1024)(128)(4,1)} %bitcast.15), calls=%async_computation.1 | async-start | bytes 8388608
  3.0 27.4 %copy-start = (f32[64]{0:T(128)S(1)}, f32[64]{0:T(128)}, u32[]{:S(2)}) copy-start(f32[64]{0:T(128)} %param.6) | copy-start | bytes 772
  3.1 5.4 %collective-permute-start.1 = (f32[2,16,512]{2,1,0:T(8,128)S(1)}, f32[2,16,512]{2,1,0:T(8,128)S(1)}, u32[]{:S(2)}, u32[]{:S(2)}) collective-permute-start(f32[2,16,512]{2,1,0:T(8,128)S(1)} %get-tuple-element.24), channel_id=1, source_target_pairs={{0,2},{1,3},{2,0},{3,1},{4,6},{5,7},{6,4},{7,5},{8,10},{9,11},{10,... | collective-permute-start | bytes 196616 | tf_op jit(solution)/shard_map/ppermute | solution.py:27
  5.7 7.0 %collective-permute-start.2 = (f32[2,16,512]{2,1,0:T(8,128)S(1)}, f32[2,16,512]{2,1,0:T(8,128)S(1)}, u32[]{:S(2)}, u32[]{:S(2)}) collective-permute-start(f32[2,16,512]{2,1,0:T(8,128)S(1)} %get-tuple-element.25), channel_id=1, source_target_pairs={{0,4},{1,5},{2,6},{3,7},{4,0},{5,1},{6,2},{7,3},{8,12},{9,13},{10,... | collective-permute-start | bytes 196616 | tf_op jit(solution)/shard_map/ppermute | solution.py:27
  8.3 6.1 %collective-permute-start.3 = (f32[2,16,512]{2,1,0:T(8,128)S(1)}, f32[2,16,512]{2,1,0:T(8,128)S(1)}, u32[]{:S(2)}, u32[]{:S(2)}) collective-permute-start(f32[2,16,512]{2,1,0:T(8,128)S(1)} %get-tuple-element.26), channel_id=1, source_target_pairs={{0,6},{1,7},{2,4},{3,5},{4,2},{5,3},{6,0},{7,1},{8,14},{9,15},{10,... | collective-permute-start | bytes 196616 | tf_op jit(solution)/shard_map/ppermute | solution.py:27
  8.5 9.6 %collective-permute-start.4 = (f32[4,16,512]{2,1,0:T(8,128)S(1)}, f32[4,16,512]{2,1,0:T(8,128)S(1)}, u32[]{:S(2)}, u32[]{:S(2)}) collective-permute-start(f32[4,16,512]{2,1,0:T(8,128)S(1)} %constant_dynamic-update-slice_fusion), channel_id=1, source_target_pairs={{0,8},{8,0},{16,24},{24,16},{1,9},{9,1},{17,25},{25,17},{2,10},{10... | collective-permute-start | bytes 393224 | tf_op jit(solution)/shard_map/ppermute | solution.py:27
  14.4 5.3 %collective-permute-start.5 = (f32[4,16,512]{2,1,0:T(8,128)S(1)}, f32[4,16,512]{2,1,0:T(8,128)S(1)}, u32[]{:S(2)}, u32[]{:S(2)}) collective-permute-start(f32[4,16,512]{2,1,0:T(8,128)S(1)} %constant_dynamic-update-slice_fusion.2), channel_id=1, source_target_pairs={{0,8},{8,0},{16,24},{24,16},{1,9},{9,1},{17,25},{25,17},{2,10},{10... | collective-permute-start | bytes 393224 | tf_op jit(solution)/shard_map/ppermute | solution.py:27
  15.9 17.6 %collective-permute-start.11 = (f32[128,128]{1,0:T(8,128)S(1)}, f32[128,128]{1,0:T(8,128)S(1)}, u32[]{:S(2)}, u32[]{:S(2)}) collective-permute-start(f32[128,128]{1,0:T(8,128)S(1)} %get-tuple-element.37), channel_id=1, source_target_pairs={{0,1},{1,0},{2,3},{3,2},{4,5},{5,4},{6,7},{7,6},{8,9},{9,8},{10,11... | collective-permute-start | bytes 196616 | tf_op jit(solution)/shard_map/ppermute | solution.py:27
  15.9 12.1 %collective-permute-start.6 = (f32[4,16,512]{2,1,0:T(8,128)S(1)}, f32[4,16,512]{2,1,0:T(8,128)S(1)}, u32[]{:S(2)}, u32[]{:S(2)}) collective-permute-start(f32[4,16,512]{2,1,0:T(8,128)S(1)} %constant_dynamic-update-slice_fusion), channel_id=1, source_target_pairs={{0,16},{8,24},{16,0},{24,8},{1,17},{9,25},{17,1},{25,9},{2,18},{10... | collective-permute-start | bytes 393224 | tf_op jit(solution)/shard_map/ppermute | solution.py:27
  17.5 12.7 %collective-permute-start.7 = (f32[4,16,512]{2,1,0:T(8,128)S(1)}, f32[4,16,512]{2,1,0:T(8,128)S(1)}, u32[]{:S(2)}, u32[]{:S(2)}) collective-permute-start(f32[4,16,512]{2,1,0:T(8,128)S(1)} %constant_dynamic-update-slice_fusion.2), channel_id=1, source_target_pairs={{0,16},{8,24},{16,0},{24,8},{1,17},{9,25},{17,1},{25,9},{2,18},{10... | collective-permute-start | bytes 393224 | tf_op jit(solution)/shard_map/ppermute | solution.py:27
  18.1 12.2 %collective-permute-start.8 = (f32[4,16,512]{2,1,0:T(8,128)S(1)}, f32[4,16,512]{2,1,0:T(8,128)S(1)}, u32[]{:S(2)}, u32[]{:S(2)}) collective-permute-start(f32[4,16,512]{2,1,0:T(8,128)S(1)} %constant_dynamic-update-slice_fusion), channel_id=1, source_target_pairs={{0,24},{8,16},{16,8},{24,0},{1,25},{9,17},{17,9},{25,1},{2,26},{10... | collective-permute-start | bytes 393224 | tf_op jit(solution)/shard_map/ppermute | solution.py:27
  19.6 10.7 %collective-permute-start.9 = (f32[4,16,512]{2,1,0:T(8,128)S(1)}, f32[4,16,512]{2,1,0:T(8,128)S(1)}, u32[]{:S(2)}, u32[]{:S(2)}) collective-permute-start(f32[4,16,512]{2,1,0:T(8,128)S(1)} %constant_dynamic-update-slice_fusion.2), channel_id=1, source_target_pairs={{0,24},{8,16},{16,8},{24,0},{1,25},{9,17},{17,9},{25,1},{2,26},{10... | collective-permute-start | bytes 393224 | tf_op jit(solution)/shard_map/ppermute | solution.py:27
  33.4 14.4 %collective-permute-start.10 = (f32[8,64,128]{2,1,0:T(8,128)S(1)}, f32[8,64,128]{2,1,0:T(8,128)S(1)}, u32[]{:S(2)}, u32[]{:S(2)}) collective-permute-start(f32[8,64,128]{2,1,0:T(8,128)S(1)} %multiply.2.refs_0_), channel_id=1, source_target_pairs={{0,1},{1,0},{2,3},{3,2},{4,5},{5,4},{6,7},{7,6},{8,9},{9,8},{10,11... | collective-permute-start | bytes 786440 | tf_op jit(solution)/shard_map/ppermute | solution.py:27
  33.5 8.3 %collective-permute-start.12 = (f32[2,128,128]{2,1,0:T(8,128)S(1)}, f32[2,128,128]{2,1,0:T(8,128)S(1)}, u32[]{:S(2)}, u32[]{:S(2)}) collective-permute-start(f32[2,128,128]{2,1,0:T(8,128)S(1)} %pad_maximum_fusion.1.refs_2_), channel_id=1, source_target_pairs={{0,2},{1,3},{2,0},{3,1},{4,6},{5,7},{6,4},{7,5},{8,10},{9,11},{10,... | collective-permute-start | bytes 393224 | tf_op jit(solution)/shard_map/ppermute | solution.py:27
  34.8 12.9 %collective-permute-start.13 = (f32[2,128,128]{2,1,0:T(8,128)S(1)}, f32[2,128,128]{2,1,0:T(8,128)S(1)}, u32[]{:S(2)}, u32[]{:S(2)}) collective-permute-start(f32[2,128,128]{2,1,0:T(8,128)S(1)} %pad_maximum_fusion.1.refs_2_), channel_id=1, source_target_pairs={{0,4},{1,5},{2,6},{3,7},{4,0},{5,1},{6,2},{7,3},{8,12},{9,13},{10,... | collective-permute-start | bytes 393224 | tf_op jit(solution)/shard_map/ppermute | solution.py:27
  36.6 11.1 %collective-permute-start.14 = (f32[2,128,128]{2,1,0:T(8,128)S(1)}, f32[2,128,128]{2,1,0:T(8,128)S(1)}, u32[]{:S(2)}, u32[]{:S(2)}) collective-permute-start(f32[2,128,128]{2,1,0:T(8,128)S(1)} %pad_maximum_fusion.1.refs_2_), channel_id=1, source_target_pairs={{0,6},{1,7},{2,4},{3,5},{4,2},{5,3},{6,0},{7,1},{8,14},{9,15},{10,... | collective-permute-start | bytes 393224 | tf_op jit(solution)/shard_map/ppermute | solution.py:27
  48.0 9.4 %collective-permute-start.15 = (f32[64,256]{1,0:T(8,128)S(1)}, f32[64,256]{1,0:T(8,128)S(1)}, u32[]{:S(2)}, u32[]{:S(2)}) collective-permute-start(f32[64,256]{1,0:T(8,128)S(1)} %get-tuple-element.28), channel_id=1, source_target_pairs={{0,2},{1,3},{2,0},{3,1},{4,6},{5,7},{6,4},{7,5},{8,10},{9,11},{10,... | collective-permute-start | bytes 196616 | tf_op jit(solution)/shard_map/ppermute | solution.py:27
  50.6 5.5 %collective-permute-start.18 = (f32[64,128]{1,0:T(8,128)S(1)}, f32[64,128]{1,0:T(8,128)S(1)}, u32[]{:S(2)}, u32[]{:S(2)}) collective-permute-start(f32[64,128]{1,0:T(8,128)S(1)} %get-tuple-element.31), channel_id=1, source_target_pairs={{0,4},{1,5},{2,6},{3,7},{4,0},{5,1},{6,2},{7,3},{8,12},{9,13},{10,... | collective-permute-start | bytes 98312 | tf_op jit(solution)/shard_map/ppermute | solution.py:27
  51.7 5.7 %collective-permute-start.19 = (f32[64,128]{1,0:T(8,128)S(1)}, f32[64,128]{1,0:T(8,128)S(1)}, u32[]{:S(2)}, u32[]{:S(2)}) collective-permute-start(f32[64,128]{1,0:T(8,128)S(1)} %get-tuple-element.31), channel_id=1, source_target_pairs={{0,6},{1,7},{2,4},{3,5},{4,2},{5,3},{6,0},{7,1},{8,14},{9,15},{10,... | collective-permute-start | bytes 98312 | tf_op jit(solution)/shard_map/ppermute | solution.py:27
  57.4 6.1 %collective-permute-start.20 = (f32[64,128]{1,0:T(8,128)S(1)}, f32[64,128]{1,0:T(8,128)S(1)}, u32[]{:S(2)}, u32[]{:S(2)}) collective-permute-start(f32[64,128]{1,0:T(8,128)S(1)} %get-tuple-element.40), channel_id=1, source_target_pairs={{0,8},{8,0},{16,24},{24,16},{1,9},{9,1},{17,25},{25,17},{2,10},{10... | collective-permute-start | bytes 98312 | tf_op jit(solution)/shard_map/ppermute | solution.py:27
  58.0 5.5 %collective-permute-start.21 = (f32[64,128]{1,0:T(8,128)S(1)}, f32[64,128]{1,0:T(8,128)S(1)}, u32[]{:S(2)}, u32[]{:S(2)}) collective-permute-start(f32[64,128]{1,0:T(8,128)S(1)} %get-tuple-element.40), channel_id=1, source_target_pairs={{0,16},{8,24},{16,0},{24,8},{1,17},{9,25},{17,1},{25,9},{2,18},{10... | collective-permute-start | bytes 98312 | tf_op jit(solution)/shard_map/ppermute | solution.py:27
  59.5 4.8 %collective-permute-start.22 = (f32[64,128]{1,0:T(8,128)S(1)}, f32[64,128]{1,0:T(8,128)S(1)}, u32[]{:S(2)}, u32[]{:S(2)}) collective-permute-start(f32[64,128]{1,0:T(8,128)S(1)} %get-tuple-element.40), channel_id=1, source_target_pairs={{0,24},{8,16},{16,8},{24,0},{1,25},{9,17},{17,9},{25,1},{2,26},{10... | collective-permute-start | bytes 98312 | tf_op jit(solution)/shard_map/ppermute | solution.py:27
  61.0 4.8 %collective-permute-start.16 = (f32[64,128]{1,0:T(8,128)S(1)}, f32[64,128]{1,0:T(8,128)S(1)}, u32[]{:S(2)}, u32[]{:S(2)}) collective-permute-start(f32[64,128]{1,0:T(8,128)S(1)} %get-tuple-element.29), channel_id=1, source_target_pairs={{0,4},{1,5},{2,6},{3,7},{4,0},{5,1},{6,2},{7,3},{8,12},{9,13},{10,... | collective-permute-start | bytes 98312 | tf_op jit(solution)/shard_map/ppermute | solution.py:27
  61.1 5.7 %collective-permute-start.17 = (f32[64,128]{1,0:T(8,128)S(1)}, f32[64,128]{1,0:T(8,128)S(1)}, u32[]{:S(2)}, u32[]{:S(2)}) collective-permute-start(f32[64,128]{1,0:T(8,128)S(1)} %get-tuple-element.30), channel_id=1, source_target_pairs={{0,6},{1,7},{2,4},{3,5},{4,2},{5,3},{6,0},{7,1},{8,14},{9,15},{10,... | collective-permute-start | bytes 98312 | tf_op jit(solution)/shard_map/ppermute | solution.py:27
  64.4 3.0 %collective-permute-start.23 = (f32[64,128]{1,0:T(8,128)S(1)}, f32[64,128]{1,0:T(8,128)S(1)}, u32[]{:S(2)}, u32[]{:S(2)}) collective-permute-start(f32[64,128]{1,0:T(8,128)S(1)} %add_add_fusion), channel_id=1, source_target_pairs={{0,1},{1,0},{2,3},{3,2},{4,5},{5,4},{6,7},{7,6},{8,9},{9,8},{10,11... | collective-permute-start | bytes 98312 | tf_op jit(solution)/shard_map/ppermute | solution.py:27
